TPU v7x, 32 devices: a whole 2x2x4 slice. The times are simulated.
32 devices in a mesh: rep: 2 (over y), shard: 16 (over z, x, core).
Axes of the slice: x: 2, y: 2, z: 4, core: 2. Of those that a mesh axis runs over, the one named last changes fastest.
Arguments:
- tokens: bfloat16 [65536, 768], P(('rep', 'shard')), may hold values from -6 to 6
- segment_ids: int32 [32, 2048], P(('rep', 'shard')), may hold values from 0 to 7, never falling along the last dimension, each value on 1 to 1024 neighbouring positions
- query_weight: bfloat16 [768, 768], P('shard'), may hold values from -0.21875 to 0.21875
- key_weight: bfloat16 [768, 768], P('shard'), may hold values from -0.21875 to 0.21875
- value_weight: bfloat16 [768, 768], P('shard'), may hold values from -0.21875 to 0.21875
- output_weight: bfloat16 [768, 768], P('shard'), may hold values from -0.875 to 0.875
- relative_table: bfloat16 [32, 768], P(None, 'shard'), may hold values from -6 to 6
- order_table: bfloat16 [2, 768], P(None, 'shard'), may hold values from -6 to 6
- content_bias: bfloat16 [768], P('shard'), may hold values from -3 to 3
- position_bias: bfloat16 [768], P('shard'), may hold values from -3 to 3
- order_bias: bfloat16 [768], P('shard'), may hold values from -3 to 3
- first_gain: bfloat16 [768], P('shard'), may hold values from 0.5 to 1.5
- first_shift: bfloat16 [768], P('shard'), may hold values from -2 to 2
- inner_weight: bfloat16 [768, 3072], P('shard'), may hold values from -0.21875 to 0.21875
- inner_bias: bfloat16 [3072], P('shard'), may hold values from -3 to 3
- outer_weight: bfloat16 [3072, 768], P('shard'), may hold values from -0.21875 to 0.21875
- outer_bias: bfloat16 [768], P('shard'), may hold values from -2 to 2
- second_gain: bfloat16 [768], P('shard'), may hold values from 0.5 to 1.5
- second_shift: bfloat16 [768], P('shard'), may hold values from -2 to 2
- cotangent: bfloat16 [32768, 768], P(('rep', 'shard')), may hold values from -6 to 6
Outputs:
- layer_out: bfloat16 [32768, 768], P(('rep', 'shard'))
- tokens_grad: float32 [65536, 768], P(('rep', 'shard'))
- query_weight_grad: float32 [768, 768], P('shard')
- key_weight_grad: float32 [768, 768], P('shard')
- value_weight_grad: float32 [768, 768], P('shard')
- output_weight_grad: float32 [768, 768], P('shard')
- relative_table_grad: float32 [32, 768], P(None, 'shard')
- order_table_grad: float32 [2, 768], P(None, 'shard')
- content_bias_grad: float32 [768], P('shard')
- position_bias_grad: float32 [768], P('shard')
- order_bias_grad: float32 [768], P('shard')
- first_gain_grad: float32 [768], P('shard')
- first_shift_grad: float32 [768], P('shard')
- inner_weight_grad: float32 [768, 3072], P('shard')
- inner_bias_grad: float32 [3072], P('shard')
- outer_weight_grad: float32 [3072, 768], P('shard')
- outer_bias_grad: float32 [768], P('shard')
- second_gain_grad: float32 [768], P('shard')
- second_shift_grad: float32 [768], P('shard')
Inputs may be any that keep to these rules, and one draw needn't show every extreme that they name: `segment_ids`: each row holds the document numbers of one sequence: never falling, each document 1 to 1024 positions, one of exactly 1024.
All inputs are finite; a program needn't handle non-finite values.
Results may differ from a plain program's by a relative error of at most 0.02.
Values may be sent and summed in bfloat16 or wider, within the bound.
A program may use at most 192 MiB of HBM per device.

v0:
```python
import math

import jax
import jax.numpy as jnp
from jax import lax
from jax.sharding import PartitionSpec as P

H = 12
DH = 64


LIMITS = (1, 2, 3, 4, 5, 6, 7, 8, 12, 16, 24, 32, 48, 64, 128)


def matmul(left, right):
    return jnp.dot(left, right, preferred_element_type=jnp.float32)


def bucket_table(length):
    query_pos = jnp.arange(length // 2, dtype=jnp.int32) * 2
    key_pos = jnp.arange(length, dtype=jnp.int32)
    offset = key_pos[None, :] - query_pos[:, None]
    distance = jnp.abs(offset)
    passed = jnp.zeros(offset.shape, jnp.int32)
    for limit in LIMITS:
        passed = passed + (distance >= limit).astype(jnp.int32)
    behind = offset < 0
    farther = (distance >= 256).astype(jnp.int32)
    return (jnp.where(behind, 15 + passed + farther, passed), behind)


def normalize(values):
    centered = values - jnp.mean(values, axis=1, keepdims=True)
    inverse = lax.rsqrt(jnp.mean(centered * centered, axis=1, keepdims=True) + 1e-05)
    return (centered * inverse, inverse)


def norm_back(grad, normed, inverse):
    return inverse * (
        grad
        - jnp.mean(grad, axis=1, keepdims=True)
        - normed * jnp.mean(grad * normed, axis=1, keepdims=True)
    )


def gelu_slope(values):
    return 0.5 * (1.0 + lax.erf(values * math.sqrt(0.5))) + values * jnp.exp(
        -0.5 * values * values
    ) / math.sqrt(2.0 * math.pi)


def head_scores(
    content_h,
    keys_h,
    position_h,
    order_h,
    relative_h,
    orders_h,
    query_row,
    key_row,
    bucket,
    behind,
    scale,
):
    table = matmul(position_h, relative_h.T)
    placed = jnp.zeros(bucket.shape, jnp.float32)
    for which in range(table.shape[1]):
        placed = placed + jnp.where(bucket == which, table[:, which : which + 1], 0.0)
    ranked = matmul(order_h, orders_h.T)
    ordered = jnp.where(behind, ranked[:, 1:2], ranked[:, 0:1])
    scores = (matmul(content_h, keys_h.T) + placed + ordered) * scale
    return jnp.where(query_row[:, None] == key_row[None, :], scores, -1e30)


def body(
    tokens,
    segment_ids,
    query_weight,
    key_weight,
    value_weight,
    output_weight,
    relative_table,
    order_table,
    content_bias,
    position_bias,
    order_bias,
    first_gain,
    first_shift,
    inner_weight,
    inner_bias,
    outer_weight,
    outer_bias,
    second_gain,
    second_shift,
    cotangent,
):
    full = (
        lax.all_gather(query_weight, "shard", axis=0, tiled=True),
        lax.all_gather(key_weight, "shard", axis=0, tiled=True),
        lax.all_gather(value_weight, "shard", axis=0, tiled=True),
        lax.all_gather(output_weight, "shard", axis=0, tiled=True),
        lax.all_gather(relative_table, "shard", axis=1, tiled=True),
        lax.all_gather(order_table, "shard", axis=1, tiled=True),
        lax.all_gather(content_bias, "shard", axis=0, tiled=True),
        lax.all_gather(position_bias, "shard", axis=0, tiled=True),
        lax.all_gather(order_bias, "shard", axis=0, tiled=True),
        lax.all_gather(first_gain, "shard", axis=0, tiled=True),
        lax.all_gather(first_shift, "shard", axis=0, tiled=True),
        lax.all_gather(inner_weight, "shard", axis=0, tiled=True),
        lax.all_gather(inner_bias, "shard", axis=0, tiled=True),
        lax.all_gather(outer_weight, "shard", axis=0, tiled=True),
        lax.all_gather(outer_bias, "shard", axis=0, tiled=True),
        lax.all_gather(second_gain, "shard", axis=0, tiled=True),
        lax.all_gather(second_shift, "shard", axis=0, tiled=True),
    )
    (
        weight_query,
        weight_key,
        weight_value,
        weight_output,
        weight_relative,
        weight_order,
        bias_content,
        bias_position,
        bias_order,
        gain_first,
        shift_first,
        weight_inner,
        bias_inner,
        weight_outer,
        bias_outer,
        gain_second,
        shift_second,
    ) = full
    f32 = jnp.float32
    bf16 = jnp.bfloat16
    count, length = segment_ids.shape
    half = length // 2
    width = tokens.shape[1]
    buckets_all = weight_relative.shape[0]
    scale = 1.0 / math.sqrt(DH)
    bucket, behind = bucket_table(length)
    pairs = tokens.astype(f32).reshape(count, half, 2, width)
    query_seg = segment_ids[:, 0::2]
    joined = (query_seg == segment_ids[:, 1::2]).astype(f32)[:, :, None]
    pooled = ((pairs[:, :, 0] + joined * pairs[:, :, 1]) / (1.0 + joined)).reshape(
        count * half, width
    )
    pooled_low = pooled.astype(bf16)
    queries = matmul(pooled_low, weight_query)
    keys = matmul(tokens, weight_key).astype(bf16)
    values = matmul(tokens, weight_value).astype(bf16)
    content = (queries + bias_content.astype(f32)).astype(bf16)
    position = (queries + bias_position.astype(f32)).astype(bf16)
    ordering = (queries + bias_order.astype(f32)).astype(bf16)

    def split(array, rows_each):
        return (
            array.reshape(count, rows_each, H, DH)
            .transpose(0, 2, 1, 3)
            .reshape(count * H, rows_each, DH)
        )

    def merge(array, rows_each):
        return (
            array.reshape(count, H, rows_each, DH)
            .transpose(0, 2, 1, 3)
            .reshape(count * rows_each, H * DH)
        )

    relative_heads = jnp.tile(
        weight_relative.reshape(buckets_all, H, DH).transpose(1, 0, 2), (count, 1, 1)
    )
    order_heads = jnp.tile(weight_order.reshape(2, H, DH).transpose(1, 0, 2), (count, 1, 1))
    query_rows = jnp.repeat(query_seg, H, axis=0)
    key_rows = jnp.repeat(segment_ids, H, axis=0)
    head_inputs = (
        split(content, half),
        split(keys, length),
        split(values, length),
        split(position, half),
        split(ordering, half),
        relative_heads,
        order_heads,
        query_rows,
        key_rows,
    )

    def attend(inputs):
        (
            content_h,
            keys_h,
            values_h,
            position_h,
            order_h,
            relative_h,
            orders_h,
            query_row,
            key_row,
        ) = inputs
        scores = head_scores(
            content_h,
            keys_h,
            position_h,
            order_h,
            relative_h,
            orders_h,
            query_row,
            key_row,
            bucket,
            behind,
            scale,
        )
        peak = jnp.max(scores, axis=1, keepdims=True)
        logsum = peak + jnp.log(jnp.sum(jnp.exp(scores - peak), axis=1, keepdims=True))
        probs = jnp.exp(scores - logsum)
        return (matmul(probs.astype(bf16), values_h), logsum[:, 0])

    head_out, logsums = lax.map(attend, head_inputs)
    context = merge(head_out, half).astype(bf16)
    attended = matmul(context, weight_output)
    first_norm, first_inverse = normalize(pooled + attended)
    first = first_norm * gain_first.astype(f32) + shift_first.astype(f32)
    first_low = first.astype(bf16)
    inner = matmul(first_low, weight_inner) + bias_inner.astype(f32)
    act_low = jax.nn.gelu(inner, approximate=False).astype(bf16)
    outer = matmul(act_low, weight_outer) + bias_outer.astype(f32)
    second_norm, second_inverse = normalize(first + outer)
    layer_out = (second_norm * gain_second.astype(f32) + shift_second.astype(f32)).astype(bf16)
    again = (
        lax.all_gather(query_weight, "shard", axis=0, tiled=True),
        lax.all_gather(key_weight, "shard", axis=0, tiled=True),
        lax.all_gather(value_weight, "shard", axis=0, tiled=True),
        lax.all_gather(output_weight, "shard", axis=0, tiled=True),
        lax.all_gather(relative_table, "shard", axis=1, tiled=True),
        lax.all_gather(order_table, "shard", axis=1, tiled=True),
        lax.all_gather(content_bias, "shard", axis=0, tiled=True),
        lax.all_gather(position_bias, "shard", axis=0, tiled=True),
        lax.all_gather(order_bias, "shard", axis=0, tiled=True),
        lax.all_gather(first_gain, "shard", axis=0, tiled=True),
        lax.all_gather(first_shift, "shard", axis=0, tiled=True),
        lax.all_gather(inner_weight, "shard", axis=0, tiled=True),
        lax.all_gather(inner_bias, "shard", axis=0, tiled=True),
        lax.all_gather(outer_weight, "shard", axis=0, tiled=True),
        lax.all_gather(outer_bias, "shard", axis=0, tiled=True),
        lax.all_gather(second_gain, "shard", axis=0, tiled=True),
        lax.all_gather(second_shift, "shard", axis=0, tiled=True),
    )
    (
        back_query,
        back_key,
        back_value,
        back_output,
        back_relative,
        back_order,
        unused_content,
        unused_position,
        unused_order,
        back_first,
        unused_shift,
        back_inner,
        unused_inner,
        back_outer,
        unused_outer,
        back_second,
        unused_second,
    ) = again
    grad_out = cotangent.astype(f32)
    second_gain_grad = jnp.sum(grad_out * second_norm, axis=0)
    second_shift_grad = jnp.sum(grad_out, axis=0)
    mid_grad = norm_back(grad_out * back_second.astype(f32), second_norm, second_inverse)
    outer_low = mid_grad.astype(bf16)
    outer_weight_grad = matmul(act_low.T, outer_low)
    outer_bias_grad = jnp.sum(outer_low.astype(f32), axis=0)
    inner_low = (matmul(outer_low, back_outer.T) * gelu_slope(inner)).astype(bf16)
    inner_weight_grad = matmul(first_low.T, inner_low)
    inner_bias_grad = jnp.sum(inner_low.astype(f32), axis=0)
    first_grad = matmul(inner_low, back_inner.T) + mid_grad
    first_gain_grad = jnp.sum(first_grad * first_norm, axis=0)
    first_shift_grad = jnp.sum(first_grad, axis=0)
    sum_grad = norm_back(first_grad * back_first.astype(f32), first_norm, first_inverse)
    attended_low = sum_grad.astype(bf16)
    output_weight_grad = matmul(context.T, attended_low)
    context_grad = matmul(attended_low, back_output.T).astype(bf16)
    back_relative_heads = jnp.tile(
        back_relative.reshape(buckets_all, H, DH).transpose(1, 0, 2), (count, 1, 1)
    )
    back_order_heads = jnp.tile(back_order.reshape(2, H, DH).transpose(1, 0, 2), (count, 1, 1))
    back_inputs = (
        head_inputs[0],
        head_inputs[1],
        head_inputs[2],
        head_inputs[3],
        head_inputs[4],
        back_relative_heads,
        back_order_heads,
        query_rows,
        key_rows,
        logsums,
        split(context_grad, half),
    )

    def attend_back(inputs):
        (
            content_h,
            keys_h,
            values_h,
            position_h,
            order_h,
            relative_h,
            orders_h,
            query_row,
            key_row,
            logsum,
            grad_h,
        ) = inputs
        scores = head_scores(
            content_h,
            keys_h,
            position_h,
            order_h,
            relative_h,
            orders_h,
            query_row,
            key_row,
            bucket,
            behind,
            scale,
        )
        probs = jnp.exp(scores - logsum[:, None])
        probs_low = probs.astype(bf16)
        value_part = matmul(probs_low.T, grad_h)
        prob_grad = matmul(grad_h, values_h.T)
        score_low = (
            probs * (prob_grad - jnp.sum(probs * prob_grad, axis=1, keepdims=True))
        ).astype(bf16)
        content_part = matmul(score_low, keys_h) * scale
        key_part = matmul(score_low.T, content_h) * scale
        scaled = score_low.astype(f32) * scale
        bucket_low = jnp.stack(
            [
                jnp.sum(jnp.where(bucket == which, scaled, 0.0), axis=1)
                for which in range(relative_h.shape[0])
            ],
            axis=1,
        ).astype(bf16)
        rank_low = jnp.stack(
            [
                jnp.sum(jnp.where(behind, 0.0, scaled), axis=1),
                jnp.sum(jnp.where(behind, scaled, 0.0), axis=1),
            ],
            axis=1,
        ).astype(bf16)
        position_part = matmul(bucket_low, relative_h)
        table_part = matmul(bucket_low.T, position_h)
        order_part = matmul(rank_low, orders_h)
        ranks_part = matmul(rank_low.T, order_h)
        return (
            content_part,
            key_part,
            value_part,
            position_part,
            order_part,
            table_part,
            ranks_part,
        )

    content_parts, key_parts, value_parts, position_parts, order_parts, table_parts, ranks_parts = (
        lax.map(attend_back, back_inputs)
    )
    content_grad = merge(content_parts, half)
    position_grad = merge(position_parts, half)
    ordering_grad = merge(order_parts, half)
    key_low = merge(key_parts, length).astype(bf16)
    value_low = merge(value_parts, length).astype(bf16)
    relative_table_grad = (
        table_parts.reshape(count, H, buckets_all, DH)
        .sum(axis=0)
        .transpose(1, 0, 2)
        .reshape(buckets_all, width)
    )
    order_table_grad = (
        ranks_parts.reshape(count, H, 2, DH).sum(axis=0).transpose(1, 0, 2).reshape(2, width)
    )
    content_bias_grad = jnp.sum(content_grad, axis=0)
    position_bias_grad = jnp.sum(position_grad, axis=0)
    order_bias_grad = jnp.sum(ordering_grad, axis=0)
    query_low = (content_grad + position_grad + ordering_grad).astype(bf16)
    query_weight_grad = matmul(pooled_low.T, query_low)
    key_weight_grad = matmul(tokens.T, key_low)
    value_weight_grad = matmul(tokens.T, value_low)
    pooled_grad = (sum_grad + matmul(query_low, back_query.T)).reshape(count, half, 1, width)
    shared = joined[:, :, :, None]
    spread = jnp.concatenate(
        [pooled_grad / (1.0 + shared), shared * pooled_grad / (1.0 + shared)], axis=2
    ).reshape(count * length, width)
    tokens_grad = matmul(key_low, back_key.T) + matmul(value_low, back_value.T) + spread
    owned = (
        lax.psum_scatter(query_weight_grad, "shard", scatter_dimension=0, tiled=True),
        lax.psum_scatter(key_weight_grad, "shard", scatter_dimension=0, tiled=True),
        lax.psum_scatter(value_weight_grad, "shard", scatter_dimension=0, tiled=True),
        lax.psum_scatter(output_weight_grad, "shard", scatter_dimension=0, tiled=True),
        lax.psum_scatter(relative_table_grad, "shard", scatter_dimension=1, tiled=True),
        lax.psum_scatter(order_table_grad, "shard", scatter_dimension=1, tiled=True),
        lax.psum_scatter(content_bias_grad, "shard", scatter_dimension=0, tiled=True),
        lax.psum_scatter(position_bias_grad, "shard", scatter_dimension=0, tiled=True),
        lax.psum_scatter(order_bias_grad, "shard", scatter_dimension=0, tiled=True),
        lax.psum_scatter(first_gain_grad, "shard", scatter_dimension=0, tiled=True),
        lax.psum_scatter(first_shift_grad, "shard", scatter_dimension=0, tiled=True),
        lax.psum_scatter(inner_weight_grad, "shard", scatter_dimension=0, tiled=True),
        lax.psum_scatter(inner_bias_grad, "shard", scatter_dimension=0, tiled=True),
        lax.psum_scatter(outer_weight_grad, "shard", scatter_dimension=0, tiled=True),
        lax.psum_scatter(outer_bias_grad, "shard", scatter_dimension=0, tiled=True),
        lax.psum_scatter(second_gain_grad, "shard", scatter_dimension=0, tiled=True),
        lax.psum_scatter(second_shift_grad, "shard", scatter_dimension=0, tiled=True),
    )
    summed = lax.psum(
        (
            owned[0],
            owned[1],
            owned[2],
            owned[3],
            owned[4],
            owned[5],
            owned[6],
            owned[7],
            owned[8],
            owned[9],
            owned[10],
            owned[11],
            owned[12],
            owned[13],
            owned[14],
            owned[15],
            owned[16],
        ),
        "rep",
    )
    return (layer_out, tokens_grad) + tuple(summed)


def solution(mesh):
    placed = (
        P(("rep", "shard"), None),
        P(("rep", "shard"), None),
        P("shard", None),
        P("shard", None),
        P("shard", None),
        P("shard", None),
        P(None, "shard"),
        P(None, "shard"),
        P("shard"),
        P("shard"),
        P("shard"),
        P("shard"),
        P("shard"),
        P("shard", None),
        P("shard"),
        P("shard", None),
        P("shard"),
        P("shard"),
        P("shard"),
        P(("rep", "shard"), None),
    )
    return jax.shard_map(
        body,
        mesh=mesh,
        in_specs=placed,
        out_specs=(
            P(("rep", "shard"), None),
            P(("rep", "shard"), None),
            P("shard", None),
            P("shard", None),
            P("shard", None),
            P("shard", None),
            P(None, "shard"),
            P(None, "shard"),
            P("shard"),
            P("shard"),
            P("shard"),
            P("shard"),
            P("shard"),
            P("shard", None),
            P("shard"),
            P("shard", None),
            P("shard"),
            P("shard"),
            P("shard"),
        ),
        check_vma=False,
    )
```

profile of v0, /device:TPU:0, one launch (start us, length us, event | category | flops | bytes accessed | tf_op | source)
XLA Modules:
  0.0 3188.3 jit_solution(17487337760717336502)
XLA Ops:
  24.7 63.2 %all-reduce.21 = (bf16[768]{0:T(1024)(128)(2,1)S(1)}, bf16[768]{0:T(1024)(128)(2,1)S(1)}, bf16[768]{0:T(1024)(128)(2,1)S(1)}, bf16[768]{0:T(1024)(128)(2,1)S(1)}...) all-reduce(bf16[768]{0:T(1024)(128)(2,1)S(1)} %dynamic-update-slice, ...), channel_id=1, replica_groups=mesh['rep'=2,'shard'=16] {'shard'}, use_global_device_ids=true, to_apply=%add | all-reduce | flops 9216 | bytes 36864
  90.9 17.2 all-gather.1
  108.9 20.3 all-gather
  129.6 7.8 reshape.307
  137.4 12.9 fusion.209
  155.5 6.8 copy.76
  167.7 6.7 copy.71
  174.5 6.5 add_convert_fusion.1
  192.3 631.1 %while.42 = (s32[]{:T(128)}, bf16[12,1024,64]{1,2,0:T(8,128)(2,1)}, f32[12,1024]{1,0:T(8,128)}, s32[12,1024]{1,0:T(8,128)S(1)}, s32[12,2048]{1,0:T(8,128)S(1)}, ...) while((s32[]{:T(128)}, bf16[12,1024,64]{1,2,0:T(8,128)(2,1)}, ...), condition=%wide.region_3.4_spmd.clone.clone.clone.clone, body=%wide.region_0.3_spmd.clone.clone.clone.sunk.clone | while | flops 872676352 | bytes 27910800 | solution.py:219
  194.0 45.1 %fusion.344 = (f32[1024]{0:T(1024)S(1)}, f32[1024,2048]{1,0:T(8,128)S(1)}) fusion(f32[1024]{0:T(1024)S(1)} %bitcast.736, f32[1024]{0:T(1024)S(1)} %bitcast.735, f32[1024]{0:T(1024)S(1)} %bitcast.712, f32[1024]{0:T(1024)S(1)} %bitcast.713, f32[1024]{0:T(1024)S(1)} %bitcast.714, f32[1024]{0:T(1024)S(1)} %bitcast.715, f32[1024]{0:T(1024)S(1)} %bitcast.716, ...), kind=kOutput, calls=%fused_computation.318.clone.3.clone | convolution fusion | flops 591395840 | bytes 9335808 | tf_op jit(solution)/shard_map/while/body/eval_jaxpr/dot_general | solution.py:16
  246.6 45.1 %fusion.344 = (f32[1024]{0:T(1024)S(1)}, f32[1024,2048]{1,0:T(8,128)S(1)}) fusion(f32[1024]{0:T(1024)S(1)} %bitcast.736, f32[1024]{0:T(1024)S(1)} %bitcast.735, f32[1024]{0:T(1024)S(1)} %bitcast.712, f32[1024]{0:T(1024)S(1)} %bitcast.713, f32[1024]{0:T(1024)S(1)} %bitcast.714, f32[1024]{0:T(1024)S(1)} %bitcast.715, f32[1024]{0:T(1024)S(1)} %bitcast.716, ...), kind=kOutput, calls=%fused_computation.318.clone.3.clone | convolution fusion | flops 591395840 | bytes 9335808 | tf_op jit(solution)/shard_map/while/body/eval_jaxpr/dot_general | solution.py:16
  299.2 45.1 %fusion.344 = (f32[1024]{0:T(1024)S(1)}, f32[1024,2048]{1,0:T(8,128)S(1)}) fusion(f32[1024]{0:T(1024)S(1)} %bitcast.736, f32[1024]{0:T(1024)S(1)} %bitcast.735, f32[1024]{0:T(1024)S(1)} %bitcast.712, f32[1024]{0:T(1024)S(1)} %bitcast.713, f32[1024]{0:T(1024)S(1)} %bitcast.714, f32[1024]{0:T(1024)S(1)} %bitcast.715, f32[1024]{0:T(1024)S(1)} %bitcast.716, ...), kind=kOutput, calls=%fused_computation.318.clone.3.clone | convolution fusion | flops 591395840 | bytes 9335808 | tf_op jit(solution)/shard_map/while/body/eval_jaxpr/dot_general | solution.py:16
  351.7 45.1 %fusion.344 = (f32[1024]{0:T(1024)S(1)}, f32[1024,2048]{1,0:T(8,128)S(1)}) fusion(f32[1024]{0:T(1024)S(1)} %bitcast.736, f32[1024]{0:T(1024)S(1)} %bitcast.735, f32[1024]{0:T(1024)S(1)} %bitcast.712, f32[1024]{0:T(1024)S(1)} %bitcast.713, f32[1024]{0:T(1024)S(1)} %bitcast.714, f32[1024]{0:T(1024)S(1)} %bitcast.715, f32[1024]{0:T(1024)S(1)} %bitcast.716, ...), kind=kOutput, calls=%fused_computation.318.clone.3.clone | convolution fusion | flops 591395840 | bytes 9335808 | tf_op jit(solution)/shard_map/while/body/eval_jaxpr/dot_general | solution.py:16
  404.3 45.1 %fusion.344 = (f32[1024]{0:T(1024)S(1)}, f32[1024,2048]{1,0:T(8,128)S(1)}) fusion(f32[1024]{0:T(1024)S(1)} %bitcast.736, f32[1024]{0:T(1024)S(1)} %bitcast.735, f32[1024]{0:T(1024)S(1)} %bitcast.712, f32[1024]{0:T(1024)S(1)} %bitcast.713, f32[1024]{0:T(1024)S(1)} %bitcast.714, f32[1024]{0:T(1024)S(1)} %bitcast.715, f32[1024]{0:T(1024)S(1)} %bitcast.716, ...), kind=kOutput, calls=%fused_computation.318.clone.3.clone | convolution fusion | flops 591395840 | bytes 9335808 | tf_op jit(solution)/shard_map/while/body/eval_jaxpr/dot_general | solution.py:16
  456.8 45.1 %fusion.344 = (f32[1024]{0:T(1024)S(1)}, f32[1024,2048]{1,0:T(8,128)S(1)}) fusion(f32[1024]{0:T(1024)S(1)} %bitcast.736, f32[1024]{0:T(1024)S(1)} %bitcast.735, f32[1024]{0:T(1024)S(1)} %bitcast.712, f32[1024]{0:T(1024)S(1)} %bitcast.713, f32[1024]{0:T(1024)S(1)} %bitcast.714, f32[1024]{0:T(1024)S(1)} %bitcast.715, f32[1024]{0:T(1024)S(1)} %bitcast.716, ...), kind=kOutput, calls=%fused_computation.318.clone.3.clone | convolution fusion | flops 591395840 | bytes 9335808 | tf_op jit(solution)/shard_map/while/body/eval_jaxpr/dot_general | solution.py:16
  509.4 45.1 %fusion.344 = (f32[1024]{0:T(1024)S(1)}, f32[1024,2048]{1,0:T(8,128)S(1)}) fusion(f32[1024]{0:T(1024)S(1)} %bitcast.736, f32[1024]{0:T(1024)S(1)} %bitcast.735, f32[1024]{0:T(1024)S(1)} %bitcast.712, f32[1024]{0:T(1024)S(1)} %bitcast.713, f32[1024]{0:T(1024)S(1)} %bitcast.714, f32[1024]{0:T(1024)S(1)} %bitcast.715, f32[1024]{0:T(1024)S(1)} %bitcast.716, ...), kind=kOutput, calls=%fused_computation.318.clone.3.clone | convolution fusion | flops 591395840 | bytes 9335808 | tf_op jit(solution)/shard_map/while/body/eval_jaxpr/dot_general | solution.py:16
  562.0 45.1 %fusion.344 = (f32[1024]{0:T(1024)S(1)}, f32[1024,2048]{1,0:T(8,128)S(1)}) fusion(f32[1024]{0:T(1024)S(1)} %bitcast.736, f32[1024]{0:T(1024)S(1)} %bitcast.735, f32[1024]{0:T(1024)S(1)} %bitcast.712, f32[1024]{0:T(1024)S(1)} %bitcast.713, f32[1024]{0:T(1024)S(1)} %bitcast.714, f32[1024]{0:T(1024)S(1)} %bitcast.715, f32[1024]{0:T(1024)S(1)} %bitcast.716, ...), kind=kOutput, calls=%fused_computation.318.clone.3.clone | convolution fusion | flops 591395840 | bytes 9335808 | tf_op jit(solution)/shard_map/while/body/eval_jaxpr/dot_general | solution.py:16
  614.5 45.1 %fusion.344 = (f32[1024]{0:T(1024)S(1)}, f32[1024,2048]{1,0:T(8,128)S(1)}) fusion(f32[1024]{0:T(1024)S(1)} %bitcast.736, f32[1024]{0:T(1024)S(1)} %bitcast.735, f32[1024]{0:T(1024)S(1)} %bitcast.712, f32[1024]{0:T(1024)S(1)} %bitcast.713, f32[1024]{0:T(1024)S(1)} %bitcast.714, f32[1024]{0:T(1024)S(1)} %bitcast.715, f32[1024]{0:T(1024)S(1)} %bitcast.716, ...), kind=kOutput, calls=%fused_computation.318.clone.3.clone | convolution fusion | flops 591395840 | bytes 9335808 | tf_op jit(solution)/shard_map/while/body/eval_jaxpr/dot_general | solution.py:16
  667.1 45.1 %fusion.344 = (f32[1024]{0:T(1024)S(1)}, f32[1024,2048]{1,0:T(8,128)S(1)}) fusion(f32[1024]{0:T(1024)S(1)} %bitcast.736, f32[1024]{0:T(1024)S(1)} %bitcast.735, f32[1024]{0:T(1024)S(1)} %bitcast.712, f32[1024]{0:T(1024)S(1)} %bitcast.713, f32[1024]{0:T(1024)S(1)} %bitcast.714, f32[1024]{0:T(1024)S(1)} %bitcast.715, f32[1024]{0:T(1024)S(1)} %bitcast.716, ...), kind=kOutput, calls=%fused_computation.318.clone.3.clone | convolution fusion | flops 591395840 | bytes 9335808 | tf_op jit(solution)/shard_map/while/body/eval_jaxpr/dot_general | solution.py:16
  719.6 45.1 %fusion.344 = (f32[1024]{0:T(1024)S(1)}, f32[1024,2048]{1,0:T(8,128)S(1)}) fusion(f32[1024]{0:T(1024)S(1)} %bitcast.736, f32[1024]{0:T(1024)S(1)} %bitcast.735, f32[1024]{0:T(1024)S(1)} %bitcast.712, f32[1024]{0:T(1024)S(1)} %bitcast.713, f32[1024]{0:T(1024)S(1)} %bitcast.714, f32[1024]{0:T(1024)S(1)} %bitcast.715, f32[1024]{0:T(1024)S(1)} %bitcast.716, ...), kind=kOutput, calls=%fused_computation.318.clone.3.clone | convolution fusion | flops 591395840 | bytes 9335808 | tf_op jit(solution)/shard_map/while/body/eval_jaxpr/dot_general | solution.py:16
  772.2 45.1 %fusion.344 = (f32[1024]{0:T(1024)S(1)}, f32[1024,2048]{1,0:T(8,128)S(1)}) fusion(f32[1024]{0:T(1024)S(1)} %bitcast.736, f32[1024]{0:T(1024)S(1)} %bitcast.735, f32[1024]{0:T(1024)S(1)} %bitcast.712, f32[1024]{0:T(1024)S(1)} %bitcast.713, f32[1024]{0:T(1024)S(1)} %bitcast.714, f32[1024]{0:T(1024)S(1)} %bitcast.715, f32[1024]{0:T(1024)S(1)} %bitcast.716, ...), kind=kOutput, calls=%fused_computation.318.clone.3.clone | convolution fusion | flops 591395840 | bytes 9335808 | tf_op jit(solution)/shard_map/while/body/eval_jaxpr/dot_general | solution.py:16
  831.1 37.5 %fusion.161 = (bf16[1024,3072]{1,0:T(8,128)(2,1)}, f32[1024,3072]{1,0:T(8,128)}) fusion(f32[3072]{0:T(1024)S(1)} %copy-done.39, bf16[768,3072]{1,0:T(8,128)(2,1)} %all-gather.17.cloned.1.call-done, f32[1024,768]{1,0:T(8,128)S(1)} %get-tuple-element.1188, f32[768]{0:T(1024)S(1)} %copy-done.27, f32[768]{0:T(1024)S(1)} %copy-done.25, ...), kind=kOutput, calls=%fused_computation.221 | convolution fusion | flops 5043388416 | bytes 26765312 | tf_op jit(solution)/shard_map/dot_general | solution.py:16
  868.7 10.1 fusion.212
  884.6 13.4 convert_reduce_fusion
  898.1 6.5 multiply_reduce_fusion.1
  911.5 1573.3 %while.43 = (s32[]{:T(128)}, f32[12,1024,64]{1,2,0:T(8,128)}, bf16[12,2048,64]{1,2,0:T(8,128)(2,1)}, bf16[12,2048,64]{1,2,0:T(8,128)(2,1)}, f32[12,1024,64]{1,2,...) while((s32[]{:T(128)}, f32[12,1024,64]{1,2,0:T(8,128)}, ...), condition=%wide.region_48.49_spmd.clone.clone.clone.clone, body=%wide.region_12.48_spmd.clone.clone.clone.sunk.clone | while | flops 2014229504 | bytes 70362368 | solution.py:369
  917.2 46.5 %multiply_reduce_fusion.8 = (f32[1024]{0:T(1024)S(1)}, f32[1024,2048]{1,0:T(8,128)S(1)}) fusion(f32[1024,2048]{1,0:T(8,128)S(1)} %fusion.364, f32[1024]{0:T(1024)S(1)} %bitcast.730, f32[1024]{0:T(1024)S(1)} %bitcast.734, f32[1024]{0:T(1024)S(1)} %bitcast.733, f32[1024]{0:T(1024)S(1)} %bitcast.693, f32[1024]{0:T(1024)S(1)} %bitcast.694, ...), kind=kOutput, calls=%fused_computation.121.clone.3.clone | convolution fusion | flops 595590144 | bytes 17728512 | tf_op jit(solution)/shard_map/while/body/eval_jaxpr/dot_general | solution.py:16
  963.7 63.8 %fusion.370 = (bf16[1024]{0:T(1024)(128)(2,1)S(1)}, bf16[1024]{0:T(1024)(128)(2,1)S(1)}, bf16[1024]{0:T(1024)(128)(2,1)S(1)}, bf16[1024]{0:T(1024)(128)(2,1)S(1)...) fusion(s32[1024]{0:T(1024)S(1)} %get-tuple-element.1888, ...), kind=kLoop, calls=%fused_computation.85.clone.1.clone | loop fusion | flops 329218048 | bytes 21049344 | tf_op jit(solution)/shard_map/while/body/eval_jaxpr/reduce_sum | solution.py:349
  1048.3 46.5 %multiply_reduce_fusion.8 = (f32[1024]{0:T(1024)S(1)}, f32[1024,2048]{1,0:T(8,128)S(1)}) fusion(f32[1024,2048]{1,0:T(8,128)S(1)} %fusion.364, f32[1024]{0:T(1024)S(1)} %bitcast.730, f32[1024]{0:T(1024)S(1)} %bitcast.734, f32[1024]{0:T(1024)S(1)} %bitcast.733, f32[1024]{0:T(1024)S(1)} %bitcast.693, f32[1024]{0:T(1024)S(1)} %bitcast.694, ...), kind=kOutput, calls=%fused_computation.121.clone.3.clone | convolution fusion | flops 595590144 | bytes 17728512 | tf_op jit(solution)/shard_map/while/body/eval_jaxpr/dot_general | solution.py:16
  1094.8 63.8 %fusion.370 = (bf16[1024]{0:T(1024)(128)(2,1)S(1)}, bf16[1024]{0:T(1024)(128)(2,1)S(1)}, bf16[1024]{0:T(1024)(128)(2,1)S(1)}, bf16[1024]{0:T(1024)(128)(2,1)S(1)...) fusion(s32[1024]{0:T(1024)S(1)} %get-tuple-element.1888, ...), kind=kLoop, calls=%fused_computation.85.clone.1.clone | loop fusion | flops 329218048 | bytes 21049344 | tf_op jit(solution)/shard_map/while/body/eval_jaxpr/reduce_sum | solution.py:349
  1179.4 46.5 %multiply_reduce_fusion.8 = (f32[1024]{0:T(1024)S(1)}, f32[1024,2048]{1,0:T(8,128)S(1)}) fusion(f32[1024,2048]{1,0:T(8,128)S(1)} %fusion.364, f32[1024]{0:T(1024)S(1)} %bitcast.730, f32[1024]{0:T(1024)S(1)} %bitcast.734, f32[1024]{0:T(1024)S(1)} %bitcast.733, f32[1024]{0:T(1024)S(1)} %bitcast.693, f32[1024]{0:T(1024)S(1)} %bitcast.694, ...), kind=kOutput, calls=%fused_computation.121.clone.3.clone | convolution fusion | flops 595590144 | bytes 17728512 | tf_op jit(solution)/shard_map/while/body/eval_jaxpr/dot_general | solution.py:16
  1225.9 63.8 %fusion.370 = (bf16[1024]{0:T(1024)(128)(2,1)S(1)}, bf16[1024]{0:T(1024)(128)(2,1)S(1)}, bf16[1024]{0:T(1024)(128)(2,1)S(1)}, bf16[1024]{0:T(1024)(128)(2,1)S(1)...) fusion(s32[1024]{0:T(1024)S(1)} %get-tuple-element.1888, ...), kind=kLoop, calls=%fused_computation.85.clone.1.clone | loop fusion | flops 329218048 | bytes 21049344 | tf_op jit(solution)/shard_map/while/body/eval_jaxpr/reduce_sum | solution.py:349
  1310.4 46.5 %multiply_reduce_fusion.8 = (f32[1024]{0:T(1024)S(1)}, f32[1024,2048]{1,0:T(8,128)S(1)}) fusion(f32[1024,2048]{1,0:T(8,128)S(1)} %fusion.364, f32[1024]{0:T(1024)S(1)} %bitcast.730, f32[1024]{0:T(1024)S(1)} %bitcast.734, f32[1024]{0:T(1024)S(1)} %bitcast.733, f32[1024]{0:T(1024)S(1)} %bitcast.693, f32[1024]{0:T(1024)S(1)} %bitcast.694, ...), kind=kOutput, calls=%fused_computation.121.clone.3.clone | convolution fusion | flops 595590144 | bytes 17728512 | tf_op jit(solution)/shard_map/while/body/eval_jaxpr/dot_general | solution.py:16
  1356.9 63.8 %fusion.370 = (bf16[1024]{0:T(1024)(128)(2,1)S(1)}, bf16[1024]{0:T(1024)(128)(2,1)S(1)}, bf16[1024]{0:T(1024)(128)(2,1)S(1)}, bf16[1024]{0:T(1024)(128)(2,1)S(1)...) fusion(s32[1024]{0:T(1024)S(1)} %get-tuple-element.1888, ...), kind=kLoop, calls=%fused_computation.85.clone.1.clone | loop fusion | flops 329218048 | bytes 21049344 | tf_op jit(solution)/shard_map/while/body/eval_jaxpr/reduce_sum | solution.py:349
  1441.4 46.5 %multiply_reduce_fusion.8 = (f32[1024]{0:T(1024)S(1)}, f32[1024,2048]{1,0:T(8,128)S(1)}) fusion(f32[1024,2048]{1,0:T(8,128)S(1)} %fusion.364, f32[1024]{0:T(1024)S(1)} %bitcast.730, f32[1024]{0:T(1024)S(1)} %bitcast.734, f32[1024]{0:T(1024)S(1)} %bitcast.733, f32[1024]{0:T(1024)S(1)} %bitcast.693, f32[1024]{0:T(1024)S(1)} %bitcast.694, ...), kind=kOutput, calls=%fused_computation.121.clone.3.clone | convolution fusion | flops 595590144 | bytes 17728512 | tf_op jit(solution)/shard_map/while/body/eval_jaxpr/dot_general | solution.py:16
  1488.0 63.8 %fusion.370 = (bf16[1024]{0:T(1024)(128)(2,1)S(1)}, bf16[1024]{0:T(1024)(128)(2,1)S(1)}, bf16[1024]{0:T(1024)(128)(2,1)S(1)}, bf16[1024]{0:T(1024)(128)(2,1)S(1)...) fusion(s32[1024]{0:T(1024)S(1)} %get-tuple-element.1888, ...), kind=kLoop, calls=%fused_computation.85.clone.1.clone | loop fusion | flops 329218048 | bytes 21049344 | tf_op jit(solution)/shard_map/while/body/eval_jaxpr/reduce_sum | solution.py:349
  1572.5 46.5 %multiply_reduce_fusion.8 = (f32[1024]{0:T(1024)S(1)}, f32[1024,2048]{1,0:T(8,128)S(1)}) fusion(f32[1024,2048]{1,0:T(8,128)S(1)} %fusion.364, f32[1024]{0:T(1024)S(1)} %bitcast.730, f32[1024]{0:T(1024)S(1)} %bitcast.734, f32[1024]{0:T(1024)S(1)} %bitcast.733, f32[1024]{0:T(1024)S(1)} %bitcast.693, f32[1024]{0:T(1024)S(1)} %bitcast.694, ...), kind=kOutput, calls=%fused_computation.121.clone.3.clone | convolution fusion | flops 595590144 | bytes 17728512 | tf_op jit(solution)/shard_map/while/body/eval_jaxpr/dot_general | solution.py:16
  1619.0 63.8 %fusion.370 = (bf16[1024]{0:T(1024)(128)(2,1)S(1)}, bf16[1024]{0:T(1024)(128)(2,1)S(1)}, bf16[1024]{0:T(1024)(128)(2,1)S(1)}, bf16[1024]{0:T(1024)(128)(2,1)S(1)...) fusion(s32[1024]{0:T(1024)S(1)} %get-tuple-element.1888, ...), kind=kLoop, calls=%fused_computation.85.clone.1.clone | loop fusion | flops 329218048 | bytes 21049344 | tf_op jit(solution)/shard_map/while/body/eval_jaxpr/reduce_sum | solution.py:349
  1703.6 46.5 %multiply_reduce_fusion.8 = (f32[1024]{0:T(1024)S(1)}, f32[1024,2048]{1,0:T(8,128)S(1)}) fusion(f32[1024,2048]{1,0:T(8,128)S(1)} %fusion.364, f32[1024]{0:T(1024)S(1)} %bitcast.730, f32[1024]{0:T(1024)S(1)} %bitcast.734, f32[1024]{0:T(1024)S(1)} %bitcast.733, f32[1024]{0:T(1024)S(1)} %bitcast.693, f32[1024]{0:T(1024)S(1)} %bitcast.694, ...), kind=kOutput, calls=%fused_computation.121.clone.3.clone | convolution fusion | flops 595590144 | bytes 17728512 | tf_op jit(solution)/shard_map/while/body/eval_jaxpr/dot_general | solution.py:16
  1750.1 63.8 %fusion.370 = (bf16[1024]{0:T(1024)(128)(2,1)S(1)}, bf16[1024]{0:T(1024)(128)(2,1)S(1)}, bf16[1024]{0:T(1024)(128)(2,1)S(1)}, bf16[1024]{0:T(1024)(128)(2,1)S(1)...) fusion(s32[1024]{0:T(1024)S(1)} %get-tuple-element.1888, ...), kind=kLoop, calls=%fused_computation.85.clone.1.clone | loop fusion | flops 329218048 | bytes 21049344 | tf_op jit(solution)/shard_map/while/body/eval_jaxpr/reduce_sum | solution.py:349
  1834.7 46.5 %multiply_reduce_fusion.8 = (f32[1024]{0:T(1024)S(1)}, f32[1024,2048]{1,0:T(8,128)S(1)}) fusion(f32[1024,2048]{1,0:T(8,128)S(1)} %fusion.364, f32[1024]{0:T(1024)S(1)} %bitcast.730, f32[1024]{0:T(1024)S(1)} %bitcast.734, f32[1024]{0:T(1024)S(1)} %bitcast.733, f32[1024]{0:T(1024)S(1)} %bitcast.693, f32[1024]{0:T(1024)S(1)} %bitcast.694, ...), kind=kOutput, calls=%fused_computation.121.clone.3.clone | convolution fusion | flops 595590144 | bytes 17728512 | tf_op jit(solution)/shard_map/while/body/eval_jaxpr/dot_general | solution.py:16
  1881.2 63.8 %fusion.370 = (bf16[1024]{0:T(1024)(128)(2,1)S(1)}, bf16[1024]{0:T(1024)(128)(2,1)S(1)}, bf16[1024]{0:T(1024)(128)(2,1)S(1)}, bf16[1024]{0:T(1024)(128)(2,1)S(1)...) fusion(s32[1024]{0:T(1024)S(1)} %get-tuple-element.1888, ...), kind=kLoop, calls=%fused_computation.85.clone.1.clone | loop fusion | flops 329218048 | bytes 21049344 | tf_op jit(solution)/shard_map/while/body/eval_jaxpr/reduce_sum | solution.py:349
  1965.7 46.5 %multiply_reduce_fusion.8 = (f32[1024]{0:T(1024)S(1)}, f32[1024,2048]{1,0:T(8,128)S(1)}) fusion(f32[1024,2048]{1,0:T(8,128)S(1)} %fusion.364, f32[1024]{0:T(1024)S(1)} %bitcast.730, f32[1024]{0:T(1024)S(1)} %bitcast.734, f32[1024]{0:T(1024)S(1)} %bitcast.733, f32[1024]{0:T(1024)S(1)} %bitcast.693, f32[1024]{0:T(1024)S(1)} %bitcast.694, ...), kind=kOutput, calls=%fused_computation.121.clone.3.clone | convolution fusion | flops 595590144 | bytes 17728512 | tf_op jit(solution)/shard_map/while/body/eval_jaxpr/dot_general | solution.py:16
  2012.2 63.8 %fusion.370 = (bf16[1024]{0:T(1024)(128)(2,1)S(1)}, bf16[1024]{0:T(1024)(128)(2,1)S(1)}, bf16[1024]{0:T(1024)(128)(2,1)S(1)}, bf16[1024]{0:T(1024)(128)(2,1)S(1)...) fusion(s32[1024]{0:T(1024)S(1)} %get-tuple-element.1888, ...), kind=kLoop, calls=%fused_computation.85.clone.1.clone | loop fusion | flops 329218048 | bytes 21049344 | tf_op jit(solution)/shard_map/while/body/eval_jaxpr/reduce_sum | solution.py:349
  2096.8 46.5 %multiply_reduce_fusion.8 = (f32[1024]{0:T(1024)S(1)}, f32[1024,2048]{1,0:T(8,128)S(1)}) fusion(f32[1024,2048]{1,0:T(8,128)S(1)} %fusion.364, f32[1024]{0:T(1024)S(1)} %bitcast.730, f32[1024]{0:T(1024)S(1)} %bitcast.734, f32[1024]{0:T(1024)S(1)} %bitcast.733, f32[1024]{0:T(1024)S(1)} %bitcast.693, f32[1024]{0:T(1024)S(1)} %bitcast.694, ...), kind=kOutput, calls=%fused_computation.121.clone.3.clone | convolution fusion | flops 595590144 | bytes 17728512 | tf_op jit(solution)/shard_map/while/body/eval_jaxpr/dot_general | solution.py:16
  2143.3 63.8 %fusion.370 = (bf16[1024]{0:T(1024)(128)(2,1)S(1)}, bf16[1024]{0:T(1024)(128)(2,1)S(1)}, bf16[1024]{0:T(1024)(128)(2,1)S(1)}, bf16[1024]{0:T(1024)(128)(2,1)S(1)...) fusion(s32[1024]{0:T(1024)S(1)} %get-tuple-element.1888, ...), kind=kLoop, calls=%fused_computation.85.clone.1.clone | loop fusion | flops 329218048 | bytes 21049344 | tf_op jit(solution)/shard_map/while/body/eval_jaxpr/reduce_sum | solution.py:349
  2227.9 46.5 %multiply_reduce_fusion.8 = (f32[1024]{0:T(1024)S(1)}, f32[1024,2048]{1,0:T(8,128)S(1)}) fusion(f32[1024,2048]{1,0:T(8,128)S(1)} %fusion.364, f32[1024]{0:T(1024)S(1)} %bitcast.730, f32[1024]{0:T(1024)S(1)} %bitcast.734, f32[1024]{0:T(1024)S(1)} %bitcast.733, f32[1024]{0:T(1024)S(1)} %bitcast.693, f32[1024]{0:T(1024)S(1)} %bitcast.694, ...), kind=kOutput, calls=%fused_computation.121.clone.3.clone | convolution fusion | flops 595590144 | bytes 17728512 | tf_op jit(solution)/shard_map/while/body/eval_jaxpr/dot_general | solution.py:16
  2274.4 63.8 %fusion.370 = (bf16[1024]{0:T(1024)(128)(2,1)S(1)}, bf16[1024]{0:T(1024)(128)(2,1)S(1)}, bf16[1024]{0:T(1024)(128)(2,1)S(1)}, bf16[1024]{0:T(1024)(128)(2,1)S(1)...) fusion(s32[1024]{0:T(1024)S(1)} %get-tuple-element.1888, ...), kind=kLoop, calls=%fused_computation.85.clone.1.clone | loop fusion | flops 329218048 | bytes 21049344 | tf_op jit(solution)/shard_map/while/body/eval_jaxpr/reduce_sum | solution.py:349
  2358.9 46.5 %multiply_reduce_fusion.8 = (f32[1024]{0:T(1024)S(1)}, f32[1024,2048]{1,0:T(8,128)S(1)}) fusion(f32[1024,2048]{1,0:T(8,128)S(1)} %fusion.364, f32[1024]{0:T(1024)S(1)} %bitcast.730, f32[1024]{0:T(1024)S(1)} %bitcast.734, f32[1024]{0:T(1024)S(1)} %bitcast.733, f32[1024]{0:T(1024)S(1)} %bitcast.693, f32[1024]{0:T(1024)S(1)} %bitcast.694, ...), kind=kOutput, calls=%fused_computation.121.clone.3.clone | convolution fusion | flops 595590144 | bytes 17728512 | tf_op jit(solution)/shard_map/while/body/eval_jaxpr/dot_general | solution.py:16
  2405.5 63.8 %fusion.370 = (bf16[1024]{0:T(1024)(128)(2,1)S(1)}, bf16[1024]{0:T(1024)(128)(2,1)S(1)}, bf16[1024]{0:T(1024)(128)(2,1)S(1)}, bf16[1024]{0:T(1024)(128)(2,1)S(1)...) fusion(s32[1024]{0:T(1024)S(1)} %get-tuple-element.1888, ...), kind=kLoop, calls=%fused_computation.85.clone.1.clone | loop fusion | flops 329218048 | bytes 21049344 | tf_op jit(solution)/shard_map/while/body/eval_jaxpr/reduce_sum | solution.py:349
  2484.9 7.0 convolution_bitcast_fusion.5
  2521.1 10.7 fusion.196
  2533.7 10.4 fusion.193
  2557.1 64.4 %reduce-scatter.27.cloned.1.call-done = f32[48,768]{1,0:T(8,128)} async-done(((f32[768,768]{1,0:T(8,128)}), f32[48,768]{1,0:T(8,128)}) %reduce-scatter.27.cloned.1.call-update) | async-done | bytes 147472
  2623.3 63.9 %reduce-scatter.19.cloned.1.call-done = f32[48,768]{1,0:T(8,128)} async-done(((f32[768,768]{1,0:T(8,128)}), f32[48,768]{1,0:T(8,128)}) %reduce-scatter.19.cloned.1.call-update) | async-done | bytes 147472 | tf_op jit(solution)/shard_map/reduce_scatter | solution.py:402
  2687.3 66.7 %reduce-scatter.17.cloned.1.call-done = f32[48,768]{1,0:T(8,128)} async-done(((f32[768,768]{1,0:T(8,128)}), f32[48,768]{1,0:T(8,128)}) %reduce-scatter.17.cloned.1.call-update) | async-done | bytes 147472 | tf_op jit(solution)/shard_map/reduce_scatter | solution.py:399
  2754.0 114.5 %reduce-scatter.21.cloned.1.call-done = f32[48,3072]{1,0:T(8,128)} async-done(((f32[768,3072]{1,0:T(8,128)}), f32[48,3072]{1,0:T(8,128)}) %reduce-scatter.21.cloned.1.call-update) | async-done | bytes 589840 | tf_op jit(solution)/shard_map/reduce_scatter | solution.py:410
  2868.5 115.7 %reduce-scatter.23.cloned.1.call-done = f32[192,768]{1,0:T(8,128)} async-done(((f32[3072,768]{1,0:T(8,128)}), f32[192,768]{1,0:T(8,128)}) %reduce-scatter.23.cloned.1.call-update) | async-done | bytes 589840 | tf_op jit(solution)/shard_map/reduce_scatter | solution.py:412
  2990.4 60.4 %all-reduce.18 = (f32[768]{0:T(1024)S(1)}, f32[768]{0:T(1024)S(1)}, f32[768]{0:T(1024)S(1)}, f32[768]{0:T(1024)S(1)}, f32[768]{0:T(1024)S(1)}, /*index=5*/f32[30...) all-reduce(f32[768]{0:T(1024)S(1)} %reduce_sum.500, ...), channel_id=8, replica_groups=mesh['rep'=2,'shard'=16] {'shard'}, use_global_device_ids=true, to_apply=%region_62.63.clone | all-reduce | flops 9216 | bytes 73728
  3051.3 10.3 copy.82
  3061.7 8.6 reshape.303
  3080.4 20.9 reduce-scatter.29.cloned.1.call-done
  3102.2 8.9 all-reduce.19
  3111.1 59.9 %all-reduce.24.cloned.1.call-done = (f32[48,768]{1,0:T(8,128)}, f32[48,768]{0,1:T(8,128)}, f32[48,768]{0,1:T(8,128)}, f32[48,768]{1,0:T(8,128)}, f32[48,3072]{1,0:T(8,128)}, /*index=5*/f32[192,768]{1,0:T(8,128)}) async-done(((f32[48,768]{1,0:T(8,128)}, f32[48,768]{0,1:T(8,128)}, f32[48,768]{0,1:T(8,128)}, f32[48,768]{1,0:T(8,128)}, f32[48,3072]{1,0:T(8,128)}, /*index=5*/f32[192,768]{1,0:T(8,128)}), ...) | async-done | bytes 1769488 | tf_op jit(solution)/shard_map/psum | solution.py:417
  (1045 shorter events, 469.4 us)
Async XLA Ops:
  7.2 143.0 %all-gather.13.cloned.1.call-start = ((), (), s32[]{:S(2)}) async-start(), calls=%async_computation.10 | async-start | bytes 1253376 | tf_op jit(solution)/shard_map/all_gather | solution.py:100
  7.9 154.4 %all-gather.11.cloned.1.call-start = ((), (), s32[]{:S(2)}) async-start(), calls=%async_computation.9 | async-start | bytes 1253376 | tf_op jit(solution)/shard_map/all_gather | solution.py:99
  8.7 165.8 %all-gather.9.cloned.1.call-start = ((), (), s32[]{:S(2)}) async-start(), calls=%async_computation.8 | async-start | bytes 1253376 | tf_op jit(solution)/shard_map/all_gather | solution.py:98
  9.4 814.1 %all-gather.15.cloned.1.call-start = ((), (), s32[]{:S(2)}) async-start(), calls=%async_computation.11 | async-start | bytes 1253376 | tf_op jit(solution)/shard_map/all_gather | solution.py:101
  10.0 821.1 %all-gather.17.cloned.1.call-start = ((), (), s32[]{:S(2)}) async-start(), calls=%async_computation.12 | async-start | bytes 5013504 | tf_op jit(solution)/shard_map/all_gather | solution.py:109
  10.6 858.1 %all-gather.19.cloned.1.call-start = ((), (), s32[]{:S(2)}) async-start(), calls=%async_computation.13 | async-start | bytes 5013504 | tf_op jit(solution)/shard_map/all_gather | solution.py:111
  11.1 2544.1 %reduce-scatter.25.cloned.1.call-start = ((), (), s32[]{:S(2)}) async-start(), calls=%async_computation.18 | async-start | bytes 2506752
  17.1 157.3 %copy-start.33 = (f32[1,1024]{1,0:T(1,128)}, f32[1,1024]{1,0:T(1,128)S(1)}, u32[]{:S(2)}) copy-start(f32[1,1024]{1,0:T(1,128)S(1)} %compare_convert_fusion) | copy-start | bytes 12292
  17.1 157.3 %copy-start.42 = (f32[1024]{0:T(1024)}, f32[1024]{0:T(1024)S(1)}, u32[]{:S(2)}) copy-start(f32[1024]{0:T(1024)S(1)} %broadcast_add_fusion) | copy-start | bytes 12292
  137.4 12.9 copy-start.9
  180.9 11.4 copy-start.30
  192.3 632.7 %copy-start.34 = (f32[1,1024]{1,0:T(1,128)S(1)}, f32[1,1024]{1,0:T(1,128)}, u32[]{:S(2)}) copy-start(f32[1,1024]{1,0:T(1,128)} %copy-done.33) | copy-start | bytes 12292
  192.3 632.7 %copy-start.43 = (f32[1024]{0:T(1024)S(1)}, f32[1024]{0:T(1024)}, u32[]{:S(2)}) copy-start(f32[1024]{0:T(1024)} %copy-done.42) | copy-start | bytes 12292
  830.5 74.1 %copy-start = (f32[1024,768]{1,0:T(8,128)}, f32[1024,768]{1,0:T(8,128)S(1)}, u32[]{:S(2)}) copy-start(f32[1024,768]{1,0:T(8,128)S(1)} %get-tuple-element.1188) | copy-start | bytes 9437188
  830.5 74.0 %copy-start.18 = (f32[1024]{0:T(1024)}, f32[1024]{0:T(1024)S(1)}, u32[]{:S(2)}) copy-start(f32[1024]{0:T(1024)S(1)} %broadcast_multiply_fusion.5) | copy-start | bytes 12292
  831.1 73.5 %copy-start.20 = (f32[1024]{0:T(1024)}, f32[1024]{0:T(1024)S(1)}, u32[]{:S(2)}) copy-start(f32[1024]{0:T(1024)S(1)} %add_rsqrt_fusion.1) | copy-start | bytes 12292
  831.1 37.6 %copy-start.41 = (f32[768]{0:T(1024)S(1)}, f32[768]{0:T(1024)}, u32[]{:S(2)}) copy-start(f32[768]{0:T(1024)} %convert_element_type.3263) | copy-start | bytes 9220
  868.7 15.9 slice-start.4
  868.7 10.7 copy-start.6
  868.7 10.7 copy-start.29
  868.7 13.0 copy-start.31
  868.7 15.9 slice-start.5
  881.7 16.3 slice-start.2
  884.6 13.5 copy-start.7
  884.6 13.4 slice-start.3
  911.7 52.1 %copy-start.16 = (s32[12,2048]{1,0:T(8,128)}, s32[12,2048]{1,0:T(8,128)S(1)}, u32[]{:S(2)}) copy-start(s32[12,2048]{1,0:T(8,128)S(1)} %get-tuple-element.1878) | copy-start | bytes 294916 | tf_op jit(solution)/shard_map/while
  1029.8 13.0 copy-start.17
  1042.8 52.0 %copy-start.16 = (s32[12,2048]{1,0:T(8,128)}, s32[12,2048]{1,0:T(8,128)S(1)}, u32[]{:S(2)}) copy-start(s32[12,2048]{1,0:T(8,128)S(1)} %get-tuple-element.1878) | copy-start | bytes 294916 | tf_op jit(solution)/shard_map/while
  1160.9 13.0 copy-start.17
  1173.9 52.0 %copy-start.16 = (s32[12,2048]{1,0:T(8,128)}, s32[12,2048]{1,0:T(8,128)S(1)}, u32[]{:S(2)}) copy-start(s32[12,2048]{1,0:T(8,128)S(1)} %get-tuple-element.1878) | copy-start | bytes 294916 | tf_op jit(solution)/shard_map/while
  1292.0 12.9 copy-start.17
  1304.9 52.0 %copy-start.16 = (s32[12,2048]{1,0:T(8,128)}, s32[12,2048]{1,0:T(8,128)S(1)}, u32[]{:S(2)}) copy-start(s32[12,2048]{1,0:T(8,128)S(1)} %get-tuple-element.1878) | copy-start | bytes 294916 | tf_op jit(solution)/shard_map/while
  1423.0 12.9 copy-start.17
  1435.9 52.0 %copy-start.16 = (s32[12,2048]{1,0:T(8,128)}, s32[12,2048]{1,0:T(8,128)S(1)}, u32[]{:S(2)}) copy-start(s32[12,2048]{1,0:T(8,128)S(1)} %get-tuple-element.1878) | copy-start | bytes 294916 | tf_op jit(solution)/shard_map/while
  1554.0 13.0 copy-start.17
  1567.0 52.0 %copy-start.16 = (s32[12,2048]{1,0:T(8,128)}, s32[12,2048]{1,0:T(8,128)S(1)}, u32[]{:S(2)}) copy-start(s32[12,2048]{1,0:T(8,128)S(1)} %get-tuple-element.1878) | copy-start | bytes 294916 | tf_op jit(solution)/shard_map/while
  1685.1 13.0 copy-start.17
  1698.1 52.0 %copy-start.16 = (s32[12,2048]{1,0:T(8,128)}, s32[12,2048]{1,0:T(8,128)S(1)}, u32[]{:S(2)}) copy-start(s32[12,2048]{1,0:T(8,128)S(1)} %get-tuple-element.1878) | copy-start | bytes 294916 | tf_op jit(solution)/shard_map/while
  1816.2 12.9 copy-start.17
  1829.1 52.0 %copy-start.16 = (s32[12,2048]{1,0:T(8,128)}, s32[12,2048]{1,0:T(8,128)S(1)}, u32[]{:S(2)}) copy-start(s32[12,2048]{1,0:T(8,128)S(1)} %get-tuple-element.1878) | copy-start | bytes 294916 | tf_op jit(solution)/shard_map/while
  1947.2 12.9 copy-start.17
  1960.2 52.0 %copy-start.16 = (s32[12,2048]{1,0:T(8,128)}, s32[12,2048]{1,0:T(8,128)S(1)}, u32[]{:S(2)}) copy-start(s32[12,2048]{1,0:T(8,128)S(1)} %get-tuple-element.1878) | copy-start | bytes 294916 | tf_op jit(solution)/shard_map/while
  2078.3 13.0 copy-start.17
  2091.3 52.0 %copy-start.16 = (s32[12,2048]{1,0:T(8,128)}, s32[12,2048]{1,0:T(8,128)S(1)}, u32[]{:S(2)}) copy-start(s32[12,2048]{1,0:T(8,128)S(1)} %get-tuple-element.1878) | copy-start | bytes 294916 | tf_op jit(solution)/shard_map/while
  2209.4 13.0 copy-start.17
  2222.4 52.0 %copy-start.16 = (s32[12,2048]{1,0:T(8,128)}, s32[12,2048]{1,0:T(8,128)S(1)}, u32[]{:S(2)}) copy-start(s32[12,2048]{1,0:T(8,128)S(1)} %get-tuple-element.1878) | copy-start | bytes 294916 | tf_op jit(solution)/shard_map/while
  2340.5 13.0 copy-start.17
  2353.4 52.0 %copy-start.16 = (s32[12,2048]{1,0:T(8,128)}, s32[12,2048]{1,0:T(8,128)S(1)}, u32[]{:S(2)}) copy-start(s32[12,2048]{1,0:T(8,128)S(1)} %get-tuple-element.1878) | copy-start | bytes 294916 | tf_op jit(solution)/shard_map/while
  2471.5 12.9 copy-start.17
  2484.9 10.2 copy-start.3
  2495.0 126.5 %reduce-scatter.27.cloned.1.call-start = ((), (), s32[]{:S(2)}) async-start(), calls=%async_computation.19 | async-start | bytes 2506752
  2504.0 183.2 %reduce-scatter.19.cloned.1.call-start = ((), (), s32[]{:S(2)}) async-start(), calls=%async_computation.15 | async-start | bytes 2506752 | tf_op jit(solution)/shard_map/reduce_scatter | solution.py:402
  2509.6 244.4 %reduce-scatter.17.cloned.1.call-start = ((), (), s32[]{:S(2)}) async-start(), calls=%async_computation.14 | async-start | bytes 2506752 | tf_op jit(solution)/shard_map/reduce_scatter | solution.py:399
  2521.0 347.4 %reduce-scatter.21.cloned.1.call-start = ((), (), s32[]{:S(2)}) async-start(), calls=%async_computation.16 | async-start | bytes 10027008 | tf_op jit(solution)/shard_map/reduce_scatter | solution.py:410
  2531.8 452.3 %reduce-scatter.23.cloned.1.call-start = ((), (), s32[]{:S(2)}) async-start(), calls=%async_computation.17 | async-start | bytes 10027008 | tf_op jit(solution)/shard_map/reduce_scatter | solution.py:412
  2544.1 535.5 %reduce-scatter.31.cloned.1.call-start = ((), (), s32[]{:S(2)}) async-start(), calls=%async_computation.21 | async-start | bytes 417792
  2545.2 556.2 %reduce-scatter.29.cloned.1.call-start = ((), (), s32[]{:S(2)}) async-start(), calls=%async_computation.20 | async-start | bytes 417792
  2547.6 623.4 %all-reduce.24.cloned.1.call-start = ((), (), s32[]{:S(2)}) async-start(), calls=%async_computation.22 | async-start | bytes 4521984 | tf_op jit(solution)/shard_map/psum | solution.py:417
  2554.1 436.3 %copy-start.32 = (f32[768]{0:T(1024)S(1)}, f32[768]{0:T(1024)}, u32[]{:S(2)}) copy-start(f32[768]{0:T(1024)} %get-tuple-element.1099) | copy-start | bytes 9220
  2554.1 436.3 %copy-start.36 = (f32[768]{0:T(1024)S(1)}, f32[768]{0:T(1024)}, u32[]{:S(2)}) copy-start(f32[768]{0:T(1024)} %get-tuple-element.991) | copy-start | bytes 9220
  2554.1 436.3 %copy-start.37 = (f32[768]{0:T(1024)S(1)}, f32[768]{0:T(1024)}, u32[]{:S(2)}) copy-start(f32[768]{0:T(1024)} %get-tuple-element.996) | copy-start | bytes 9220
  2554.1 436.3 %copy-start.40 = (f32[3072]{0:T(1024)S(1)}, f32[3072]{0:T(1024)}, u32[]{:S(2)}) copy-start(f32[3072]{0:T(1024)} %get-tuple-element.1194) | copy-start | bytes 36868
  2554.1 436.3 %copy-start.45 = (f32[768]{0:T(1024)S(1)}, f32[768]{0:T(1024)}, u32[]{:S(2)}) copy-start(f32[768]{0:T(1024)} %get-tuple-element.989) | copy-start | bytes 9220
  2554.1 436.3 %copy-start.46 = (f32[768]{0:T(1024)S(1)}, f32[768]{0:T(1024)}, u32[]{:S(2)}) copy-start(f32[768]{0:T(1024)} %get-tuple-element.994) | copy-start | bytes 9220
  (28 other events, 138.6 us)
Sparse Core Ops, SparseCore 0:
  10.3 41.1 all-gather.12
  53.7 37.4 all-gather.10
  93.6 37.7 all-gather.8
  133.5 37.1 all-gather.14
  172.7 52.1 all-gather.16
  227.1 51.8 all-gather.18
  2495.1 60.1 reduce-scatter.24
  2559.5 61.9 reduce-scatter.26
  2625.3 61.9 reduce-scatter.18
  2691.9 61.9 reduce-scatter.16
  2758.1 110.3 reduce-scatter.20
  2873.0 111.1 reduce-scatter.22
  2987.6 55.3 reduce-scatter.30
  3046.8 54.5 reduce-scatter.28
  3104.5 66.4 all-reduce.23
where the time goes:
time: 3200 us; the launch traced here: 3190 us
  matrix products  1540 us (48%)
  other arithmetic  802 us (25%)
  waiting for transfers between devices  511 us (16%)
  blocking collectives  170 us (5%)
  local copies, waits for them, and re-layouts  144 us (4%)
    dot_general x198, matrix products, matmul(): return jnp.dot(left, right, preferred_element_type=jnp.float32)  1540 us
    reduce_sum x12, other arithmetic, attend_back(): jnp.sum(jnp.where(behind, 0.0, scaled), axis=1)  765 us
    unnamed x2, blocking collectives  124 us
    reduce_scatter x1, waiting for transfers between devices, body(): lax.psum_scatter(outer_weight_grad, 'shard', scatter_dimension=0, tiled=T...  116 us
    reduce_scatter x1, waiting for transfers between devices, body(): lax.psum_scatter(inner_weight_grad, 'shard', scatter_dimension=0, tiled=T...  115 us
    unnamed x19, waiting for transfers between devices  90.3 us
    reduce_scatter x1, waiting for transfers between devices, body(): lax.psum_scatter(query_weight_grad, 'shard', scatter_dimension=0, tiled=T...  66.7 us
  transfers between devices with their start and end apart: 15, of which 8 were waited for; matrix products, arithmetic and copies ran while one was open for 27% of the time, Pallas kernels for 0%

commit v1 on v0

v1 whole, which is shorter than its diff:
```python
import math
import jax
import jax.numpy as jnp
import numpy as np
from jax import lax
from jax.experimental import pallas as pl
from jax.experimental.pallas import tpu as pltpu
from jax.sharding import PartitionSpec as P

LIMITS = (1, 2, 3, 4, 5, 6, 7, 8, 12, 16, 24, 32, 48, 64, 128)
BQ = 128
NEAR = 640
CHUNK = 256
LOG2E = math.log2(math.e)
LN2 = math.log(2.0)
BIG = 1e30
f32 = jnp.float32
bf16 = jnp.bfloat16


def bucket_of(offset):
    distance = np.abs(offset)
    passed = sum((distance >= limit).astype(np.int32) for limit in LIMITS)
    return np.where(offset < 0, 15 + passed + (distance >= 256), passed).astype(np.int32)


def near_index():
    row = np.arange(BQ)[None, :, None]
    tile = np.arange(-2, 3)[:, None, None]
    lane = np.arange(128)[None, None, :]
    return bucket_of(128 * tile + lane - 2 * row)


def bucket_onehot():
    out = np.zeros((7 * 128, 128), np.float32)
    offsets = np.concatenate([np.full(256, -300), np.arange(-256, 128), np.full(256, 300)])
    out[np.arange(896), bucket_of(offsets)] = 1
    out[:, 32] = offsets >= 0
    out[:, 33] = offsets < 0
    return out


def nt(left, right):
    return lax.dot_general(left, right, (((1,), (1,)), ((), ())), preferred_element_type=f32)


def nn(left, right):
    return lax.dot_general(left, right, (((1,), (0,)), ((), ())), preferred_element_type=f32)


def tn(left, right):
    return lax.dot_general(left, right, (((0,), (0,)), ((), ())), preferred_element_type=f32)


def halves(array):
    low = lax.broadcasted_iota(jnp.int32, array.shape, 1) < 64
    zero = jnp.zeros_like(array)
    return jnp.where(low, array, zero), jnp.where(low, zero, array)


def pick(array):
    half = array.shape[0] // 2
    low = lax.broadcasted_iota(jnp.int32, (half, 128), 1) < 64
    return jnp.where(low, array[:half], array[half:])


def take(table, index):
    return jnp.take_along_axis(table, index, axis=1, mode="promise_in_bounds")


def forward_kernel(
    behind_ref, ahead_ref, content_ref, position_ref, ordering_ref, key_ref, value_ref,
    relative_ref, order_ref, away_ref, document_ref, index_ref,
    probs_ref, context_ref, mixed_ref, inverse_ref,
    keys, values, table, scores, peak, total,
):
    step = pl.program_id(1)
    length = key_ref.shape[0]

    @pl.when(step == 0)
    def _():
        keys[: 256, :128] = jnp.zeros((256, 128), bf16)
        keys[256 + length :, :128] = jnp.zeros((256, 128), bf16)
        keys[256 : 256 + length, :128] = key_ref[...]
        keys[:, 128:] = away_ref[...]
        values[: 256, :128] = jnp.zeros((256, 128), bf16)
        values[256 + length :, :128] = jnp.zeros((256, 128), bf16)
        values[256 : 256 + length, :128] = value_ref[...]
        values[:, 128:] = jnp.ones((length + 512, 128), bf16)
        table[...] = jnp.zeros((256, 256), bf16)
        even, odd = halves(relative_ref[...])
        after = lax.broadcasted_iota(jnp.int32, (32, 128), 0) < 16
        orders = jnp.where(after, order_ref[0:1, :].astype(f32), order_ref[1:2, :].astype(f32))
        even_order, odd_order = halves(orders)
        table[0:32, :128] = even
        table[128:160, :128] = odd
        table[0:32, 128:] = even_order.astype(bf16)
        table[128:160, 128:] = odd_order.astype(bf16)

    even, odd = halves(content_ref[...])
    document = document_ref[...]
    query = jnp.concatenate(
        [jnp.concatenate([even, document], 1), jnp.concatenate([odd, document], 1)], 0
    )
    places = nt(jnp.concatenate([position_ref[...], ordering_ref[...]], 1), table[...]) * (0.125 * LOG2E)
    place = (places[:, :128], places[:, 128:])
    near = pl.multiple_of(step * 256, 256)
    near_scores = nt(query, keys[pl.ds(near, NEAR), :])
    best = None
    for tile in range(5):
        index = index_ref[tile]
        bias = jnp.concatenate([take(place[0], index), take(place[1], index)], 0)
        part = near_scores[:, tile * 128 : tile * 128 + 128] + bias
        scores[:, pl.ds(near + tile * 128, 128)] = part
        best = part if best is None else jnp.maximum(best, part)
    peak[...] = best
    behind, ahead = behind_ref[step], ahead_ref[step]

    def far_scores(start, bias):
        part = nt(query, keys[pl.ds(start, CHUNK), :]) + bias
        scores[:, pl.ds(start, CHUNK)] = part
        peak[...] = jnp.maximum(peak[...], jnp.maximum(part[:, :128], part[:, 128:]))

    @pl.when(behind > 0)
    def _():
        bias = jnp.concatenate([place[0][:, 31:32], place[1][:, 31:32]], 0)

        @pl.loop(0, behind)
        def _(chunk):
            far_scores(pl.multiple_of(near - 256 * (chunk + 1), 128), bias)

    @pl.when(ahead > 0)
    def _():
        bias = jnp.concatenate([place[0][:, 15:16], place[1][:, 15:16]], 0)

        @pl.loop(0, ahead)
        def _(chunk):
            far_scores(pl.multiple_of(near + NEAR + 256 * chunk, 128), bias)

    top = jnp.max(peak[...], axis=1, keepdims=True)
    probs = jnp.exp2(scores[:, pl.ds(near, NEAR)] - top).astype(bf16)
    probs_ref[0, 0, :, pl.ds(near, NEAR)] = probs
    total[...] = nn(probs, values[pl.ds(near, NEAR), :])

    def far_total(start):
        probs = jnp.exp2(scores[:, pl.ds(start, CHUNK)] - top).astype(bf16)
        probs_ref[0, 0, :, pl.ds(start, CHUNK)] = probs
        total[...] += nn(probs, values[pl.ds(start, CHUNK), :])

    @pl.loop(0, behind)
    def _(chunk):
        far_total(pl.multiple_of(near - 256 * (chunk + 1), 128))

    @pl.loop(0, ahead)
    def _(chunk):
        far_total(pl.multiple_of(near + NEAR + 256 * chunk, 128))

    inverse = 1.0 / total[:, 128:]
    mixed = pick(total[:, :128] * inverse)
    inverse_ref[...] = pick(inverse)
    mixed_ref[...] = mixed
    context_ref[...] = mixed.astype(bf16)


def backward_kernel(
    behind_ref, ahead_ref, probs_ref, grad_ref, mixed_ref, inverse_ref, content_ref, position_ref, ordering_ref,
    key_ref, value_ref, relative_ref, order_ref, turn_ref, onehot_ref,
    query_ref, key_low_ref, value_low_ref, relative_out, order_out, sums_out,
    keys, values, table, key_total, value_total, query_total, far_behind, far_ahead, bucket, table_total, sums,
):
    step = pl.program_id(1)
    length = key_ref.shape[0]

    @pl.when(step == 0)
    def _():
        for scratch, ref in ((keys, key_ref), (values, value_ref)):
            scratch[:256, :] = jnp.zeros((256, 128), bf16)
            scratch[256 + length :, :] = jnp.zeros((256, 128), bf16)
            scratch[256 : 256 + length, :] = ref[...]
        table[...] = jnp.zeros((256, 256), bf16)
        even, odd = halves(relative_ref[...])
        table[0:32, :128] = even
        table[128:160, :128] = odd
        slot = lax.broadcasted_iota(jnp.int32, (32, 128), 0)
        orders = jnp.where(slot == 0, order_ref[0:1, :].astype(f32), order_ref[1:2, :].astype(f32))
        even, odd = halves(jnp.where(slot < 2, orders, 0.0))
        table[32:64, 128:] = even.astype(bf16)
        table[160:192, 128:] = odd.astype(bf16)
        key_total[...] = jnp.zeros(key_total.shape, f32)
        value_total[...] = jnp.zeros(value_total.shape, f32)
        table_total[...] = jnp.zeros(table_total.shape, f32)
        sums[...] = jnp.zeros(sums.shape, f32)

    scaled = (grad_ref[...].astype(f32) * inverse_ref[...]).astype(bf16)
    even, odd = halves(scaled)
    grads = jnp.concatenate([even, odd], 0)
    even, odd = halves(scaled.astype(f32) * mixed_ref[...])
    delta = jnp.concatenate(
        [jnp.sum(even, axis=1, keepdims=True), jnp.sum(odd, axis=1, keepdims=True)], 0
    )
    even, odd = halves(content_ref[...])
    content = jnp.concatenate([even, odd], 0)
    grads_t = grads.T
    content_t = content.T
    near = pl.multiple_of(step * 256, 256)

    def visit(start, size):
        probs = probs_ref[0, 0, :, pl.ds(start, size)]
        prob_grad = nt(grads, values[pl.ds(start, size), :])
        score = probs.astype(f32) * (prob_grad - delta)
        score_low = score.astype(bf16)
        value_total[:, pl.ds(start, size)] += nn(grads_t, probs)
        key_total[:, pl.ds(start, size)] += nn(content_t, score_low)
        return score, nn(score_low, keys[pl.ds(start, size), :])

    score, query_part = visit(near, NEAR)
    query_total[...] = query_part
    parts = [score[:, 128 * t : 128 * t + 128] for t in range(5)]
    turn = turn_ref[...]
    turns = jnp.concatenate([turn, turn], 0)
    tiles = [take(part, turns) for part in parts]
    lane = lax.broadcasted_iota(jnp.int32, (64, 128), 1)
    row = lax.broadcasted_iota(jnp.int32, (64, 128), 0)
    first = lane + 2 * row < 128
    zero = jnp.zeros((64, 128), f32)
    for quarter in range(4):
        rows = slice(64 * quarter, 64 * quarter + 64)
        own = [tile[rows] for tile in tiles]
        if quarter % 2 == 0:
            near_parts = [jnp.where(first, own[t], own[t + 1]) for t in range(3)]
            far_behind[rows] = jnp.where(first, zero, own[0])
            far_ahead[rows] = jnp.where(first, own[3], zero) + parts[4][rows]
        else:
            near_parts = [jnp.where(first, own[t + 1], own[t + 2]) for t in range(3)]
            far_behind[rows] = parts[0][rows] + jnp.where(first, zero, own[1])
            far_ahead[rows] = jnp.where(first, own[4], zero)
        for t in range(3):
            bucket[rows, 256 + 128 * t : 384 + 128 * t] = near_parts[t].astype(bf16)

    @pl.loop(0, behind_ref[step])
    def _(chunk):
        score, part = visit(pl.multiple_of(near - 256 * (chunk + 1), 128), CHUNK)
        query_total[...] += part
        far_behind[...] += score[:, :128] + score[:, 128:]

    @pl.loop(0, ahead_ref[step])
    def _(chunk):
        score, part = visit(pl.multiple_of(near + NEAR + 256 * chunk, 128), CHUNK)
        query_total[...] += part
        far_ahead[...] += score[:, :128] + score[:, 128:]

    for ref, place in ((far_behind, 0), (far_ahead, 640)):
        whole = ref[...]
        coarse = whole.astype(bf16)
        bucket[:, place : place + 128] = coarse
        bucket[:, place + 128 : place + 256] = (whole - coarse.astype(f32)).astype(bf16)
    low = (nn(bucket[...], onehot_ref[...]) * 0.125).astype(bf16)
    low = jnp.concatenate([low[:BQ], low[BQ:]], 1)
    placed = nn(low, table[...])
    content_grad = pick(query_total[...]) * 0.125
    query_ref[...] = (content_grad + placed[:, :128] + placed[:, 128:]).astype(bf16)
    table_total[...] += tn(low, jnp.concatenate([position_ref[...], ordering_ref[...]], 1))
    sums[0:1, :] += jnp.sum(content_grad, axis=0, keepdims=True)
    sums[1:2, :] += jnp.sum(placed[:, :128], axis=0, keepdims=True)
    sums[2:3, :] += jnp.sum(placed[:, 128:], axis=0, keepdims=True)

    @pl.when(step == pl.num_programs(1) - 1)
    def _():
        key_low_ref[...] = (key_total[:, 256 : 256 + length] * LN2).T.astype(bf16)
        value_low_ref[...] = value_total[:, 256 : 256 + length].T.astype(bf16)
        low_lane = lax.broadcasted_iota(jnp.int32, (32, 128), 1) < 64
        relative_out[...] = jnp.where(low_lane, table_total[0:32, :128], table_total[128:160, :128])
        order_out[...] = jnp.where(low_lane[:8], table_total[32:40, 128:], table_total[160:168, 128:])
        sums_out[...] = sums[...]


def ranges(segments):
    length = segments.shape[1]
    own = segments[0]
    blocks = length // (2 * BQ)
    start = 2 * BQ * jnp.arange(blocks, dtype=jnp.int32)
    first = jnp.sum((own[None, :] < own[start][:, None]).astype(jnp.int32), axis=1)
    last = jnp.sum((own[None, :] <= own[start + 2 * BQ - 2][:, None]).astype(jnp.int32), axis=1)
    behind = jnp.maximum(start - 256 - first + CHUNK - 1, 0) // CHUNK
    ahead = jnp.maximum(last - (start - 256 + NEAR) + CHUNK - 1, 0) // CHUNK
    return behind, ahead


def documents(segments):
    length = segments.shape[1]
    lane = jnp.arange(128, dtype=jnp.int32)[None, :]
    same = segments[0][:, None] == lane
    query = same[0::2].astype(bf16)
    away = jnp.where((lane < 8) & ~same, -BIG, 0.0).astype(bf16)
    pad = jnp.broadcast_to(jnp.where(lane < 8, -BIG, 0.0).astype(bf16), (256, 128))
    return query, jnp.concatenate([pad, away, pad], 0)


def attend(behind, ahead, content, position, ordering, keys, values, relative, order, away, document):
    rows, width = content.shape
    length = keys.shape[0]
    padded = length + 512
    pairs, blocks = width // 128, rows // BQ
    tile = pl.BlockSpec((BQ, 128), lambda p, i, *_: (i, p))
    whole = pl.BlockSpec((length, 128), lambda p, i, *_: (0, p))
    return pl.pallas_call(
        forward_kernel,
        name="attend",
        out_shape=(
            jax.ShapeDtypeStruct((pairs, blocks, 2 * BQ, padded), bf16),
            jax.ShapeDtypeStruct((rows, width), bf16),
            jax.ShapeDtypeStruct((rows, width), f32),
            jax.ShapeDtypeStruct((rows, width), f32),
        ),
        grid_spec=pltpu.PrefetchScalarGridSpec(
            num_scalar_prefetch=2,
            grid=(pairs, blocks),
            in_specs=[
                tile, tile, tile, whole, whole,
                pl.BlockSpec((32, 128), lambda p, i, *_: (0, p)),
                pl.BlockSpec((2, 128), lambda p, i, *_: (0, p)),
                pl.BlockSpec((padded, 128), lambda p, i, *_: (0, 0)),
                pl.BlockSpec((BQ, 128), lambda p, i, *_: (i, 0)),
                pl.BlockSpec((5, BQ, 128), lambda p, i, *_: (0, 0, 0)),
            ],
            out_specs=[pl.BlockSpec((1, 1, 2 * BQ, padded), lambda p, i, *_: (p, i, 0, 0)), tile, tile, tile],
            scratch_shapes=[
                pltpu.VMEM((padded, 256), bf16),
                pltpu.VMEM((padded, 256), bf16),
                pltpu.VMEM((256, 256), bf16),
                pltpu.VMEM((2 * BQ, padded), f32),
                pltpu.VMEM((2 * BQ, 128), f32),
                pltpu.VMEM((2 * BQ, 256), f32),
            ],
        ),
        compiler_params=pltpu.CompilerParams(dimension_semantics=("arbitrary", "arbitrary"), vmem_limit_bytes=48 << 20),
        cost_estimate=pl.CostEstimate(flops=40 * 10**9, bytes_accessed=70 * 10**6, transcendentals=10**7),
    )(behind, ahead, content, position, ordering, keys, values, relative, order, away, document, jnp.asarray(near_index()))


def attend_back(behind, ahead, probs, grad, mixed, inverse, content, position, ordering, keys, values, relative, order):
    rows, width = content.shape
    length = keys.shape[0]
    padded = length + 512
    pairs, blocks = width // 128, rows // BQ
    tile = pl.BlockSpec((BQ, 128), lambda p, i, *_: (i, p))
    whole = pl.BlockSpec((length, 128), lambda p, i, *_: (0, p))
    small = lambda n: pl.BlockSpec((n, 128), lambda p, i, *_: (0, p))
    fixed = lambda n: pl.BlockSpec((n, 128), lambda p, i, *_: (0, 0))
    turn = (np.arange(128)[None, :] + 2 * np.arange(BQ)[:, None]) % 128
    return pl.pallas_call(
        backward_kernel,
        name="attend_back",
        out_shape=(
            jax.ShapeDtypeStruct((rows, width), bf16),
            jax.ShapeDtypeStruct((length, width), bf16),
            jax.ShapeDtypeStruct((length, width), bf16),
            jax.ShapeDtypeStruct((32, width), f32),
            jax.ShapeDtypeStruct((8, width), f32),
            jax.ShapeDtypeStruct((8, width), f32),
        ),
        grid_spec=pltpu.PrefetchScalarGridSpec(
            num_scalar_prefetch=2,
            grid=(pairs, blocks),
            in_specs=[
                pl.BlockSpec((1, 1, 2 * BQ, padded), lambda p, i, *_: (p, i, 0, 0)),
                tile, tile, tile, tile, tile, tile, whole, whole, small(32), small(2), fixed(BQ), fixed(896),
            ],
            out_specs=[tile, whole, whole, small(32), small(8), small(8)],
            scratch_shapes=[
                pltpu.VMEM((padded, 128), bf16),
                pltpu.VMEM((padded, 128), bf16),
                pltpu.VMEM((256, 256), bf16),
                pltpu.VMEM((128, padded), f32),
                pltpu.VMEM((128, padded), f32),
                pltpu.VMEM((2 * BQ, 128), f32),
                pltpu.VMEM((2 * BQ, 128), f32),
                pltpu.VMEM((2 * BQ, 128), f32),
                pltpu.VMEM((2 * BQ, 896), bf16),
                pltpu.VMEM((256, 256), f32),
                pltpu.VMEM((8, 128), f32),
            ],
        ),
        compiler_params=pltpu.CompilerParams(dimension_semantics=("arbitrary", "arbitrary"), vmem_limit_bytes=48 << 20),
        cost_estimate=pl.CostEstimate(flops=80 * 10**9, bytes_accessed=70 * 10**6, transcendentals=0),
    )(behind, ahead, probs, grad, mixed, inverse, content, position, ordering, keys, values, relative, order,
      jnp.asarray(turn, jnp.int32), jnp.asarray(bucket_onehot(), bf16))


def matmul(left, right):
    return jnp.dot(left, right, preferred_element_type=jnp.float32)


def normalize(values):
    centered = values - jnp.mean(values, axis=1, keepdims=True)
    inverse = lax.rsqrt(jnp.mean(centered * centered, axis=1, keepdims=True) + 1e-05)
    return (centered * inverse, inverse)


def norm_back(grad, normed, inverse):
    return inverse * (
        grad
        - jnp.mean(grad, axis=1, keepdims=True)
        - normed * jnp.mean(grad * normed, axis=1, keepdims=True)
    )


def gelu_slope(values):
    return 0.5 * (1.0 + lax.erf(values * math.sqrt(0.5))) + values * jnp.exp(
        -0.5 * values * values
    ) / math.sqrt(2.0 * math.pi)


def body(
    tokens,
    segment_ids,
    query_weight,
    key_weight,
    value_weight,
    output_weight,
    relative_table,
    order_table,
    content_bias,
    position_bias,
    order_bias,
    first_gain,
    first_shift,
    inner_weight,
    inner_bias,
    outer_weight,
    outer_bias,
    second_gain,
    second_shift,
    cotangent,
):
    full = (
        lax.all_gather(query_weight, "shard", axis=0, tiled=True),
        lax.all_gather(key_weight, "shard", axis=0, tiled=True),
        lax.all_gather(value_weight, "shard", axis=0, tiled=True),
        lax.all_gather(output_weight, "shard", axis=0, tiled=True),
        lax.all_gather(relative_table, "shard", axis=1, tiled=True),
        lax.all_gather(order_table, "shard", axis=1, tiled=True),
        lax.all_gather(content_bias, "shard", axis=0, tiled=True),
        lax.all_gather(position_bias, "shard", axis=0, tiled=True),
        lax.all_gather(order_bias, "shard", axis=0, tiled=True),
        lax.all_gather(first_gain, "shard", axis=0, tiled=True),
        lax.all_gather(first_shift, "shard", axis=0, tiled=True),
        lax.all_gather(inner_weight, "shard", axis=0, tiled=True),
        lax.all_gather(inner_bias, "shard", axis=0, tiled=True),
        lax.all_gather(outer_weight, "shard", axis=0, tiled=True),
        lax.all_gather(outer_bias, "shard", axis=0, tiled=True),
        lax.all_gather(second_gain, "shard", axis=0, tiled=True),
        lax.all_gather(second_shift, "shard", axis=0, tiled=True),
    )
    (
        weight_query,
        weight_key,
        weight_value,
        weight_output,
        weight_relative,
        weight_order,
        bias_content,
        bias_position,
        bias_order,
        gain_first,
        shift_first,
        weight_inner,
        bias_inner,
        weight_outer,
        bias_outer,
        gain_second,
        shift_second,
    ) = full
    count, length = segment_ids.shape
    half = length // 2
    width = tokens.shape[1]
    pairs = tokens.astype(f32).reshape(count, half, 2, width)
    query_seg = segment_ids[:, 0::2]
    joined = (query_seg == segment_ids[:, 1::2]).astype(f32)[:, :, None]
    pooled = ((pairs[:, :, 0] + joined * pairs[:, :, 1]) / (1.0 + joined)).reshape(
        count * half, width
    )
    pooled_low = pooled.astype(bf16)
    queries = matmul(pooled_low, weight_query)
    keys = matmul(tokens, weight_key).astype(bf16)
    values = matmul(tokens, weight_value).astype(bf16)
    content = ((queries + bias_content.astype(f32)) * (0.125 * LOG2E)).astype(bf16)
    position = (queries + bias_position.astype(f32)).astype(bf16)
    ordering = (queries + bias_order.astype(f32)).astype(bf16)
    behind, ahead = ranges(segment_ids)
    document, away = documents(segment_ids)
    probs, context, mixed, inverse = attend(
        behind, ahead, content, position, ordering, keys, values, weight_relative, weight_order, away, document
    )
    attended = matmul(context, weight_output)
    first_norm, first_inverse = normalize(pooled + attended)
    first = first_norm * gain_first.astype(f32) + shift_first.astype(f32)
    first_low = first.astype(bf16)
    inner = matmul(first_low, weight_inner) + bias_inner.astype(f32)
    act_low = jax.nn.gelu(inner, approximate=False).astype(bf16)
    outer = matmul(act_low, weight_outer) + bias_outer.astype(f32)
    second_norm, second_inverse = normalize(first + outer)
    layer_out = (second_norm * gain_second.astype(f32) + shift_second.astype(f32)).astype(bf16)
    grad_out = cotangent.astype(f32)
    second_gain_grad = jnp.sum(grad_out * second_norm, axis=0)
    second_shift_grad = jnp.sum(grad_out, axis=0)
    mid_grad = norm_back(grad_out * gain_second.astype(f32), second_norm, second_inverse)
    outer_low = mid_grad.astype(bf16)
    outer_weight_grad = matmul(act_low.T, outer_low)
    outer_bias_grad = jnp.sum(outer_low.astype(f32), axis=0)
    inner_low = (matmul(outer_low, weight_outer.T) * gelu_slope(inner)).astype(bf16)
    inner_weight_grad = matmul(first_low.T, inner_low)
    inner_bias_grad = jnp.sum(inner_low.astype(f32), axis=0)
    first_grad = matmul(inner_low, weight_inner.T) + mid_grad
    first_gain_grad = jnp.sum(first_grad * first_norm, axis=0)
    first_shift_grad = jnp.sum(first_grad, axis=0)
    sum_grad = norm_back(first_grad * gain_first.astype(f32), first_norm, first_inverse)
    attended_low = sum_grad.astype(bf16)
    output_weight_grad = matmul(context.T, attended_low)
    context_grad = matmul(attended_low, weight_output.T).astype(bf16)
    query_low, key_low, value_low, relative_table_grad, order_table_grad, bias_sums = attend_back(
        behind, ahead, probs, context_grad, mixed, inverse, content, position, ordering,
        keys, values, weight_relative, weight_order,
    )
    order_table_grad = order_table_grad[:2]
    content_bias_grad, position_bias_grad, order_bias_grad = bias_sums[0], bias_sums[1], bias_sums[2]
    query_weight_grad = matmul(pooled_low.T, query_low)
    key_weight_grad = matmul(tokens.T, key_low)
    value_weight_grad = matmul(tokens.T, value_low)
    pooled_grad = (sum_grad + matmul(query_low, weight_query.T)).reshape(count, half, 1, width)
    shared = joined[:, :, :, None]
    spread = jnp.concatenate(
        [pooled_grad / (1.0 + shared), shared * pooled_grad / (1.0 + shared)], axis=2
    ).reshape(count * length, width)
    tokens_grad = matmul(key_low, weight_key.T) + matmul(value_low, weight_value.T) + spread
    owned = (
        lax.psum_scatter(query_weight_grad, "shard", scatter_dimension=0, tiled=True),
        lax.psum_scatter(key_weight_grad, "shard", scatter_dimension=0, tiled=True),
        lax.psum_scatter(value_weight_grad, "shard", scatter_dimension=0, tiled=True),
        lax.psum_scatter(output_weight_grad, "shard", scatter_dimension=0, tiled=True),
        lax.psum_scatter(relative_table_grad, "shard", scatter_dimension=1, tiled=True),
        lax.psum_scatter(order_table_grad, "shard", scatter_dimension=1, tiled=True),
        lax.psum_scatter(content_bias_grad, "shard", scatter_dimension=0, tiled=True),
        lax.psum_scatter(position_bias_grad, "shard", scatter_dimension=0, tiled=True),
        lax.psum_scatter(order_bias_grad, "shard", scatter_dimension=0, tiled=True),
        lax.psum_scatter(first_gain_grad, "shard", scatter_dimension=0, tiled=True),
        lax.psum_scatter(first_shift_grad, "shard", scatter_dimension=0, tiled=True),
        lax.psum_scatter(inner_weight_grad, "shard", scatter_dimension=0, tiled=True),
        lax.psum_scatter(inner_bias_grad, "shard", scatter_dimension=0, tiled=True),
        lax.psum_scatter(outer_weight_grad, "shard", scatter_dimension=0, tiled=True),
        lax.psum_scatter(outer_bias_grad, "shard", scatter_dimension=0, tiled=True),
        lax.psum_scatter(second_gain_grad, "shard", scatter_dimension=0, tiled=True),
        lax.psum_scatter(second_shift_grad, "shard", scatter_dimension=0, tiled=True),
    )
    summed = lax.psum(
        (
            owned[0],
            owned[1],
            owned[2],
            owned[3],
            owned[4],
            owned[5],
            owned[6],
            owned[7],
            owned[8],
            owned[9],
            owned[10],
            owned[11],
            owned[12],
            owned[13],
            owned[14],
            owned[15],
            owned[16],
        ),
        "rep",
    )
    return (layer_out, tokens_grad) + tuple(summed)


def solution(mesh):
    placed = (
        P(("rep", "shard"), None),
        P(("rep", "shard"), None),
        P("shard", None),
        P("shard", None),
        P("shard", None),
        P("shard", None),
        P(None, "shard"),
        P(None, "shard"),
        P("shard"),
        P("shard"),
        P("shard"),
        P("shard"),
        P("shard"),
        P("shard", None),
        P("shard"),
        P("shard", None),
        P("shard"),
        P("shard"),
        P("shard"),
        P(("rep", "shard"), None),
    )
    return jax.shard_map(
        body,
        mesh=mesh,
        in_specs=placed,
        out_specs=(
            P(("rep", "shard"), None),
            P(("rep", "shard"), None),
            P("shard", None),
            P("shard", None),
            P("shard", None),
            P("shard", None),
            P(None, "shard"),
            P(None, "shard"),
            P("shard"),
            P("shard"),
            P("shard"),
            P("shard"),
            P("shard"),
            P("shard", None),
            P("shard"),
            P("shard", None),
            P("shard"),
            P("shard"),
            P("shard"),
        ),
        check_vma=False,
    )
```

time: 3200 us -> 1200 us (0.38)
  matrix products: 1540 us -> 148 us
  other arithmetic: 802 us -> 17.7 us
  Pallas kernels: 0 us -> 195 us
  local copies, waits for them, and re-layouts: 144 us -> 83.5 us
  waiting for transfers between devices: 511 us -> 559 us
    dot_general x198 -> x18, matrix products: 1540 us -> 148 us  [matmul(): return jnp.dot(left, right, preferred_element_type=jnp.float32)]
    reduce_sum x25 -> x1, other arithmetic: 784 us -> 0.22 us  [ranges(): jnp.sum((own[None, :] <= own[start + 2 * BQ - 2][:, None]).astype(jnp.int...]
    pallas_call x0 -> x2, Pallas kernels: none -> 195 us  [the longest x1 99.1 us: attend(): pl.pallas_call(forward_kernel, name='attend', out_shape=(jax.ShapeDtypeSt...]
    unnamed x19, waiting for transfers between devices: 90.3 us -> 139 us
  transfers between devices with their start and end apart: 15 -> 15, of which waited for: 8 -> 8; matrix products, arithmetic and copies ran while one was open for 27% -> 16% of each run, Pallas kernels for 0% -> 8%
where the time goes in v1:
time: 1200 us; the launch traced here: 1190 us
  waiting for transfers between devices  559 us (47%)
  Pallas kernels  195 us (16%)
  blocking collectives  170 us (14%)
  matrix products  148 us (12%)
  local copies, waits for them, and re-layouts  83.5 us (7%)
  other arithmetic  17.7 us (1%)
  between operations  17.6 us (1%)
    dot_general x18, matrix products, matmul(): return jnp.dot(left, right, preferred_element_type=jnp.float32)  148 us
    unnamed x19, waiting for transfers between devices  139 us
    unnamed x2, blocking collectives  124 us
    reduce_scatter x1, waiting for transfers between devices, body(): lax.psum_scatter(inner_weight_grad, 'shard', scatter_dimension=0, tiled=T...  116 us
    reduce_scatter x1, waiting for transfers between devices, body(): lax.psum_scatter(outer_weight_grad, 'shard', scatter_dimension=0, tiled=T...  115 us
    pallas_call x1, Pallas kernels, attend(): pl.pallas_call(forward_kernel, name='attend', out_shape=(jax.ShapeDtypeSt...  99.1 us
    pallas_call x1, Pallas kernels, attend_back(): pl.pallas_call(backward_kernel, name='attend_back', out_shape=(jax.ShapeD...  95.9 us
    reduce_scatter x1, waiting for transfers between devices, body(): lax.psum_scatter(query_weight_grad, 'shard', scatter_dimension=0, tiled=T...  66.1 us
  transfers between devices with their start and end apart: 15, of which 8 were waited for; matrix products, arithmetic and copies ran while one was open for 16% of the time, Pallas kernels for 8%

profile of v1, /device:TPU:0, one launch (start us, length us, event | category | flops | bytes accessed | tf_op | source)
XLA Modules:
  0.0 1190.6 jit_solution(3430739781738237835)
XLA Ops:
  11.2 0.9 slice.28
  12.1 0.9 slice.29
  13.1 1.3 fusion.45
  15.8 0.8 dynamic-update-slice
  20.0 0.8 dynamic-update-slice.6
  20.8 0.8 dynamic-update-slice.7
  22.5 0.8 dynamic-update-slice.5
  23.3 63.2 %all-reduce.21 = (bf16[768]{0:T(1024)(128)(2,1)S(1)}, bf16[768]{0:T(1024)(128)(2,1)S(1)}, bf16[768]{0:T(1024)(128)(2,1)S(1)}, bf16[768]{0:T(1024)(128)(2,1)S(1)}...) all-reduce(bf16[768]{0:T(1024)(128)(2,1)S(1)} %dynamic-update-slice, ...), channel_id=1, replica_groups=mesh['rep'=2,'shard'=16] {'shard'}, use_global_device_ids=true, to_apply=%add | all-reduce | flops 9216 | bytes 36864
  86.6 7.8 reshape.193
  94.4 12.7 %fusion.44 = (f32[1,1024,1,768]{3,2,1,0:T(1,128)}, f32[1,1024,1,768]{3,2,1,0:T(1,128)}) fusion(f32[1,1024,2,768]{3,2,1,0:T(2,128)} %reshape.193), kind=kLoop, calls=%fused_computation.114 | loop fusion | bytes 12582912 | tf_op jit(solution)/shard_map/slice | solution.py:480
  110.0 17.6 %all-gather = bf16[16,48,32]{1,2,0:T(8,128)(2,1)S(1)} all-gather(bf16[1,48,32]{1,2,0:T(8,128)(2,1)S(1)} %bitcast.91), channel_id=1, replica_groups=mesh['rep'=2,'shard'=16] {'shard'}, dimensions={0}, use_global_device_ids=true | all-gather | bytes 52224 | tf_op jit(solution)/shard_map/all_gather | solution.py:441
  127.8 19.1 %all-gather.1 = bf16[16,48,2]{1,2,0:T(2,128)(2,1)S(1)} all-gather(bf16[1,48,2]{1,2,0:T(2,128)(2,1)S(1)} %bitcast.92), channel_id=1, replica_groups=mesh['rep'=2,'shard'=16] {'shard'}, dimensions={0}, use_global_device_ids=true | all-gather | bytes 3264 | tf_op jit(solution)/shard_map/all_gather | solution.py:442
  148.7 5.0 fusion.25
  153.6 6.5 convolution_convert_fusion.value_ref
  160.1 6.7 convolution_convert_fusion.1.key_ref
  166.8 5.0 add_convert_fusion.1
  171.8 99.1 %attend.1 = (bf16[6,8,256,2560]{3,2,1,0:T(8,128)(2,1)}, bf16[1024,768]{1,0:T(8,128)(2,1)S(1)}, f32[1024,768]{1,0:T(8,128)}, f32[1024,768]{1,0:T(8,128)}) custom-call(s32[8]{0:T(128)S(1)} %get-tuple-element.185.behind_ref, s32[8]{0:T(128)S(1)} %get-tuple-element.184.ahead_ref, bf16[1024,768]{1,0:T(8,128)(2,1)S(1)} %get-tuple-element.172.content_ref, ...), custom_call_target="tpu_custom_call" | custom-call | flops 40000000000 | bytes 70000000 | tf_op jit(solution)/shard_map/attend/pallas_call | solution.py:306
  271.0 1.2 copy-done.5
  272.1 1.2 copy-done.6
  273.3 4.4 fusion.46
  277.8 1.6 copy-done.10
  279.9 37.2 %fusion.2 = (bf16[1024,3072]{1,0:T(8,128)(2,1)}, f32[1024,3072]{1,0:T(8,128)}) fusion(f32[3072]{0:T(1024)S(1)} %convert_element_type.118, bf16[768,3072]{1,0:T(8,128)(2,1)} %all-gather.17.cloned.1.call-done, f32[1024,768]{1,0:T(8,128)} %copy-done.10, f32[768]{0:T(1024)S(1)} %convert_element_type.116, f32[768]{0:T(1024)S(1)} %convert_element_type.115, ...), kind=kOutput, calls=%fused_computation.6 | convolution fusion | flops 5043388416 | bytes 26765312 | tf_op jit(solution)/shard_map/dot_general | solution.py:391
  317.1 9.7 fusion.47
  328.3 2.3 fusion.22
  330.6 2.9 convert_reduce_fusion.2
  333.6 13.7 %convert_reduce_fusion = (f32[3072]{0:T(1024)}, bf16[1024,3072]{1,0:T(8,128)(2,1)S(1)}) fusion(f32[1024,3072]{1,0:T(8,128)} %get-tuple-element.178, f32[3072]{0:T(1024)S(1)} %convert_element_type.118, bf16[3072,768]{1,0:T(8,128)(2,1)S(1)} %copy-done.34, f32[1024,768]{1,0:T(8,128)S(1)} %get-tuple-element.164), kind=kOutput, calls=%fused_computation.13 | convolution fusion | flops 4873516032 | bytes 26763264 | tf_op jit(solution)/shard_map/dot_general | solution.py:391
  347.3 6.0 multiply_reduce_fusion
  353.4 1.0 subtract_multiply_fusion
  354.6 1.4 convolution_convert_fusion.2.grad_ref
  356.3 1.0 copy-done.7
  357.3 95.9 %attend_back.1 = (bf16[1024,768]{1,0:T(8,128)(2,1)S(1)}, bf16[2048,768]{1,0:T(8,128)(2,1)}, bf16[2048,768]{1,0:T(8,128)(2,1)}, f32[32,768]{1,0:T(8,128)S(1)}, f3...) custom-call(s32[8]{0:T(128)S(1)} %get-tuple-element.185.behind_ref, s32[8]{0:T(128)S(1)} %get-tuple-element.184.ahead_ref, ...), custom_call_target="tpu_custom_call" | custom-call | flops 80000000000 | bytes 70000000 | tf_op jit(solution)/shard_map/attend_back/pallas_call | solution.py:351
  453.3 5.9 convolution_bitcast_fusion.1
  459.2 3.2 copy.67
  462.5 6.9 convolution_bitcast_fusion
  469.4 3.2 copy.69
  472.7 4.7 fusion.27
  477.5 4.8 fusion.30
  482.4 10.6 fusion.36
  493.7 11.0 fusion.39
  504.8 1.0 copy.73
  507.2 0.9 copy.71
  508.2 3.5 divide_bitcast_fusion.1
  511.7 3.1 pad_maximum_fusion
  514.9 44.1 %reduce-scatter.25.cloned.1.call-done = f32[48,768]{1,0:T(8,128)} async-done(((f32[768,768]{1,0:T(8,128)}), f32[48,768]{1,0:T(8,128)}) %reduce-scatter.25.cloned.1.call-update) | async-done | bytes 147472
  559.0 1.8 copy.68
  560.8 64.4 %reduce-scatter.27.cloned.1.call-done = f32[48,768]{1,0:T(8,128)} async-done(((f32[768,768]{1,0:T(8,128)}), f32[48,768]{1,0:T(8,128)}) %reduce-scatter.27.cloned.1.call-update) | async-done | bytes 147472
  625.3 1.8 copy.70
  627.1 64.0 %reduce-scatter.19.cloned.1.call-done = f32[48,768]{1,0:T(8,128)} async-done(((f32[768,768]{1,0:T(8,128)}), f32[48,768]{1,0:T(8,128)}) %reduce-scatter.19.cloned.1.call-update) | async-done | bytes 147472 | tf_op jit(solution)/shard_map/reduce_scatter | solution.py:540
  691.1 66.1 %reduce-scatter.17.cloned.1.call-done = f32[48,768]{1,0:T(8,128)} async-done(((f32[768,768]{1,0:T(8,128)}), f32[48,768]{1,0:T(8,128)}) %reduce-scatter.17.cloned.1.call-update) | async-done | bytes 147472 | tf_op jit(solution)/shard_map/reduce_scatter | solution.py:537
  757.2 114.5 %reduce-scatter.23.cloned.1.call-done = f32[192,768]{1,0:T(8,128)} async-done(((f32[3072,768]{1,0:T(8,128)}), f32[192,768]{1,0:T(8,128)}) %reduce-scatter.23.cloned.1.call-update) | async-done | bytes 589840 | tf_op jit(solution)/shard_map/reduce_scatter | solution.py:550
  871.7 115.6 %reduce-scatter.21.cloned.1.call-done = f32[48,3072]{1,0:T(8,128)} async-done(((f32[768,3072]{1,0:T(8,128)}), f32[48,3072]{1,0:T(8,128)}) %reduce-scatter.21.cloned.1.call-update) | async-done | bytes 589840 | tf_op jit(solution)/shard_map/reduce_scatter | solution.py:548
  987.5 60.9 %all-reduce.18 = (f32[768]{0:T(1024)S(1)}, f32[768]{0:T(1024)S(1)}, f32[768]{0:T(1024)S(1)}, f32[768]{0:T(1024)S(1)}, f32[768]{0:T(1024)S(1)}, /*index=5*/f32[30...) all-reduce(f32[768]{0:T(1024)S(1)} %get-tuple-element.125, ...), channel_id=8, replica_groups=mesh['rep'=2,'shard'=16] {'shard'}, use_global_device_ids=true, to_apply=%region_22.23.clone | all-reduce | flops 9216 | bytes 73728
  1048.9 10.3 copy.64
  1059.2 8.6 reshape.191
  1067.9 4.8 fusion.48
  1072.8 4.5 add_add_fusion
  1078.2 26.4 %reduce-scatter.29.cloned.1.call-done = f32[48,32]{1,0:T(8,128)} async-done(((f32[768,32]{1,0:T(8,128)}), f32[48,32]{1,0:T(8,128)}) %reduce-scatter.29.cloned.1.call-update) | async-done | bytes 6160
  1105.4 8.8 all-reduce.19
  1114.2 59.9 %all-reduce.24.cloned.1.call-done = (f32[48,768]{1,0:T(8,128)}, f32[48,768]{0,1:T(8,128)}, f32[48,768]{0,1:T(8,128)}, f32[48,768]{1,0:T(8,128)}, f32[48,3072]{1,0:T(8,128)}, /*index=5*/f32[192,768]{1,0:T(8,128)}) async-done(((f32[48,768]{1,0:T(8,128)}, f32[48,768]{0,1:T(8,128)}, f32[48,768]{0,1:T(8,128)}, f32[48,768]{1,0:T(8,128)}, f32[48,3072]{1,0:T(8,128)}, /*index=5*/f32[192,768]{1,0:T(8,128)}), ...) | async-done | bytes 1769488 | tf_op jit(solution)/shard_map/psum | solution.py:555
  1174.1 1.9 copy.65
  1175.9 1.8 copy.66
  1177.7 1.6 copy.102
  1179.3 1.6 copy.103
  1180.9 1.9 copy.104
  (183 shorter events, 19.6 us)
Async XLA Ops:
  7.2 146.4 %all-gather.13.cloned.1.call-start = ((), (), s32[]{:S(2)}) async-start(), calls=%async_computation.10 | async-start | bytes 1253376 | tf_op jit(solution)/shard_map/all_gather | solution.py:439
  7.9 152.2 %all-gather.11.cloned.1.call-start = ((), (), s32[]{:S(2)}) async-start(), calls=%async_computation.9 | async-start | bytes 1253376 | tf_op jit(solution)/shard_map/all_gather | solution.py:438
  8.7 158.2 %all-gather.9.cloned.1.call-start = ((), (), s32[]{:S(2)}) async-start(), calls=%async_computation.8 | async-start | bytes 1253376 | tf_op jit(solution)/shard_map/all_gather | solution.py:437
  9.4 263.9 %all-gather.15.cloned.1.call-start = ((), (), s32[]{:S(2)}) async-start(), calls=%async_computation.11 | async-start | bytes 1253376 | tf_op jit(solution)/shard_map/all_gather | solution.py:440
  10.0 270.0 %all-gather.17.cloned.1.call-start = ((), (), s32[]{:S(2)}) async-start(), calls=%async_computation.12 | async-start | bytes 5013504 | tf_op jit(solution)/shard_map/all_gather | solution.py:448
  10.6 306.6 %all-gather.19.cloned.1.call-start = ((), (), s32[]{:S(2)}) async-start(), calls=%async_computation.13 | async-start | bytes 5013504 | tf_op jit(solution)/shard_map/all_gather | solution.py:450
  11.1 547.8 %reduce-scatter.25.cloned.1.call-start = ((), (), s32[]{:S(2)}) async-start(), calls=%async_computation.18 | async-start | bytes 2506752
  86.5 62.1 %copy-start.23 = (f32[1,1024]{1,0:T(1,128)}, f32[1,1024]{1,0:T(1,128)S(1)}, u32[]{:S(2)}) copy-start(f32[1,1024]{1,0:T(1,128)S(1)} %compare_convert_fusion) | copy-start | bytes 12292
  86.6 62.1 %copy-start.27 = (f32[1024]{0:T(1024)}, f32[1024]{0:T(1024)S(1)}, u32[]{:S(2)}) copy-start(f32[1024]{0:T(1024)S(1)} %broadcast_add_fusion) | copy-start | bytes 12292
  94.4 12.7 %copy-start.8 = (s32[1,2048]{1,0:T(1,128)S(1)}, s32[1,2048]{1,0:T(1,128)}, u32[]{:S(2)}) copy-start(s32[1,2048]{1,0:T(1,128)} %param.24) | copy-start | bytes 24580
  94.4 15.6 %copy-start.32 = (bf16[32,48]{1,0:T(8,128)(2,1)S(1)}, bf16[32,48]{1,0:T(8,128)(2,1)}, u32[]{:S(2)}) copy-start(bf16[32,48]{1,0:T(8,128)(2,1)} %param.29) | copy-start | bytes 9220
  94.4 33.4 %copy-start.33 = (bf16[2,48]{1,0:T(2,128)(2,1)S(1)}, bf16[2,48]{1,0:T(2,128)(2,1)}, u32[]{:S(2)}) copy-start(bf16[2,48]{1,0:T(2,128)(2,1)} %param.30) | copy-start | bytes 580
  147.1 170.1 %copy-start.20 = (f32[768]{0:T(1024)}, f32[768]{0:T(1024)S(1)}, u32[]{:S(2)}) copy-start(f32[768]{0:T(1024)S(1)} %convert_element_type.116) | copy-start | bytes 9220
  166.8 5.0 copy-start
  271.0 1.2 copy-start.5
  272.1 1.2 copy-start.6
  273.3 4.4 copy-start.3
  277.7 1.6 copy-start.10
  326.9 1.4 copy-start.14
  326.9 1.4 copy-start.22
  327.4 3.2 copy-start.25
  330.6 2.9 copy-start.34
  330.6 16.6 %slice-start = ((s8[4718592]{0:T(1024)(128)(4,1)}), s8[4194304]{0:T(1024)(128)(4,1)S(1)}, s32[]{:S(2)}) async-start(s8[4718592]{0:T(1024)(128)(4,1)} %bitcast.93), calls=%async_computation.23 | async-start | bytes 8388608
  333.5 13.7 %copy-start.15 = (f32[1024,768]{1,0:T(8,128)}, f32[1024,768]{1,0:T(8,128)S(1)}, u32[]{:S(2)}) copy-start(f32[1024,768]{1,0:T(8,128)S(1)} %get-tuple-element.164) | copy-start | bytes 9437188
  333.5 13.7 %copy-start.11 = (f32[1024,768]{1,0:T(8,128)S(1)}, f32[1024,768]{1,0:T(8,128)}, u32[]{:S(2)}) copy-start(f32[1024,768]{1,0:T(8,128)} %copy-done.10) | copy-start | bytes 9437188
  333.5 13.7 %slice-start.1 = ((s8[4718592]{0:T(1024)(128)(4,1)}), s8[524288]{0:T(1024)(128)(4,1)S(1)}, s32[]{:S(2)}) async-start(s8[4718592]{0:T(1024)(128)(4,1)} %bitcast.93), calls=%async_computation.24 | async-start | bytes 1048576
  347.3 6.1 copy-start.13
  353.4 1.3 copy-start.37
  354.6 1.6 copy-start.17
  354.6 1.6 copy-start.1
  354.6 1.6 copy-start.2
  354.6 2.7 copy-start.7
  357.3 95.9 %copy-start.16 = (bf16[2048,768]{1,0:T(8,128)(2,1)S(1)}, bf16[2048,768]{1,0:T(8,128)(2,1)}, u32[]{:S(2)}) copy-start(bf16[2048,768]{1,0:T(8,128)(2,1)} %param.23) | copy-start | bytes 9437188
  462.4 162.8 %reduce-scatter.27.cloned.1.call-start = ((), (), s32[]{:S(2)}) async-start(), calls=%async_computation.19 | async-start | bytes 2506752
  469.4 3.2 copy-start.4
  472.6 218.5 %reduce-scatter.19.cloned.1.call-start = ((), (), s32[]{:S(2)}) async-start(), calls=%async_computation.15 | async-start | bytes 2506752 | tf_op jit(solution)/shard_map/reduce_scatter | solution.py:540
  477.4 279.8 %reduce-scatter.17.cloned.1.call-start = ((), (), s32[]{:S(2)}) async-start(), calls=%async_computation.14 | async-start | bytes 2506752 | tf_op jit(solution)/shard_map/reduce_scatter | solution.py:537
  482.3 389.4 %reduce-scatter.23.cloned.1.call-start = ((), (), s32[]{:S(2)}) async-start(), calls=%async_computation.17 | async-start | bytes 10027008 | tf_op jit(solution)/shard_map/reduce_scatter | solution.py:550
  493.0 0.7 copy-start.21
  493.0 494.3 %reduce-scatter.21.cloned.1.call-start = ((), (), s32[]{:S(2)}) async-start(), calls=%async_computation.16 | async-start | bytes 10027008 | tf_op jit(solution)/shard_map/reduce_scatter | solution.py:548
  504.7 3.4 copy-start.24
  504.7 3.4 copy-start.28
  504.7 3.5 copy-start.36
  504.8 572.6 %reduce-scatter.31.cloned.1.call-start = ((), (), s32[]{:S(2)}) async-start(), calls=%async_computation.21 | async-start | bytes 417792
  505.8 598.7 %reduce-scatter.29.cloned.1.call-start = ((), (), s32[]{:S(2)}) async-start(), calls=%async_computation.20 | async-start | bytes 417792
  508.1 666.0 %all-reduce.24.cloned.1.call-start = ((), (), s32[]{:S(2)}) async-start(), calls=%async_computation.22 | async-start | bytes 4521984 | tf_op jit(solution)/shard_map/psum | solution.py:555
  514.8 472.6 %copy-start.26 = (f32[768]{0:T(1024)S(1)}, f32[768]{0:T(1024)}, u32[]{:S(2)}) copy-start(f32[768]{0:T(1024)} %get-tuple-element.163) | copy-start | bytes 9220
  514.8 472.6 %copy-start.29 = (f32[768]{0:T(1024)S(1)}, f32[768]{0:T(1024)}, u32[]{:S(2)}) copy-start(f32[768]{0:T(1024)} %get-tuple-element.117) | copy-start | bytes 9220
  514.8 472.6 %copy-start.30 = (f32[768]{0:T(1024)S(1)}, f32[768]{0:T(1024)}, u32[]{:S(2)}) copy-start(f32[768]{0:T(1024)} %get-tuple-element.122) | copy-start | bytes 9220
  514.9 472.6 %copy-start.31 = (f32[3072]{0:T(1024)S(1)}, f32[3072]{0:T(1024)}, u32[]{:S(2)}) copy-start(f32[3072]{0:T(1024)} %get-tuple-element.182) | copy-start | bytes 36868
  1059.2 8.7 copy-start.35
  1067.9 4.8 copy-start.9
  1067.9 4.8 copy-start.12
  1067.9 4.9 copy-start.18
  1174.1 8.7 copy-start.19
Sparse Core Ops, SparseCore 0:
  10.3 41.0 all-gather.12
  53.7 37.5 all-gather.10
  93.6 37.5 all-gather.8
  133.3 37.4 all-gather.14
  172.9 52.2 all-gather.16
  227.3 51.9 all-gather.18
  462.6 96.3 reduce-scatter.24
  563.2 61.9 reduce-scatter.26
  629.0 62.0 reduce-scatter.18
  695.2 61.9 reduce-scatter.16
  761.3 110.3 reduce-scatter.22
  876.2 111.0 reduce-scatter.20
  990.8 55.3 reduce-scatter.30
  1049.9 54.5 reduce-scatter.28
  1107.6 66.3 all-reduce.23

commit v2 on v1

v2 whole, which is shorter than its diff:
```python
import functools
import math

import jax
import jax.numpy as jnp
import numpy as np
from jax import lax
from jax.experimental import pallas as pl
from jax.experimental.pallas import tpu as pltpu
from jax.sharding import PartitionSpec as P

LIMITS = (1, 2, 3, 4, 5, 6, 7, 8, 12, 16, 24, 32, 48, 64, 128)
BQ = 128
NEAR = 640
CHUNK = 256
LOG2E = math.log2(math.e)
LN2 = math.log(2.0)
BIG = 1e30
f32 = jnp.float32
bf16 = jnp.bfloat16


def bucket_of(offset):
    distance = np.abs(offset)
    passed = sum((distance >= limit).astype(np.int32) for limit in LIMITS)
    return np.where(offset < 0, 15 + passed + (distance >= 256), passed).astype(np.int32)


def near_index():
    row = np.arange(BQ)[None, :, None]
    tile = np.arange(-2, 3)[:, None, None]
    lane = np.arange(128)[None, None, :]
    return bucket_of(128 * tile + lane - 2 * row)


def bucket_onehot():
    out = np.zeros((4 * 128, 128), np.float32)
    offsets = np.concatenate([np.arange(-256, 128), np.full(64, -300), np.full(64, 300)])
    out[np.arange(512), bucket_of(offsets)] = 1
    out[:, 32] = offsets >= 0
    out[:, 33] = offsets < 0
    return out


def nt(left, right):
    return lax.dot_general(left, right, (((1,), (1,)), ((), ())), preferred_element_type=f32)


def nn(left, right):
    return lax.dot_general(left, right, (((1,), (0,)), ((), ())), preferred_element_type=f32)


def tn(left, right):
    return lax.dot_general(left, right, (((0,), (0,)), ((), ())), preferred_element_type=f32)


def halves(array):
    low = lax.broadcasted_iota(jnp.int32, array.shape, 1) < 64
    zero = jnp.zeros_like(array)
    return jnp.where(low, array, zero), jnp.where(low, zero, array)


def pick(array):
    half = array.shape[0] // 2
    low = lax.broadcasted_iota(jnp.int32, (half, 128), 1) < 64
    return jnp.where(low, array[:half], array[half:])


def take(table, index):
    return jnp.take_along_axis(table, index, axis=1, mode="promise_in_bounds")


def lanes_of(p):
    return slice(128 * p, 128 * p + 128)


def forward_kernel(
    group, behind_ref, ahead_ref, content_ref, position_ref, ordering_ref, key_ref, value_ref,
    relative_ref, order_ref, away_ref, document_ref, index_ref,
    probs_ref, context_ref, mixed_ref, inverse_ref,
    keys, values, table, bias, scores, peak, total,
):
    step = pl.program_id(1)
    length = key_ref.shape[0]

    @pl.when((step == 0) & (pl.program_id(0) == 0))
    def _():
        for p in range(group):
            for scratch in (keys, values):
                scratch[p, :256, :128] = jnp.zeros((256, 128), bf16)
                scratch[p, 256 + length :, :128] = jnp.zeros((256, 128), bf16)
            keys[p, :, 128:] = away_ref[...]
            values[p, :, 128:] = jnp.ones((length + 512, 128), bf16)

    @pl.when(step == 0)
    def _():
        after = lax.broadcasted_iota(jnp.int32, (32, 128), 0) < 16
        table[...] = jnp.zeros(table.shape, bf16)
        for p in range(group):
            lanes = lanes_of(p)
            keys[p, 256 : 256 + length, :128] = key_ref[:, lanes]
            values[p, 256 : 256 + length, :128] = value_ref[:, lanes]
            orders = jnp.where(after, order_ref[0:1, lanes].astype(f32), order_ref[1:2, lanes].astype(f32)).astype(bf16)
            for half, (relative, order) in enumerate(zip(halves(relative_ref[:, lanes]), halves(orders))):
                both = jnp.concatenate([relative, order], 1)
                table[p, 128 * half : 128 * half + 32, :] = both

    document = document_ref[...]
    near = pl.multiple_of(step * 256, 256)
    queries = []
    for p in range(group):
        even, odd = halves(content_ref[:, lanes_of(p)])
        queries.append(jnp.concatenate(
            [jnp.concatenate([even, document], 1), jnp.concatenate([odd, document], 1)], 0
        ))
    for p in range(group):
        lanes = lanes_of(p)
        places = nt(jnp.concatenate([position_ref[:, lanes], ordering_ref[:, lanes]], 1), table[p]) * (0.125 * LOG2E)
        place = (places[:, :128], places[:, 128:])
        near_scores = nt(queries[p], keys[p, pl.ds(near, NEAR), :])
        for half in range(2):
            rows = slice(BQ * half, BQ * half + BQ)
            for side, bucket in ((0, 31), (1, 15)):
                bias[p, rows, 128 * side : 128 * side + 128] = jnp.broadcast_to(place[half][:, bucket : bucket + 1], (BQ, 128))
            for quarter in range(2):
                own = slice(64 * quarter, 64 * quarter + 64)
                rows = slice(BQ * half + 64 * quarter, BQ * half + 64 * quarter + 64)
                best = None
                for tile in range(NEAR // 128):
                    if tile == 4 - 4 * quarter:
                        extra = bias[p, rows, 128 - 128 * quarter : 256 - 128 * quarter]
                    else:
                        extra = take(place[half][own], index_ref[tile, own])
                    part = near_scores[rows, 128 * tile : 128 * tile + 128] + extra
                    scores[p, rows, pl.ds(near + 128 * tile, 128)] = part
                    best = part if best is None else jnp.maximum(best, part)
                peak[p, rows, :] = best
    behind = behind_ref[step]
    far = behind + ahead_ref[step]

    def start_of(chunk):
        return pl.multiple_of(jnp.where(chunk < behind, near - 256 * (chunk + 1), near + NEAR + 256 * (chunk - behind)), 128)

    @pl.loop(0, far)
    def _(chunk):
        start = start_of(chunk)
        place = pl.multiple_of(jnp.where(chunk < behind, 0, 128), 128)
        for p in range(group):
            part = nt(queries[p], keys[p, pl.ds(start, CHUNK), :])
            extra = bias[p, :, pl.ds(place, 128)]
            left, right = part[:, :128] + extra, part[:, 128:] + extra
            scores[p, :, pl.ds(start, 128)] = left
            scores[p, :, pl.ds(start + 128, 128)] = right
            peak[p] = jnp.maximum(peak[p], jnp.maximum(left, right))

    tops = [jnp.max(peak[p], axis=1, keepdims=True) for p in range(group)]
    for p in range(group):
        peak[p] = jnp.broadcast_to(tops[p], (2 * BQ, 128))
        probs = jnp.exp2(scores[p, :, pl.ds(near, NEAR)] - tops[p]).astype(bf16)
        probs_ref[p, 0, :, pl.ds(near, NEAR)] = probs
        total[p] = nn(probs, values[p, pl.ds(near, NEAR), :])

    @pl.loop(0, far)
    def _(chunk):
        start = start_of(chunk)
        for p in range(group):
            top = peak[p]
            left = jnp.exp2(scores[p, :, pl.ds(start, 128)] - top).astype(bf16)
            right = jnp.exp2(scores[p, :, pl.ds(start + 128, 128)] - top).astype(bf16)
            probs = jnp.concatenate([left, right], 1)
            probs_ref[p, 0, :, pl.ds(start, CHUNK)] = probs
            total[p] += nn(probs, values[p, pl.ds(start, CHUNK), :])

    for p in range(group):
        lanes = lanes_of(p)
        inverse = 1.0 / total[p, :, 128:]
        mixed = pick(total[p, :, :128] * inverse)
        inverse_ref[:, lanes] = pick(inverse)
        mixed_ref[:, lanes] = mixed
        context_ref[:, lanes] = mixed.astype(bf16)


def backward_kernel(
    group, behind_ref, ahead_ref, probs_ref, grad_ref, mixed_ref, inverse_ref, content_ref, position_ref, ordering_ref,
    key_ref, value_ref, relative_ref, order_ref, turn_ref, onehot_ref,
    query_ref, key_low_ref, value_low_ref, relative_out, order_out, sums_out,
    keys, values, table, key_total, value_total, query_total, far_total, bucket, table_total, sums,
):
    step = pl.program_id(1)
    length = key_ref.shape[0]

    @pl.when(step == 0)
    def _():
        slot = lax.broadcasted_iota(jnp.int32, (32, 128), 0)
        table[...] = jnp.zeros(table.shape, bf16)
        for p in range(group):
            lanes = lanes_of(p)
            for scratch, ref in ((keys, key_ref), (values, value_ref)):
                scratch[p, :256, :] = jnp.zeros((256, 128), bf16)
                scratch[p, 256 + length :, :] = jnp.zeros((256, 128), bf16)
                scratch[p, 256 : 256 + length, :] = ref[:, lanes]
            even, odd = halves(relative_ref[:, lanes])
            table[p, 0:32, :128] = even
            table[p, 128:160, :128] = odd
            orders = jnp.where(slot == 0, order_ref[0:1, lanes].astype(f32), order_ref[1:2, lanes].astype(f32))
            even, odd = halves(jnp.where(slot < 2, orders, 0.0))
            table[p, 32:64, 128:] = even.astype(bf16)
            table[p, 160:192, 128:] = odd.astype(bf16)
        key_total[...] = jnp.zeros(key_total.shape, f32)
        value_total[...] = jnp.zeros(value_total.shape, f32)
        table_total[...] = jnp.zeros(table_total.shape, f32)
        sums[...] = jnp.zeros(sums.shape, f32)

    near = pl.multiple_of(step * 256, 256)
    grads, grads_t, content_t, deltas = [], [], [], []
    for p in range(group):
        lanes = lanes_of(p)
        scaled = (grad_ref[:, lanes].astype(f32) * inverse_ref[:, lanes]).astype(bf16)
        both = jnp.concatenate(halves(scaled), 0)
        even, odd = halves(scaled.astype(f32) * mixed_ref[:, lanes])
        deltas.append(jnp.concatenate(
            [jnp.sum(even, axis=1, keepdims=True), jnp.sum(odd, axis=1, keepdims=True)], 0
        ))
        grads.append(both)
        grads_t.append(both.T)
        content_t.append(jnp.concatenate(halves(content_ref[:, lanes]), 0).T)

    def visit(p, start, size):
        probs = probs_ref[p, 0, :, pl.ds(start, size)]
        prob_grad = nt(grads[p], values[p, pl.ds(start, size), :])
        score = probs.astype(f32) * (prob_grad - deltas[p])
        score_low = score.astype(bf16)
        value_total[p, :, pl.ds(start, size)] += nn(grads_t[p], probs)
        key_total[p, :, pl.ds(start, size)] += nn(content_t[p], score_low)
        return score, nn(score_low, keys[p, pl.ds(start, size), :])

    turn = turn_ref[...]
    turns = jnp.concatenate([turn, turn], 0)
    lane = lax.broadcasted_iota(jnp.int32, (64, 128), 1)
    row = lax.broadcasted_iota(jnp.int32, (64, 128), 0)
    first = lane + 2 * row < 128
    zero = jnp.zeros((64, 128), f32)
    for p in range(group):
        score, query_total[p] = visit(p, near, NEAR)
        parts = [score[:, 128 * t : 128 * t + 128] for t in range(5)]
        tiles = [take(part, turns) for part in parts]
        for quarter in range(4):
            rows = slice(64 * quarter, 64 * quarter + 64)
            own = [tile[rows] for tile in tiles]
            if quarter % 2 == 0:
                near_parts = [jnp.where(first, own[t], own[t + 1]) for t in range(3)]
                far_total[p, 0, rows] = jnp.where(first, zero, own[0])
                far_total[p, 1, rows] = jnp.where(first, own[3], zero) + parts[4][rows]
            else:
                near_parts = [jnp.where(first, own[t + 1], own[t + 2]) for t in range(3)]
                far_total[p, 0, rows] = parts[0][rows] + jnp.where(first, zero, own[1])
                far_total[p, 1, rows] = jnp.where(first, own[4], zero)
            for t in range(3):
                bucket[p, rows, 128 * t : 128 * t + 128] = near_parts[t].astype(bf16)
    behind = behind_ref[step]

    @pl.loop(0, behind + ahead_ref[step])
    def _(chunk):
        start = pl.multiple_of(jnp.where(chunk < behind, near - 256 * (chunk + 1), near + NEAR + 256 * (chunk - behind)), 128)
        side = jnp.where(chunk < behind, 0, 1)
        for p in range(group):
            score, part = visit(p, start, CHUNK)
            query_total[p] += part
            far_total[p, side] += score[:, :128] + score[:, 128:]

    for p in range(group):
        lanes = lanes_of(p)
        folded = [far_total[p, side] + pltpu.roll(far_total[p, side], 64, 1) for side in range(2)]
        low_lane = lax.broadcasted_iota(jnp.int32, folded[0].shape, 1) < 64
        bucket[p, :, 384:] = jnp.where(low_lane, *folded).astype(bf16)
        low = (nn(bucket[p], onehot_ref[...]) * 0.125).astype(bf16)
        low = jnp.concatenate([low[:BQ], low[BQ:]], 1)
        placed = nn(low, table[p])
        content_grad = pick(query_total[p]) * 0.125
        query_ref[:, lanes] = (content_grad + placed[:, :128] + placed[:, 128:]).astype(bf16)
        table_total[p] += tn(low, jnp.concatenate([position_ref[:, lanes], ordering_ref[:, lanes]], 1))
        for j, term in enumerate((content_grad, placed[:, :128], placed[:, 128:])):
            sums[j : j + 1, lanes] += jnp.sum(term, axis=0, keepdims=True)

    @pl.when(step == pl.num_programs(1) - 1)
    def _():
        low_lane = lax.broadcasted_iota(jnp.int32, (32, 128), 1) < 64
        for p in range(group):
            lanes = lanes_of(p)
            key_low_ref[:, lanes] = (key_total[p, :, 256 : 256 + length] * LN2).T.astype(bf16)
            value_low_ref[:, lanes] = value_total[p, :, 256 : 256 + length].T.astype(bf16)
            relative_out[:, lanes] = jnp.where(low_lane, table_total[p, 0:32, :128], table_total[p, 128:160, :128])
            order_out[:, lanes] = jnp.where(low_lane[:8], table_total[p, 32:40, 128:], table_total[p, 160:168, 128:])
        sums_out[...] = sums[...]


def fixed(*shape):
    return pl.BlockSpec(shape, lambda *_: (0,) * len(shape), pipeline_mode=pl.Buffered(1))


def ranges(segments):
    length = segments.shape[1]
    own = segments[0]
    blocks = length // (2 * BQ)
    start = 2 * BQ * jnp.arange(blocks, dtype=jnp.int32)
    first = jnp.sum((own[None, :] < own[start][:, None]).astype(jnp.int32), axis=1)
    last = jnp.sum((own[None, :] <= own[start + 2 * BQ - 2][:, None]).astype(jnp.int32), axis=1)
    behind = jnp.maximum(start - 256 - first + CHUNK - 1, 0) // CHUNK
    ahead = jnp.maximum(last - (start - 256 + NEAR) + CHUNK - 1, 0) // CHUNK
    return behind, ahead


def documents(segments):
    length = segments.shape[1]
    lane = jnp.arange(128, dtype=jnp.int32)[None, :]
    same = segments[0][:, None] == lane
    query = same[0::2].astype(bf16)
    away = jnp.where((lane < 8) & ~same, -BIG, 0.0).astype(bf16)
    pad = jnp.broadcast_to(jnp.where(lane < 8, -BIG, 0.0).astype(bf16), (256, 128))
    return query, jnp.concatenate([pad, away, pad], 0)


GROUP = 3


def attend(behind, ahead, content, position, ordering, keys, values, relative, order, away, document):
    rows, width = content.shape
    length = keys.shape[0]
    padded = length + 512
    pairs, blocks, group = width // 128, rows // BQ, GROUP
    wide = 128 * group
    tile = pl.BlockSpec((BQ, wide), lambda p, i, *_: (i, p))
    whole = pl.BlockSpec((length, wide), lambda p, i, *_: (0, p), pipeline_mode=pl.Buffered(1))
    return pl.pallas_call(
        functools.partial(forward_kernel, group),
        name="attend",
        out_shape=(
            jax.ShapeDtypeStruct((pairs, blocks, 2 * BQ, padded), bf16),
            jax.ShapeDtypeStruct((rows, width), bf16),
            jax.ShapeDtypeStruct((rows, width), f32),
            jax.ShapeDtypeStruct((rows, width), f32),
        ),
        grid_spec=pltpu.PrefetchScalarGridSpec(
            num_scalar_prefetch=2,
            grid=(pairs // group, blocks),
            in_specs=[
                tile, tile, tile, whole, whole,
                pl.BlockSpec((32, wide), lambda p, i, *_: (0, p)),
                pl.BlockSpec((2, wide), lambda p, i, *_: (0, p)),
                fixed(padded, 128),
                pl.BlockSpec((BQ, 128), lambda p, i, *_: (i, 0)),
                fixed(5, BQ, 128),
            ],
            out_specs=[pl.BlockSpec((group, 1, 2 * BQ, padded), lambda p, i, *_: (p, i, 0, 0)), tile, tile, tile],
            scratch_shapes=[
                pltpu.VMEM((group, padded, 256), bf16),
                pltpu.VMEM((group, padded, 256), bf16),
                pltpu.VMEM((group, 256, 256), bf16),
                pltpu.VMEM((group, 2 * BQ, 256), f32),
                pltpu.VMEM((group, 2 * BQ, padded), f32),
                pltpu.VMEM((group, 2 * BQ, 128), f32),
                pltpu.VMEM((group, 2 * BQ, 256), f32),
            ],
        ),
        compiler_params=pltpu.CompilerParams(dimension_semantics=("arbitrary", "arbitrary"), vmem_limit_bytes=48 << 20),
        cost_estimate=pl.CostEstimate(flops=40 * 10**9, bytes_accessed=70 * 10**6, transcendentals=10**7),
    )(behind, ahead, content, position, ordering, keys, values, relative, order, away, document,
      jnp.asarray(near_index()))


def attend_back(behind, ahead, probs, grad, mixed, inverse, content, position, ordering, keys, values, relative, order):
    rows, width = content.shape
    length = keys.shape[0]
    padded = length + 512
    pairs, blocks, group = width // 128, rows // BQ, GROUP
    wide = 128 * group
    tile = pl.BlockSpec((BQ, wide), lambda p, i, *_: (i, p))
    whole = pl.BlockSpec((length, wide), lambda p, i, *_: (0, p), pipeline_mode=pl.Buffered(1))
    small = lambda n: pl.BlockSpec((n, wide), lambda p, i, *_: (0, p))
    turn = (np.arange(128)[None, :] + 2 * np.arange(BQ)[:, None]) % 128
    return pl.pallas_call(
        functools.partial(backward_kernel, group),
        name="attend_back",
        out_shape=(
            jax.ShapeDtypeStruct((rows, width), bf16),
            jax.ShapeDtypeStruct((length, width), bf16),
            jax.ShapeDtypeStruct((length, width), bf16),
            jax.ShapeDtypeStruct((32, width), f32),
            jax.ShapeDtypeStruct((8, width), f32),
            jax.ShapeDtypeStruct((8, width), f32),
        ),
        grid_spec=pltpu.PrefetchScalarGridSpec(
            num_scalar_prefetch=2,
            grid=(pairs // group, blocks),
            in_specs=[
                pl.BlockSpec((group, 1, 2 * BQ, padded), lambda p, i, *_: (p, i, 0, 0)),
                tile, tile, tile, tile, tile, tile, whole, whole, small(32), small(2), fixed(BQ, 128), fixed(512, 128),
            ],
            out_specs=[tile, whole, whole, small(32), small(8), small(8)],
            scratch_shapes=[
                pltpu.VMEM((group, padded, 128), bf16),
                pltpu.VMEM((group, padded, 128), bf16),
                pltpu.VMEM((group, 256, 256), bf16),
                pltpu.VMEM((group, 128, padded), f32),
                pltpu.VMEM((group, 128, padded), f32),
                pltpu.VMEM((group, 2 * BQ, 128), f32),
                pltpu.VMEM((group, 2, 2 * BQ, 128), f32),
                pltpu.VMEM((group, 2 * BQ, 512), bf16),
                pltpu.VMEM((group, 256, 256), f32),
                pltpu.VMEM((8, wide), f32),
            ],
        ),
        compiler_params=pltpu.CompilerParams(dimension_semantics=("arbitrary", "arbitrary"), vmem_limit_bytes=48 << 20),
        cost_estimate=pl.CostEstimate(flops=80 * 10**9, bytes_accessed=70 * 10**6, transcendentals=0),
    )(behind, ahead, probs, grad, mixed, inverse, content, position, ordering, keys, values, relative, order,
      jnp.asarray(turn, jnp.int32), jnp.asarray(bucket_onehot(), bf16))


MESH = pl.DeviceIdType.MESH


class Place:
    def __init__(self, replicas, shards):
        self.replicas, self.shards = replicas, shards
        self.cores = 2 if shards % 2 == 0 else 1
        chips = shards // self.cores
        self.across = 2 if chips % 2 == 0 else 1
        self.line = chips // self.across
        self.replica = lax.axis_index("rep")
        own = lax.axis_index("shard")
        self.own = own
        self.core = lax.rem(own, self.cores)
        self.column = lax.rem(own // self.cores, self.across)
        self.spot = own // (self.cores * self.across)

    def shard(self, spot, column, core):
        return (spot * self.across + column) * self.cores + core

    def other_column(self, step):
        return lax.rem(self.column + step, self.across)

    def other_replica(self, step):
        return lax.rem(self.replica + step, self.replicas)

    def device(self, spot=None, column=None, core=None, replica=None):
        spot = self.spot if spot is None else spot
        column = self.column if column is None else column
        core = self.core if core is None else core
        replica = self.replica if replica is None else replica
        return (replica, self.shard(spot, column, core))

    def meet(self):
        barrier = pltpu.get_barrier_semaphore()

        def greet(device):
            pl.semaphore_signal(barrier, inc=1, device_id=device, device_id_type=MESH)

        fixed = 0
        if self.cores > 1:
            greet(self.device(core=1 - self.core))
            fixed += 1
        for step in range(1, self.across):
            greet(self.device(column=self.other_column(step)))
            fixed += 1
        for step in range(1, self.replicas):
            greet(self.device(replica=self.other_replica(step)))
            fixed += 1
        for step, there in ((1, self.spot < self.line - 1), (-1, self.spot > 0)):

            @pl.when(there)
            def _():
                greet(self.device(spot=self.spot + step))

        lined = (self.spot < self.line - 1).astype(jnp.int32) + (self.spot > 0).astype(jnp.int32)
        pl.semaphore_wait(barrier, fixed + lined)


def parts_of(columns, replicas):
    return replicas if columns % (128 * replicas) == 0 else 1


def columns_of(part, parts, columns):
    size = columns // parts
    return pl.ds(pl.multiple_of(part * size, 128), size)


def when(condition, action):
    if condition is True:
        action()
    else:
        pl.when(condition)(action)


def gather_kernel(replicas, shards, count, *refs):
    here = Place(replicas, shards)
    sources, wholes = refs[:count], refs[count : 2 * count]
    line_send, line_recv, cross_send, cross_recv, rep_send, rep_recv, core_send, core_recv = refs[2 * count :]
    here.meet()
    pending = []

    def send(source, whole_view, send_sem, recv_sem, device, condition=True):
        copy = pltpu.make_async_remote_copy(
            src_ref=source, dst_ref=whole_view, send_sem=send_sem, recv_sem=recv_sem, device_id=device, device_id_type=MESH
        )
        when(condition, copy.start)
        pending.append((condition, copy.wait_send))

    def arrived(view, recv_sem, condition=True):
        copy = pltpu.make_async_remote_copy(
            src_ref=view, dst_ref=view, send_sem=recv_sem, recv_sem=recv_sem, device_id=here.device(), device_id_type=MESH
        )
        when(condition, copy.wait_recv)

    def view(k, spot, column, core, part=None):
        whole = wholes[k].at[here.shard(spot, column, core)]
        if part is None:
            return whole
        columns = whole.shape[1]
        return whole.at[:, columns_of(part, parts_of(columns, replicas), columns)]

    def spread(k, spot, condition, own=False):
        columns = wholes[k].shape[2]
        parts = parts_of(columns, replicas)
        part = here.replica if parts > 1 else 0
        target = view(k, spot, here.column, here.core)
        source = sources[k] if own else target
        for step in range(1, here.across):
            cut = columns_of(part, parts, columns)
            send(source.at[:, cut], target.at[:, cut], cross_send.at[k, step, spot], cross_recv.at[k, here.column, spot],
                 here.device(column=here.other_column(step)), condition)
        if here.cores > 1:
            send(source, target, core_send.at[k, 0, here.column, spot], core_recv.at[k, 0, here.column, spot],
                 here.device(core=1 - here.core), condition)

    def crossed(k, spot, condition):
        columns = wholes[k].shape[2]
        parts = parts_of(columns, replicas)
        part = here.replica if parts > 1 else 0
        for step in range(1, here.across):
            column = here.other_column(step)
            piece = view(k, spot, column, here.core, part)
            arrived(piece, cross_recv.at[k, column, spot], condition)
            if parts > 1:
                for hop in range(1, replicas):
                    send(piece, piece, rep_send.at[k, hop, column, spot], rep_recv.at[k, here.replica, column, spot],
                         here.device(replica=here.other_replica(hop)), condition)
            if here.cores > 1:
                send(piece, piece, core_send.at[k, 1, column, spot], core_recv.at[k, 1, column, spot],
                     here.device(core=1 - here.core), condition)

    def replicated(k, spot, condition):
        parts = parts_of(wholes[k].shape[2], replicas)
        if parts == 1:
            return
        for step in range(1, here.across):
            column = here.other_column(step)
            for hop in range(1, replicas):
                replica = here.other_replica(hop)
                piece = view(k, spot, column, here.core, replica)
                arrived(piece, rep_recv.at[k, replica, column, spot], condition)
                if here.cores > 1:
                    send(piece, piece, core_send.at[k, 1 + hop, column, spot], core_recv.at[k, 1 + hop, column, spot],
                         here.device(core=1 - here.core), condition)

    def at(distance, action):
        for k in range(count):
            if distance == 0:
                action(k, here.spot, True)
            else:
                action(k, here.spot - distance, here.spot >= distance)
                action(k, here.spot + distance, here.spot + distance < here.line)

    for k in range(count):
        own = view(k, here.spot, here.column, here.core)
        send(sources[k], own, line_send.at[k, 0, here.spot], line_recv.at[k, here.spot],
             here.device(spot=here.spot + 1), here.spot < here.line - 1)
        send(sources[k], own, line_send.at[k, 1, here.spot], line_recv.at[k, here.spot],
             here.device(spot=here.spot - 1), here.spot > 0)
        spread(k, here.spot, True, own=True)
    for k in range(count):
        wholes[k][here.own] = sources[k][...]

    def along(distance):
        for k in range(count):
            for sign in (-1, 1):
                spot = here.spot + sign * distance
                condition = (spot >= 0) & (spot < here.line)
                piece = view(k, spot, here.column, here.core)
                arrived(piece, line_recv.at[k, spot], condition)
                onward = here.spot - sign
                send(piece, piece, line_send.at[k, 0 if sign < 0 else 1, spot], line_recv.at[k, spot],
                     here.device(spot=onward), condition & (onward >= 0) & (onward < here.line))
                spread(k, spot, condition)

    for distance in range(here.line + 2):
        if 1 <= distance < here.line:
            along(distance)
        if 1 <= distance <= here.line:
            at(distance - 1, crossed)
        if 2 <= distance:
            at(distance - 2, replicated)
    if here.cores > 1:
        for k in range(count):
            columns = wholes[k].shape[2]
            parts = parts_of(columns, replicas)
            for spot in range(here.line):
                other = 1 - here.core
                arrived(view(k, spot, here.column, other), core_recv.at[k, 0, here.column, spot])
                for step in range(1, here.across):
                    column = here.other_column(step)
                    part = here.replica if parts > 1 else 0
                    arrived(view(k, spot, column, other, part), core_recv.at[k, 1, column, spot])
                    for hop in range(1, replicas if parts > 1 else 1):
                        arrived(view(k, spot, column, other, here.other_replica(hop)), core_recv.at[k, 1 + hop, column, spot])
    for condition, wait in pending:
        when(condition, wait)


def gather(mesh, arrays, collective_id):
    replicas, shards = mesh.shape["rep"], mesh.shape["shard"]
    count = len(arrays)
    line = shards // 4
    dma = pltpu.SemaphoreType.DMA
    vmem = pl.BlockSpec(memory_space=pltpu.VMEM)
    moved = sum(a.size * 2 * shards for a in arrays)
    return pl.pallas_call(
        functools.partial(gather_kernel, replicas, shards, count),
        name="gather",
        out_shape=[jax.ShapeDtypeStruct((shards,) + a.shape, a.dtype) for a in arrays],
        in_specs=[vmem] * count,
        out_specs=[vmem] * count,
        scratch_shapes=[
            dma((count, 2, line)), dma((count, line)),
            dma((count, 2, line)), dma((count, 2, line)),
            dma((count, replicas, 2, line)), dma((count, replicas, 2, line)),
            dma((count, replicas + 1, 2, line)), dma((count, replicas + 1, 2, line)),
        ],
        compiler_params=pltpu.CompilerParams(collective_id=collective_id, has_side_effects=True, vmem_limit_bytes=56 << 20),
        cost_estimate=pl.CostEstimate(flops=0, bytes_accessed=moved * 4, transcendentals=0),
    )(*arrays)


def scatter_kernel(replicas, shards, count, chunks, extra, *refs):
    here = Place(replicas, shards)
    take = lambda number: [refs_left.pop(0) for _ in range(number)]
    refs_left = list(refs)
    sources, extras, outs, extra_outs = take(count), take(extra), take(count), take(extra)
    core_bufs, rep_bufs, cross_bufs, line_bufs, last_bufs = (take(count) for _ in range(5))
    extra_bufs = take(extra)
    (core_send, core_recv, rep_send, rep_recv, cross_send, cross_recv, line_send, line_recv, last_send, last_recv) = refs_left
    here.meet()
    pending = []

    def send(source, target, send_sem, recv_sem, device, condition=True):
        copy = pltpu.make_async_remote_copy(
            src_ref=source, dst_ref=target, send_sem=send_sem, recv_sem=recv_sem, device_id=device, device_id_type=MESH
        )
        when(condition, copy.start)
        pending.append((condition, copy.wait_send))

    def arrived(view, recv_sem, condition=True):
        copy = pltpu.make_async_remote_copy(
            src_ref=view, dst_ref=view, send_sem=recv_sem, recv_sem=recv_sem, device_id=here.device(), device_id_type=MESH
        )
        when(condition, copy.wait_recv)

    def add(target, source):
        target[...] = target[...] + source[...]

    steps = range(1, here.across)
    hops = range(1, replicas)

    def split(j):
        return parts_of(chunks[j][2], replicas)

    def columns(j, part=None):
        _, low, size = chunks[j]
        if part is None or split(j) == 1:
            return pl.ds(low, size)
        size = size // replicas
        return pl.ds(pl.multiple_of(low + part * size, 128), size)

    def compact(j):
        _, low, size = chunks[j]
        return pl.ds(low // split(j), size // split(j))

    def mixed(j, column):
        k = chunks[j][0]
        mine = core_bufs[k].at[column, :, :, columns(j)]
        own = sources[k].at[:, column, here.core, :, columns(j)]
        if here.cores > 1:
            arrived(mine, core_recv.at[j, column])
            add(mine, own)
        else:
            mine[...] = own[...]

    def stage_rep(j):
        k = chunks[j][0]
        for step in steps:
            column = here.other_column(step)
            mixed(j, column)
            if split(j) > 1:
                for hop in hops:
                    replica = here.other_replica(hop)
                    send(core_bufs[k].at[column, :, :, columns(j, replica)], rep_bufs[k].at[hop - 1, step - 1, :, :, compact(j)],
                         rep_send.at[j, hop, step], rep_recv.at[j, hop, step], here.device(replica=replica))

    def stage_cross(j):
        k = chunks[j][0]
        for step in steps:
            column = here.other_column(step)
            mine = core_bufs[k].at[column, :, :, columns(j, here.replica)]
            if split(j) > 1:
                for hop in hops:
                    piece = rep_bufs[k].at[hop - 1, step - 1, :, :, compact(j)]
                    arrived(piece, rep_recv.at[j, hop, step])
                    add(mine, piece)
            send(mine, cross_bufs[k].at[step - 1, :, :, compact(j)], cross_send.at[j, step], cross_recv.at[j, step],
                 here.device(column=column))
        mixed(j, here.column)

    def stage_line(distance, j):
        k = chunks[j][0]
        if distance == here.line - 1:
            for step in steps:
                piece = cross_bufs[k].at[step - 1, :, :, compact(j)]
                arrived(piece, cross_recv.at[j, step])
                add(core_bufs[k].at[here.column, :, :, columns(j, here.replica)], piece)
        for sign, way in ((1, 0), (-1, 1)):
            target = here.spot + sign * distance
            inside = (target >= 0) & (target < here.line)
            before = here.spot - sign
            fed = inside & (before >= 0) & (before < here.line)
            mine = core_bufs[k].at[here.column, target, :, columns(j)]
            piece = line_bufs[k].at[way, target, :, columns(j)]
            arrived(piece, line_recv.at[j, way, target], fed)
            when(fed, functools.partial(add, mine, piece))
            send(mine, piece, line_send.at[j, way, target], line_recv.at[j, way, target],
                 here.device(spot=here.spot + sign), inside)

    def stage_last(j):
        k = chunks[j][0]
        mine = core_bufs[k].at[here.column, here.spot, :, columns(j)]
        for sign, way in ((1, 0), (-1, 1)):
            before = here.spot - sign
            fed = (before >= 0) & (before < here.line)
            piece = line_bufs[k].at[way, here.spot, :, columns(j)]
            arrived(piece, line_recv.at[j, way, here.spot], fed)
            when(fed, functools.partial(add, mine, piece))
        for hop in hops:
            send(mine, last_bufs[k].at[here.replica, :, columns(j)], last_send.at[j, hop], last_recv.at[j, here.replica],
                 here.device(replica=here.other_replica(hop)))

    def finish(own, buffer, out, semaphore, cut):
        for hop in hops:
            replica = here.other_replica(hop)
            arrived(buffer.at[replica, :, cut], semaphore.at[replica])
        result = None
        for replica in range(replicas):
            term = jnp.where(here.replica == replica, own[...].astype(f32), buffer[replica, :, cut].astype(f32))
            result = term if result is None else result + term
        out[:, cut] = result

    def stage_finish(j):
        k = chunks[j][0]
        finish(core_bufs[k].at[here.column, here.spot, :, columns(j)], last_bufs[k], outs[k], last_recv.at[j], columns(j))

    if here.cores > 1:
        for j, (k, _, _) in enumerate(chunks):
            for step in (*steps, 0):
                column = here.other_column(step)
                send(sources[k].at[:, column, 1 - here.core, :, columns(j)], core_bufs[k].at[column, :, :, columns(j)],
                     core_send.at[j, column], core_recv.at[j, column], here.device(core=1 - here.core))
    stages = [stage_rep, stage_cross]
    stages += [functools.partial(stage_line, distance) for distance in range(here.line - 1, 0, -1)]
    stages += [stage_last, stage_finish]
    total = len(chunks)
    for time in range(total + len(stages) - 1):
        for place in reversed(range(len(stages))):
            if 0 <= time - place < total:
                stages[place](time - place)
        if time == 0:
            for e in range(extra):
                for hop in hops:
                    send(extras[e], extra_bufs[e].at[here.replica], last_send.at[total + e, hop],
                         last_recv.at[total + e, here.replica], here.device(replica=here.other_replica(hop)))
    for e in range(extra):
        finish(extras[e], extra_bufs[e], extra_outs[e], last_recv.at[total + e], pl.ds(0, extras[e].shape[1]))
    for condition, wait in pending:
        when(condition, wait)


def scatter(mesh, arrays, widths, extras, collective_id):
    replicas, shards = mesh.shape["rep"], mesh.shape["shard"]
    count, extra = len(arrays), len(extras)
    dma = pltpu.SemaphoreType.DMA
    vmem = pl.BlockSpec(memory_space=pltpu.VMEM)
    cores = across = 2
    line = shards // (cores * across)
    shapes = [a.shape[1:] for a in arrays]
    chunks = [
        (k, low, min(width, shapes[k][1])) for k, width in enumerate(widths) for low in range(0, shapes[k][1], min(width, shapes[k][1]))
    ]
    cuts = [(shapes[k][0], shapes[k][1] // parts_of(min(width, shapes[k][1]), replicas)) for k, width in enumerate(widths)]
    moved = sum(a.size * 2 for a in arrays)
    number = len(chunks)
    buffers = (
        [pltpu.VMEM((across, line) + s, bf16) for s in shapes]
        + [pltpu.VMEM((replicas - 1, across - 1, line) + s, bf16) for s in cuts]
        + [pltpu.VMEM((across - 1, line) + s, bf16) for s in cuts]
        + [pltpu.VMEM((2, line) + s, bf16) for s in shapes]
        + [pltpu.VMEM((replicas,) + s, bf16) for s in shapes]
        + [pltpu.VMEM((replicas,) + e.shape, bf16) for e in extras]
    )
    return pl.pallas_call(
        functools.partial(scatter_kernel, replicas, shards, count, chunks, extra),
        name="scatter",
        out_shape=[jax.ShapeDtypeStruct(s, f32) for s in shapes] + [jax.ShapeDtypeStruct(e.shape, f32) for e in extras],
        in_specs=[vmem] * (count + extra),
        out_specs=[vmem] * (count + extra),
        scratch_shapes=buffers + [
            dma((number, across)), dma((number, across)),
            dma((number, replicas, across)), dma((number, replicas, across)),
            dma((number, across)), dma((number, across)),
            dma((number, 2, line)), dma((number, 2, line)),
            dma((number + extra, replicas)), dma((number + extra, replicas)),
        ],
        compiler_params=pltpu.CompilerParams(collective_id=collective_id, has_side_effects=True, vmem_limit_bytes=62 << 20),
        cost_estimate=pl.CostEstimate(flops=0, bytes_accessed=moved * 4, transcendentals=0),
    )(*[a.reshape((line, across, cores) + a.shape[1:]) for a in arrays], *extras)


FIRST_VECTOR = 34


def mixing(mix):
    rows = mix.shape[0]
    place = lax.broadcasted_iota(jnp.int32, (rows, 2 * rows), 1) - 2 * lax.broadcasted_iota(jnp.int32, (rows, 2 * rows), 0)
    own = jnp.broadcast_to(mix[:, :1], place.shape)
    next_one = jnp.broadcast_to(mix[:, 64:65], place.shape)
    return jnp.where(place == 0, own, jnp.where(place == 1, next_one, 0.0)).astype(bf16)


def project_kernel(
    tokens_ref, mix_ref, weight_ref, small_ref,
    pooled_ref, content_ref, position_ref, ordering_ref, key_ref, value_ref,
):
    width = tokens_ref.shape[1]
    tokens = tokens_ref[...]
    pooled = nn(mixing(mix_ref[...]), tokens)
    pooled_ref[...] = pooled
    key_ref[...] = nn(tokens, weight_ref[:, width : 2 * width]).astype(bf16)
    value_ref[...] = nn(tokens, weight_ref[:, 2 * width :]).astype(bf16)
    queries = nn(pooled.astype(bf16), weight_ref[:, :width])
    bias = small_ref[FIRST_VECTOR : FIRST_VECTOR + 3, :].astype(f32)
    content_ref[...] = ((queries + bias[0:1]) * (0.125 * LOG2E)).astype(bf16)
    position_ref[...] = (queries + bias[1:2]).astype(bf16)
    ordering_ref[...] = (queries + bias[2:3]).astype(bf16)


def project(tokens, mix, weight, small):
    length, width = tokens.shape
    block = 256
    steps = length // block
    whole = pl.BlockSpec((block, width), lambda i: (i, 0))
    half = pl.BlockSpec((block // 2, width), lambda i: (i, 0))
    rows = jax.ShapeDtypeStruct((length // 2, width), bf16)
    full = jax.ShapeDtypeStruct((length, width), bf16)
    return pl.pallas_call(
        project_kernel,
        name="project",
        grid=(steps,),
        out_shape=(jax.ShapeDtypeStruct((length // 2, width), f32), rows, rows, rows, full, full),
        in_specs=[whole, pl.BlockSpec((block // 2, 128), lambda i: (i, 0)), fixed(*weight.shape), fixed(*small.shape)],
        out_specs=[half, half, half, half, whole, whole],
        compiler_params=pltpu.CompilerParams(vmem_limit_bytes=40 << 20),
        cost_estimate=pl.CostEstimate(flops=5 * length * width * width, bytes_accessed=10 * length * width, transcendentals=0),
    )(tokens, mix, weight, small)


def mean(values):
    return jnp.mean(values, axis=1, keepdims=True)


def normalize(values):
    centered = values - mean(values)
    inverse = lax.rsqrt(mean(centered * centered) + 1e-05)
    return centered * inverse, inverse


def norm_back(grad, normed, inverse):
    return inverse * (grad - mean(grad) - normed * mean(grad * normed))


def column_sum(values):
    return jnp.sum(values, axis=0, keepdims=True)


def middle_kernel(
    blocks, context_ref, pooled_ref, cotangent_ref, wide_ref, outer_ref, small_ref, bias_ref,
    layer_ref, sum_ref, context_grad_ref, sums_ref, inner_sums_ref, output_out, inner_out, outer_out,
    act, back, slope, first_all, outer_all, attended_all, context_all,
):
    step = pl.program_id(0)
    size, width = pooled_ref.shape
    hidden = bias_ref.shape[1]
    chunks = [slice(c * width, (c + 1) * width) for c in range(hidden // width)]

    @pl.when(step == 0)
    def _():
        sums_ref[...] = jnp.zeros(sums_ref.shape, f32)
        inner_sums_ref[...] = jnp.zeros(inner_sums_ref.shape, f32)

    @pl.when(step < blocks)
    def _():
        rows = pl.ds(pl.multiple_of(step * size, size), size)

        def vector(j):
            return small_ref[FIRST_VECTOR + j : FIRST_VECTOR + j + 1, :].astype(f32)

        context = context_ref[...]
        context_all[rows, :] = context
        first_norm, first_inverse = normalize(pooled_ref[...] + nn(context, wide_ref[:, :width]))
        first = first_norm * vector(3) + vector(4)
        first_low = first.astype(bf16)
        first_all[rows, :] = first_low
        outer = None
        for cut in chunks:
            inner = nn(first_low, wide_ref[:, width + cut.start : width + cut.stop]) + bias_ref[:, cut].astype(f32)
            cumulative = 0.5 * (1.0 + lax.erf(inner * math.sqrt(0.5)))
            act_low = (inner * cumulative).astype(bf16)
            act[rows, cut] = act_low
            slope[:, cut] = cumulative + inner * (jnp.exp(-0.5 * inner * inner) * (1.0 / math.sqrt(2.0 * math.pi)))
            part = nn(act_low, outer_ref[cut, :])
            outer = part if outer is None else outer + part
        second_norm, second_inverse = normalize(first + outer + vector(5))
        layer_ref[...] = (second_norm * vector(6) + vector(7)).astype(bf16)
        cotangent = cotangent_ref[...].astype(f32)
        mid_grad = norm_back(cotangent * vector(6), second_norm, second_inverse)
        outer_low = mid_grad.astype(bf16)
        outer_all[rows, :] = outer_low
        first_grad = mid_grad
        for cut in chunks:
            inner_grad = nt(outer_low, outer_ref[cut, :]) * slope[:, cut]
            inner_low = inner_grad.astype(bf16)
            back[rows, cut] = inner_low
            inner_sums_ref[0:1, cut] += column_sum(inner_low.astype(f32))
            first_grad = first_grad + nt(inner_low, wide_ref[:, width + cut.start : width + cut.stop])
        sum_grad = norm_back(first_grad * vector(3), first_norm, first_inverse)
        sum_ref[...] = sum_grad
        attended_low = sum_grad.astype(bf16)
        attended_all[rows, :] = attended_low
        context_grad_ref[...] = nt(attended_low, wide_ref[:, :width]).astype(bf16)
        for j, term in enumerate(
            (first_grad * first_norm, first_grad, outer_low.astype(f32), cotangent * second_norm, cotangent)
        ):
            sums_ref[j : j + 1, :] += column_sum(term)

    for c, cut in enumerate(chunks):

        @pl.when(step == blocks + c)
        def _():
            outer_out[...] = tn(act[:, cut], outer_all[...]).astype(bf16)
            inner_out[...] = tn(first_all[...], back[:, cut]).astype(bf16)

    @pl.when(step == blocks + len(chunks))
    def _():
        output_out[...] = tn(context_all[...], attended_all[...]).astype(bf16)


def middle(context, pooled, cotangent, wide, outer, small, bias):
    rows, width = context.shape
    hidden = bias.shape[1]
    size = 256
    blocks, chunks = rows // size, hidden // width
    block = pl.BlockSpec((size, width), lambda i: (jnp.minimum(i, blocks - 1), 0))
    chunk = lambda i: jnp.clip(i - blocks, 0, chunks - 1)
    low = jax.ShapeDtypeStruct((rows, width), bf16)
    flops = 18 * rows * width * hidden
    return pl.pallas_call(
        functools.partial(middle_kernel, blocks),
        name="middle",
        grid=(blocks + chunks + 1,),
        out_shape=(
            low,
            jax.ShapeDtypeStruct((rows, width), f32),
            low,
            jax.ShapeDtypeStruct((8, width), f32),
            jax.ShapeDtypeStruct((8, hidden), f32),
            jax.ShapeDtypeStruct((width, width), bf16),
            jax.ShapeDtypeStruct((width, hidden), bf16),
            jax.ShapeDtypeStruct((hidden, width), bf16),
        ),
        in_specs=[block, block, block, fixed(*wide.shape), fixed(*outer.shape), fixed(*small.shape), fixed(*bias.shape)],
        out_specs=[
            block, block, block, fixed(8, width), fixed(8, hidden), fixed(width, width),
            pl.BlockSpec((width, width), lambda i: (0, chunk(i))),
            pl.BlockSpec((width, width), lambda i: (chunk(i), 0)),
        ],
        scratch_shapes=[
            pltpu.VMEM((rows, hidden), bf16),
            pltpu.VMEM((rows, hidden), bf16),
            pltpu.VMEM((size, hidden), f32),
            pltpu.VMEM((rows, width), bf16),
            pltpu.VMEM((rows, width), bf16),
            pltpu.VMEM((rows, width), bf16),
            pltpu.VMEM((rows, width), bf16),
        ],
        compiler_params=pltpu.CompilerParams(vmem_limit_bytes=60 << 20),
        cost_estimate=pl.CostEstimate(flops=flops, bytes_accessed=40 * rows * width, transcendentals=2 * rows * hidden),
    )(context, pooled, cotangent, wide, outer, small, bias)


def tail_kernel(
    tokens_ref, key_ref, value_ref, query_ref, sum_ref, pooled_ref, mix_ref, weight_ref,
    tokens_grad_ref, weight_grad_ref, total,
):
    step = pl.program_id(0)
    width = tokens_ref.shape[1]

    @pl.when(step == 0)
    def _():
        total[...] = jnp.zeros(total.shape, f32)

    tokens, query_low, key_low, value_low = tokens_ref[...], query_ref[...], key_ref[...], value_ref[...]
    pooled_grad = sum_ref[...] + nt(query_low, weight_ref[:, :width])
    coarse = pooled_grad.astype(bf16)
    fine = (pooled_grad - coarse.astype(f32)).astype(bf16)
    mix = mixing(mix_ref[...])
    tokens_grad_ref[...] = (
        tn(mix, coarse) + tn(mix, fine)
        + nt(key_low, weight_ref[:, width : 2 * width])
        + nt(value_low, weight_ref[:, 2 * width :])
    )
    total[:, :width] += tn(pooled_ref[...].astype(bf16), query_low)
    total[:, width : 2 * width] += tn(tokens, key_low)
    total[:, 2 * width :] += tn(tokens, value_low)

    @pl.when(step == pl.num_programs(0) - 1)
    def _():
        weight_grad_ref[...] = total[...].astype(bf16)


def tail(tokens, key_low, value_low, query_low, sum_grad, pooled, mix, weight):
    length, width = tokens.shape
    block = 256
    whole = pl.BlockSpec((block, width), lambda i: (i, 0))
    half = pl.BlockSpec((block // 2, width), lambda i: (i, 0))
    return pl.pallas_call(
        tail_kernel,
        name="tail",
        grid=(length // block,),
        out_shape=(jax.ShapeDtypeStruct((length, width), f32), jax.ShapeDtypeStruct((width, 3 * width), bf16)),
        in_specs=[whole, whole, whole, half, half, half, pl.BlockSpec((block // 2, 128), lambda i: (i, 0)), fixed(*weight.shape)],
        out_specs=[whole, fixed(width, 3 * width)],
        scratch_shapes=[pltpu.VMEM((width, 3 * width), f32)],
        compiler_params=pltpu.CompilerParams(vmem_limit_bytes=48 << 20),
        cost_estimate=pl.CostEstimate(flops=10 * length * width * width, bytes_accessed=16 * length * width, transcendentals=0),
    )(tokens, key_low, value_low, query_low, sum_grad, pooled, mix, weight)


def body(
    mesh,
    tokens,
    segment_ids,
    query_weight,
    key_weight,
    value_weight,
    output_weight,
    relative_table,
    order_table,
    content_bias,
    position_bias,
    order_bias,
    first_gain,
    first_shift,
    inner_weight,
    inner_bias,
    outer_weight,
    outer_bias,
    second_gain,
    second_shift,
    cotangent,
):
    shards = mesh.shape["shard"]
    width = tokens.shape[1]
    hidden = inner_weight.shape[1]
    each = width // shards
    folds = hidden // width
    vectors = (content_bias, position_bias, order_bias, first_gain, first_shift, outer_bias, second_gain, second_shift)
    small = jnp.concatenate(
        [relative_table, order_table] + [v[None, :] for v in vectors] + [inner_bias.reshape(folds, each)], 0
    )
    small_rows = small.shape[0]
    spare = -small_rows % 16
    small = jnp.pad(small, ((0, spare), (0, 128 - each)))
    projections, small_all = gather(mesh, [jnp.concatenate([query_weight, key_weight, value_weight], 1), small], 0)
    projections = projections.reshape(width, 3 * width)
    small_all = small_all[:, :, :each].transpose(1, 0, 2).reshape(-1, width)
    weight_relative, weight_order = small_all[:32], small_all[32:34]
    bias_inner = small_all[42 : 42 + folds].reshape(folds, shards, each).transpose(1, 0, 2).reshape(1, hidden)
    wide = lax.all_gather(jnp.concatenate([output_weight, inner_weight], 1), "shard", axis=0, tiled=True)
    weight_outer = lax.all_gather(outer_weight, "shard", axis=0, tiled=True)

    joined = (segment_ids[0, 0::2] == segment_ids[0, 1::2])[:, None]
    own = jnp.where(joined, 0.5, 1.0)
    mix = jnp.where(jnp.arange(128)[None, :] < 64, own, 1.0 - own)
    pooled, content, position, ordering, keys, values = project(tokens, mix, projections, small_all)
    behind, ahead = ranges(segment_ids)
    document, away = documents(segment_ids)
    probs, context, mixed, inverse = attend(
        behind, ahead, content, position, ordering, keys, values, weight_relative, weight_order, away, document
    )
    layer_out, sum_grad, context_grad, sums, inner_sums, output_grad, inner_grad, outer_grad = middle(
        context, pooled, cotangent, wide, weight_outer, small_all, bias_inner
    )
    query_low, key_low, value_low, relative_grad, order_grad, bias_sums = attend_back(
        behind, ahead, probs, context_grad, mixed, inverse, content, position, ordering,
        keys, values, weight_relative, weight_order,
    )
    tokens_grad, projection_grad = tail(tokens, key_low, value_low, query_low, sum_grad, pooled, mix, projections)
    small_grad = jnp.concatenate(
        [relative_grad, order_grad[:2], bias_sums[:3], sums[:5],
         inner_sums[0].reshape(shards, folds, each).transpose(1, 0, 2).reshape(folds, width)],
        0,
    )
    small_grad = small_grad.reshape(small_rows, shards, each).transpose(1, 0, 2)
    small_grad = jnp.pad(small_grad, ((0, 0), (0, spare), (0, 128 - each))).astype(bf16)
    outer_part = lax.psum_scatter(outer_grad, "shard", scatter_dimension=0, tiled=True)
    inner_sum, output_sum, projection_sum, small_sum, outer_sum = scatter(
        mesh,
        [
            inner_grad.reshape(shards, each, hidden),
            output_grad.reshape(shards, each, width),
            projection_grad.reshape(shards, each, 3 * width),
            small_grad,
        ],
        [width, width, width, 128],
        [outer_part],
        1,
    )
    small_sum = small_sum[:, :each]
    own = [small_sum[34 + j] for j in range(8)]
    return (
        layer_out,
        tokens_grad,
        *[projection_sum[:, j * width : (j + 1) * width] for j in range(3)],
        output_sum,
        small_sum[:32],
        small_sum[32:34],
        *own[:5],
        inner_sum,
        small_sum[42 : 42 + folds].reshape(folds * each),
        outer_sum,
        *own[5:],
    )


def solution(mesh):
    placed = (
        P(("rep", "shard"), None),
        P(("rep", "shard"), None),
        P("shard", None),
        P("shard", None),
        P("shard", None),
        P("shard", None),
        P(None, "shard"),
        P(None, "shard"),
        P("shard"),
        P("shard"),
        P("shard"),
        P("shard"),
        P("shard"),
        P("shard", None),
        P("shard"),
        P("shard", None),
        P("shard"),
        P("shard"),
        P("shard"),
        P(("rep", "shard"), None),
    )
    return jax.shard_map(
        functools.partial(body, mesh),
        mesh=mesh,
        in_specs=placed,
        out_specs=(
            P(("rep", "shard"), None),
            P(("rep", "shard"), None),
            P("shard", None),
            P("shard", None),
            P("shard", None),
            P("shard", None),
            P(None, "shard"),
            P(None, "shard"),
            P("shard"),
            P("shard"),
            P("shard"),
            P("shard"),
            P("shard"),
            P("shard", None),
            P("shard"),
            P("shard", None),
            P("shard"),
            P("shard"),
            P("shard"),
        ),
        check_vma=False,
    )
```

time: 1200 us -> 456 us (0.38)
  waiting for transfers between devices: 559 us -> 0.73 us
  Pallas kernels: 195 us -> 389 us
  blocking collectives: 170 us -> 0 us
  matrix products: 148 us -> 0 us
  local copies, waits for them, and re-layouts: 83.5 us -> 38.5 us
  other arithmetic: 17.7 us -> 4.81 us
    reduce_scatter x4 -> x1, waiting for transfers between devices: 360 us -> 0.01 us  [body(): lax.psum_scatter(outer_grad, 'shard', scatter_dimension=0, tiled=True)]
    pallas_call x2 -> x7, Pallas kernels: 195 us -> 389 us  [the longest x1 107 us: scatter(): pl.pallas_call(functools.partial(scatter_kernel, replicas, shards, count,...]
    dot_general x18 -> x0, matrix products: 148 us -> none  [matmul(): return jnp.dot(left, right, preferred_element_type=jnp.float32)]
    unnamed x19 -> x3, waiting for transfers between devices: 139 us -> 0.71 us
    unnamed x2 -> x0, blocking collectives: 124 us -> none
    psum x1 -> x0, waiting for transfers between devices: 59.9 us -> none  [body(): lax.psum((owned[0], owned[1], owned[2], owned[3], owned[4], owned[5], own...]
    all_gather x2 -> x0, blocking collectives: 36.8 us -> none  [the longest x1 19.1 us: body(): lax.all_gather(order_table, 'shard', axis=1, tiled=True)]
    unnamed x124 -> x37, local copies, waits for them, and re-layouts: 40 us -> 19.1 us
  transfers between devices with their start and end apart: 15 -> 3, of which waited for: 8 -> 0; matrix products, arithmetic and copies ran while one was open for 16% -> 4% of each run, Pallas kernels for 8% -> 50%
where the time goes in v2:
time: 456 us; the launch traced here: 447 us
  Pallas kernels  389 us (85%)
  local copies, waits for them, and re-layouts  38.5 us (8%)
  between operations  14.3 us (3%)
  other arithmetic  4.81 us (1%)
    pallas_call x1, Pallas kernels, scatter(): pl.pallas_call(functools.partial(scatter_kernel, replicas, shards, count,...  107 us
    pallas_call x1, Pallas kernels, attend_back(): pl.pallas_call(functools.partial(backward_kernel, group), name='attend_ba...  72.8 us
    pallas_call x1, Pallas kernels, attend(): pl.pallas_call(functools.partial(forward_kernel, group), name='attend', o...  61 us
    pallas_call x1, Pallas kernels, middle(): pl.pallas_call(functools.partial(middle_kernel, blocks), name='middle', g...  60.2 us
    pallas_call x1, Pallas kernels, gather(): pl.pallas_call(functools.partial(gather_kernel, replicas, shards, count),...  51 us
    pallas_call x1, Pallas kernels, tail(): pl.pallas_call(tail_kernel, name='tail', grid=(length // block,), out_sha...  25.6 us
    unnamed x37, local copies, waits for them, and re-layouts  19.1 us
    pallas_call x1, Pallas kernels, project(): pl.pallas_call(project_kernel, name='project', grid=(steps,), out_shape=(...  11.2 us
  transfers between devices with their start and end apart: 3, of which 0 were waited for; matrix products, arithmetic and copies ran while one was open for 4% of the time, Pallas kernels for 50%

profile of v2, /device:TPU:0, one launch (start us, length us, event | category | flops | bytes accessed | tf_op | source)
XLA Modules:
  0.0 447.0 jit_solution(10164162618377994074)
XLA Ops:
  7.2 0.0 all-gather.5.cloned.1.call-start
  7.2 0.7 all-gather.5.cloned.1.call-update
  7.9 0.0 all-gather.3.cloned.1.call-start
  8.0 1.7 pad_maximum_fusion.1
  9.7 0.0 all-gather.3.cloned.1.call-update
  9.7 0.0 reduce-scatter.2.cloned.1.call-start
  9.8 0.9 slice.99
  10.7 0.9 slice.98
  11.7 0.7 reshape.143
  12.4 2.2 concatenate.26
  14.6 0.6 pad.9.refs_1_
  15.2 1.7 pad_maximum_fusion.2.refs_0_
  16.9 51.0 %gather.13 = (bf16[16,48,2304]{2,1,0:T(8,128)(2,1)}, bf16[16,48,128]{2,1,0:T(8,128)(2,1)}) custom-call(bf16[48,2304]{1,0:T(8,128)(2,1)} %pad_maximum_fusion.2.refs_0_, bf16[48,128]{1,0:T(8,128)(2,1)} %pad.9.refs_1_), custom_call_target="tpu_custom_call" | custom-call | bytes 14942208 | tf_op jit(solution)/shard_map/gather/pallas_call | solution.py:626
  67.9 0.9 slice_bitcast_fusion
  68.9 0.1 copy.56
  69.0 0.6 gather_fusion
  69.6 0.6 gather_fusion.1
  70.3 0.3 iota_compare_fusion
  70.6 0.8 slice.105
  71.4 0.1 convert_element_type.31.document_ref
  71.5 0.1 slice.104.order_ref
  71.6 0.7 reshape.146.bias_ref
  72.3 0.2 reshape.145.small_ref
  72.6 0.1 copy.57
  72.6 0.2 slice.102.relative_ref
  72.8 0.2 convert_reduce_fusion
  73.1 0.3 broadcast_select_fusion.mix_ref
  73.5 0.3 select_convert_fusion
  73.9 0.0 copy-start.4
  73.9 11.2 %project.1 = (f32[1024,768]{1,0:T(8,128)S(1)}, bf16[1024,768]{1,0:T(8,128)(2,1)S(1)}, bf16[1024,768]{1,0:T(8,128)(2,1)S(1)}, bf16[1024,768]{1,0:T(8,128)(2,1)S(1...) custom-call(bf16[2048,768]{1,0:T(8,128)(2,1)} %tokens_ref.3, f32[1024,128]{1,0:T(8,128)S(1)} %broadcast_select_fusion.mix_ref, ...), custom_call_target="tpu_custom_call" | custom-call | flops 6039797760 | bytes 15728640 | tf_op jit(solution)/shard_map/project/pallas_call | solution.py:869
  85.1 1.7 copy-done.7
  86.8 1.6 copy-done.8
  88.4 1.1 copy-done.10
  89.6 61.0 %attend.1 = (bf16[6,8,256,2560]{3,2,1,0:T(8,128)(2,1)}, bf16[1024,768]{1,0:T(8,128)(2,1)S(1)}, f32[1024,768]{1,0:T(8,128)}, f32[1024,768]{1,0:T(8,128)}) custom-call(s32[8]{0:T(128)S(1)} %get-tuple-element.99.behind_ref, s32[8]{0:T(128)S(1)} %get-tuple-element.98.ahead_ref, bf16[1024,768]{1,0:T(8,128)(2,1)S(1)} %get-tuple-element.54.content_ref, ...), custom_call_target="tpu_custom_call" | custom-call | flops 40000000000 | bytes 70000000 | tf_op jit(solution)/shard_map/attend/pallas_call | solution.py:334
  150.6 1.2 copy-done.9
  151.8 1.2 copy-done.13
  153.0 60.2 %middle.1 = (bf16[1024,768]{1,0:T(8,128)(2,1)}, f32[1024,768]{1,0:T(8,128)}, bf16[1024,768]{1,0:T(8,128)(2,1)}, f32[8,768]{1,0:T(8,128)}, f32[8,3072]{1,0:T(8,12...) custom-call(bf16[1024,768]{1,0:T(8,128)(2,1)} %copy-done.13, ...), custom_call_target="tpu_custom_call" | custom-call | flops 43486543872 | bytes 31457280 | tf_op jit(solution)/shard_map/middle/pallas_call | solution.py:980
  213.2 0.0 reduce-scatter.2.cloned.1.call-update
  213.2 0.9 copy-done.5
  214.1 1.4 copy-done.14
  215.5 72.8 %attend_back.1 = (bf16[1024,768]{1,0:T(8,128)(2,1)S(1)}, bf16[2048,768]{1,0:T(8,128)(2,1)}, bf16[2048,768]{1,0:T(8,128)(2,1)}, f32[32,768]{1,0:T(8,128)S(1)}, f3...) custom-call(s32[8]{0:T(128)S(1)} %get-tuple-element.99.behind_ref, s32[8]{0:T(128)S(1)} %get-tuple-element.98.ahead_ref, ...), custom_call_target="tpu_custom_call" | custom-call | flops 80000000000 | bytes 70000000 | tf_op jit(solution)/shard_map/attend_back/pallas_call | solution.py:381
  288.3 1.1 copy-done.11
  289.4 0.1 concatenate.30
  289.5 0.1 concatenate.31
  289.6 0.9 fusion
  290.6 0.1 reshape_squeeze.4
  290.7 0.1 concatenate.32
  290.8 0.2 concatenate.29
  291.0 0.3 concatenate.33
  291.3 0.7 pad.10
  292.0 1.9 copy-done.3
  294.0 1.4 copy-done.12
  295.4 25.6 %tail.1 = (f32[2048,768]{1,0:T(8,128)}, bf16[768,2304]{1,0:T(8,128)(2,1)}) custom-call(bf16[2048,768]{1,0:T(8,128)(2,1)S(1)} %copy-done.3, bf16[2048,768]{1,0:T(8,128)(2,1)} %get-tuple-element.66.key_ref, bf16[2048,768]{1,0:T(8,128)(2,1)} %get-tuple-element.67.value_ref, bf16[1024,768]{1,0:T(8,128)(2,1)S(1)} %copy-done.12, ...), custom_call_target="tpu_custom_call" | custom-call | flops 12079595520 | bytes 25165824 | tf_op jit(solution)/shard_map/tail/pallas_call | solution.py:1049
  321.0 0.0 reduce-scatter.2.cloned.1.call-done.refs_4_
  321.1 106.6 %scatter.1 = (f32[48,3072]{1,0:T(8,128)}, f32[48,768]{1,0:T(8,128)}, f32[48,2304]{1,0:T(8,128)}, f32[48,128]{1,0:T(8,128)}, f32[192,768]{1,0:T(8,128)}) custom-call(bf16[4,2,2,48,3072]{4,3,2,1,0:T(8,128)(2,1)} %bitcast.46, bf16[4,2,2,48,768]{4,3,2,1,0:T(8,128)(2,1)} %bitcast.48, bf16[4,2,2,48,2304]{4,3,2,1,0:T(8,128)(2,1)} %bitcast.47, ...), custom_call_target="tpu_custom_call" | custom-call | bytes 38535168 | tf_op jit(solution)/shard_map/scatter/pallas_call | solution.py:815
  427.7 1.2 slice.115
  428.9 0.7 slice.121
  429.6 1.4 slice_bitcast_fusion.2
  431.1 1.3 slice.114
  432.4 1.8 fusion.3
  434.2 0.6 reshape.148
  434.9 1.6 copy.66
  436.4 1.9 copy.67
  438.4 1.9 copy.68
  (49 shorter events, 0.3 us)
Async XLA Ops:
  7.2 61.8 %copy-start.15 = (s32[1,2048]{1,0:T(1,128)S(1)}, s32[1,2048]{1,0:T(1,128)}, u32[]{:S(2)}) copy-start(s32[1,2048]{1,0:T(1,128)} %param.24) | copy-start | bytes 24580
  7.2 145.8 %all-gather.5.cloned.1.call-start = ((), (), s32[]{:S(2)}) async-start(), calls=%async_computation.2 | async-start | bytes 5013504 | tf_op jit(solution)/shard_map/all_gather | solution.py:1103
  7.9 145.0 %all-gather.3.cloned.1.call-start = ((), (), s32[]{:S(2)}) async-start(), calls=%async_computation.1 | async-start | bytes 6266880 | tf_op jit(solution)/shard_map/all_gather | solution.py:1102
  9.7 311.3 %reduce-scatter.2.cloned.1.call-start = ((), (), s32[]{:S(2)}) async-start(), calls=%async_computation.3 | async-start | bytes 5013504 | tf_op jit(solution)/shard_map/reduce_scatter | solution.py:1129
  72.5 12.5 %copy-start.2 = (bf16[48,768]{1,0:T(8,128)(2,1)}, bf16[48,768]{1,0:T(8,128)(2,1)S(1)}, u32[]{:S(2)}) copy-start(bf16[48,768]{1,0:T(8,128)(2,1)S(1)} %reshape.145.small_ref) | copy-start | bytes 221188
  73.4 11.6 %copy-start = (f32[1024,128]{1,0:T(8,128)}, f32[1024,128]{1,0:T(8,128)S(1)}, u32[]{:S(2)}) copy-start(f32[1024,128]{1,0:T(8,128)S(1)} %broadcast_select_fusion.mix_ref) | copy-start | bytes 1572868
  73.9 15.7 %copy-start.4 = (s32[5,128,128]{2,1,0:T(8,128)S(1)}, s32[5,128,128]{2,1,0:T(8,128)}, u32[]{:S(2)}) copy-start(s32[5,128,128]{2,1,0:T(8,128)} %constant.71.clone.index_ref) | copy-start | bytes 983044
  85.1 1.7 copy-start.7
  86.8 1.6 copy-start.8
  88.4 1.1 copy-start.10
  150.6 1.2 copy-start.9
  151.8 1.2 copy-start.13
  213.2 0.9 copy-start.5
  213.2 0.9 copy-start.6
  214.1 1.4 copy-start.14
  215.5 75.2 %copy-start.16 = (f32[8,768]{1,0:T(8,128)S(1)}, f32[8,768]{1,0:T(8,128)}, u32[]{:S(2)}) copy-start(f32[8,768]{1,0:T(8,128)} %get-tuple-element.77) | copy-start | bytes 73732
  215.5 76.6 %copy-start.1 = (f32[1024,128]{1,0:T(8,128)S(1)}, f32[1024,128]{1,0:T(8,128)}, u32[]{:S(2)}) copy-start(f32[1024,128]{1,0:T(8,128)} %copy-done) | copy-start | bytes 1572868
  288.3 1.1 copy-start.11
  292.0 1.9 copy-start.3
  294.0 1.4 copy-start.12
Sparse Core Ops, SparseCore 0:
  10.3 59.9 all-gather.4
  73.2 61.4 all-gather.2
  213.3 84.6 reduce-scatter.1

commit v3 on v2

--- a/solution.py
+++ b/solution.py
@@ -67,11 +67,20 @@
 
 
 def take(table, index):
-    return jnp.take_along_axis(table, index, axis=1, mode="promise_in_bounds")
+    numbers = lax.GatherDimensionNumbers(
+        offset_dims=(), collapsed_slice_dims=(1,), start_index_map=(1,),
+        operand_batching_dims=(0,), start_indices_batching_dims=(0,),
+    )
+    return lax.gather(table, index[:, :, None], numbers, (1, 1), mode=lax.GatherScatterMode.PROMISE_IN_BOUNDS)
 
 
 def lanes_of(p):
     return slice(128 * p, 128 * p + 128)
+
+
+def far_start(chunk, behind, far, near):
+    start = jnp.where(chunk < behind, near - CHUNK * (chunk + 1), near + NEAR + CHUNK * (chunk - behind))
+    return pl.multiple_of(jnp.where(chunk < far, start, 0), 128)
 
 
 def forward_kernel(
@@ -104,6 +113,9 @@
             for half, (relative, order) in enumerate(zip(halves(relative_ref[:, lanes]), halves(orders))):
                 both = jnp.concatenate([relative, order], 1)
                 table[p, 128 * half : 128 * half + 32, :] = both
+                for side, bucket in ((0, 31), (1, 15)):
+                    start = 256 + 256 * side + 128 * half
+                    table[p, start : start + 128, :] = jnp.broadcast_to(both[bucket : bucket + 1].astype(f32), (128, 256)).astype(bf16)
 
     document = document_ref[...]
     near = pl.multiple_of(step * 256, 256)
@@ -116,12 +128,13 @@
     for p in range(group):
         lanes = lanes_of(p)
         places = nt(jnp.concatenate([position_ref[:, lanes], ordering_ref[:, lanes]], 1), table[p]) * (0.125 * LOG2E)
-        place = (places[:, :128], places[:, 128:])
+        place = (places[:, :128], places[:, 128:256])
         near_scores = nt(queries[p], keys[p, pl.ds(near, NEAR), :])
         for half in range(2):
             rows = slice(BQ * half, BQ * half + BQ)
-            for side, bucket in ((0, 31), (1, 15)):
-                bias[p, rows, 128 * side : 128 * side + 128] = jnp.broadcast_to(place[half][:, bucket : bucket + 1], (BQ, 128))
+            for side in range(2):
+                start = 256 + 256 * side + 128 * half
+                bias[p, rows, 128 * side : 128 * side + 128] = places[:, start : start + 128]
             for quarter in range(2):
                 own = slice(64 * quarter, 64 * quarter + 64)
                 rows = slice(BQ * half + 64 * quarter, BQ * half + 64 * quarter + 64)
@@ -139,19 +152,20 @@
     far = behind + ahead_ref[step]
 
     def start_of(chunk):
-        return pl.multiple_of(jnp.where(chunk < behind, near - 256 * (chunk + 1), near + NEAR + 256 * (chunk - behind)), 128)
-
-    @pl.loop(0, far)
-    def _(chunk):
-        start = start_of(chunk)
-        place = pl.multiple_of(jnp.where(chunk < behind, 0, 128), 128)
-        for p in range(group):
-            part = nt(queries[p], keys[p, pl.ds(start, CHUNK), :])
-            extra = bias[p, :, pl.ds(place, 128)]
-            left, right = part[:, :128] + extra, part[:, 128:] + extra
-            scores[p, :, pl.ds(start, 128)] = left
-            scores[p, :, pl.ds(start + 128, 128)] = right
-            peak[p] = jnp.maximum(peak[p], jnp.maximum(left, right))
+        return far_start(chunk, behind, far, near)
+
+    @pl.loop(0, (far + 1) // 2)
+    def _(two):
+        for chunk in (2 * two, 2 * two + 1):
+            start = start_of(chunk)
+            place = pl.multiple_of(jnp.where(chunk < behind, 0, 128), 128)
+            for p in range(group):
+                part = nt(queries[p], keys[p, pl.ds(start, CHUNK), :])
+                extra = bias[p, :, pl.ds(place, 128)]
+                left, right = part[:, :128] + extra, part[:, 128:] + extra
+                scores[p, :, pl.ds(start, 128)] = left
+                scores[p, :, pl.ds(start + 128, 128)] = right
+                peak[p] = jnp.maximum(peak[p], jnp.maximum(left, right))
 
     tops = [jnp.max(peak[p], axis=1, keepdims=True) for p in range(group)]
     for p in range(group):
@@ -160,16 +174,19 @@
         probs_ref[p, 0, :, pl.ds(near, NEAR)] = probs
         total[p] = nn(probs, values[p, pl.ds(near, NEAR), :])
 
-    @pl.loop(0, far)
-    def _(chunk):
-        start = start_of(chunk)
+    @pl.loop(0, (far + 1) // 2)
+    def _(two):
+        starts = [start_of(2 * two), start_of(2 * two + 1)]
         for p in range(group):
             top = peak[p]
-            left = jnp.exp2(scores[p, :, pl.ds(start, 128)] - top).astype(bf16)
-            right = jnp.exp2(scores[p, :, pl.ds(start + 128, 128)] - top).astype(bf16)
-            probs = jnp.concatenate([left, right], 1)
-            probs_ref[p, 0, :, pl.ds(start, CHUNK)] = probs
-            total[p] += nn(probs, values[p, pl.ds(start, CHUNK), :])
+            parts = []
+            for start in starts:
+                left = jnp.exp2(scores[p, :, pl.ds(start, 128)] - top).astype(bf16)
+                right = jnp.exp2(scores[p, :, pl.ds(start + 128, 128)] - top).astype(bf16)
+                probs = jnp.concatenate([left, right], 1)
+                probs_ref[p, 0, :, pl.ds(start, CHUNK)] = probs
+                parts.append(nn(probs, values[p, pl.ds(start, CHUNK), :]))
+            total[p] += parts[0] + parts[1]
 
     for p in range(group):
         lanes = lanes_of(p)
@@ -259,14 +276,17 @@
                 bucket[p, rows, 128 * t : 128 * t + 128] = near_parts[t].astype(bf16)
     behind = behind_ref[step]
 
-    @pl.loop(0, behind + ahead_ref[step])
-    def _(chunk):
-        start = pl.multiple_of(jnp.where(chunk < behind, near - 256 * (chunk + 1), near + NEAR + 256 * (chunk - behind)), 128)
-        side = jnp.where(chunk < behind, 0, 1)
-        for p in range(group):
-            score, part = visit(p, start, CHUNK)
-            query_total[p] += part
-            far_total[p, side] += score[:, :128] + score[:, 128:]
+    far = behind + ahead_ref[step]
+
+    @pl.loop(0, (far + 1) // 2)
+    def _(two):
+        for chunk in (2 * two, 2 * two + 1):
+            start = far_start(chunk, behind, far, near)
+            side = jnp.where(chunk < behind, 0, 1)
+            for p in range(group):
+                score, part = visit(p, start, CHUNK)
+                query_total[p] += part
+                far_total[p, side] += score[:, :128] + score[:, 128:]
 
     for p in range(group):
         lanes = lanes_of(p)
@@ -300,24 +320,16 @@
 
 def ranges(segments):
     length = segments.shape[1]
-    own = segments[0]
-    blocks = length // (2 * BQ)
-    start = 2 * BQ * jnp.arange(blocks, dtype=jnp.int32)
-    first = jnp.sum((own[None, :] < own[start][:, None]).astype(jnp.int32), axis=1)
-    last = jnp.sum((own[None, :] <= own[start + 2 * BQ - 2][:, None]).astype(jnp.int32), axis=1)
+    own = segments[0][None, :]
+    place = jnp.arange(length, dtype=jnp.int32)[None, :]
+    start = 2 * BQ * jnp.arange(length // (2 * BQ), dtype=jnp.int32)
+    count = lambda marks: jnp.sum(marks.astype(jnp.int32), axis=1)
+    at = lambda where: jnp.sum(jnp.where(place == where[:, None], own, 0), axis=1)
+    first = count(own < at(start)[:, None])
+    last = count(own <= at(start + 2 * BQ - 2)[:, None])
     behind = jnp.maximum(start - 256 - first + CHUNK - 1, 0) // CHUNK
     ahead = jnp.maximum(last - (start - 256 + NEAR) + CHUNK - 1, 0) // CHUNK
     return behind, ahead
-
-
-def documents(segments):
-    length = segments.shape[1]
-    lane = jnp.arange(128, dtype=jnp.int32)[None, :]
-    same = segments[0][:, None] == lane
-    query = same[0::2].astype(bf16)
-    away = jnp.where((lane < 8) & ~same, -BIG, 0.0).astype(bf16)
-    pad = jnp.broadcast_to(jnp.where(lane < 8, -BIG, 0.0).astype(bf16), (256, 128))
-    return query, jnp.concatenate([pad, away, pad], 0)
 
 
 GROUP = 3
@@ -355,14 +367,14 @@
             scratch_shapes=[
                 pltpu.VMEM((group, padded, 256), bf16),
                 pltpu.VMEM((group, padded, 256), bf16),
-                pltpu.VMEM((group, 256, 256), bf16),
+                pltpu.VMEM((group, 768, 256), bf16),
                 pltpu.VMEM((group, 2 * BQ, 256), f32),
                 pltpu.VMEM((group, 2 * BQ, padded), f32),
                 pltpu.VMEM((group, 2 * BQ, 128), f32),
                 pltpu.VMEM((group, 2 * BQ, 256), f32),
             ],
         ),
-        compiler_params=pltpu.CompilerParams(dimension_semantics=("arbitrary", "arbitrary"), vmem_limit_bytes=48 << 20),
+        compiler_params=pltpu.CompilerParams(dimension_semantics=("arbitrary", "arbitrary"), vmem_limit_bytes=62 << 20),
         cost_estimate=pl.CostEstimate(flops=40 * 10**9, bytes_accessed=70 * 10**6, transcendentals=10**7),
     )(behind, ahead, content, position, ordering, keys, values, relative, order, away, document,
       jnp.asarray(near_index()))
@@ -410,7 +422,7 @@
                 pltpu.VMEM((8, wide), f32),
             ],
         ),
-        compiler_params=pltpu.CompilerParams(dimension_semantics=("arbitrary", "arbitrary"), vmem_limit_bytes=48 << 20),
+        compiler_params=pltpu.CompilerParams(dimension_semantics=("arbitrary", "arbitrary"), vmem_limit_bytes=62 << 20),
         cost_estimate=pl.CostEstimate(flops=80 * 10**9, bytes_accessed=70 * 10**6, transcendentals=0),
     )(behind, ahead, probs, grad, mixed, inverse, content, position, ordering, keys, values, relative, order,
       jnp.asarray(turn, jnp.int32), jnp.asarray(bucket_onehot(), bf16))
@@ -831,51 +843,60 @@
 
 
 FIRST_VECTOR = 34
-
-
-def mixing(mix):
-    rows = mix.shape[0]
-    place = lax.broadcasted_iota(jnp.int32, (rows, 2 * rows), 1) - 2 * lax.broadcasted_iota(jnp.int32, (rows, 2 * rows), 0)
-    own = jnp.broadcast_to(mix[:, :1], place.shape)
-    next_one = jnp.broadcast_to(mix[:, 64:65], place.shape)
-    return jnp.where(place == 0, own, jnp.where(place == 1, next_one, 0.0)).astype(bf16)
+VMEM_ALL = 62 << 20
+
+
+def place_of(rows):
+    return lax.broadcasted_iota(jnp.int32, (rows, 2 * rows), 1) - 2 * lax.broadcasted_iota(jnp.int32, (rows, 2 * rows), 0)
+
+
+def mixing(own, rest):
+    place = place_of(own.shape[0])
+    return jnp.where(place == 0, own, jnp.where(place == 1, rest, 0.0)).astype(bf16)
 
 
 def project_kernel(
-    tokens_ref, mix_ref, weight_ref, small_ref,
-    pooled_ref, content_ref, position_ref, ordering_ref, key_ref, value_ref,
+    tokens_ref, hot_ref, weight_ref, small_ref,
+    pooled_ref, content_ref, position_ref, ordering_ref, key_ref, value_ref, document_ref, mix_ref,
 ):
     width = tokens_ref.shape[1]
+    rows = pooled_ref.shape[0]
     tokens = tokens_ref[...]
-    pooled = nn(mixing(mix_ref[...]), tokens)
+    place = place_of(rows)
+    first, second = (nn(jnp.where(place == j, 1.0, 0.0).astype(bf16), hot_ref[...]) for j in range(2))
+    document_ref[...] = first.astype(bf16)
+    own = 1.0 / (1.0 + jnp.sum(first * second, axis=1, keepdims=True))
+    mix_ref[...] = jnp.broadcast_to(own, mix_ref.shape)
+    pooled = nn(mixing(own, 1.0 - own), tokens)
     pooled_ref[...] = pooled
     key_ref[...] = nn(tokens, weight_ref[:, width : 2 * width]).astype(bf16)
     value_ref[...] = nn(tokens, weight_ref[:, 2 * width :]).astype(bf16)
     queries = nn(pooled.astype(bf16), weight_ref[:, :width])
-    bias = small_ref[FIRST_VECTOR : FIRST_VECTOR + 3, :].astype(f32)
+    bias = small_ref[2:5, :].astype(f32)
     content_ref[...] = ((queries + bias[0:1]) * (0.125 * LOG2E)).astype(bf16)
     position_ref[...] = (queries + bias[1:2]).astype(bf16)
     ordering_ref[...] = (queries + bias[2:3]).astype(bf16)
 
 
-def project(tokens, mix, weight, small):
+def project(tokens, hot, weight, small):
     length, width = tokens.shape
     block = 256
     steps = length // block
-    whole = pl.BlockSpec((block, width), lambda i: (i, 0))
-    half = pl.BlockSpec((block // 2, width), lambda i: (i, 0))
+    whole = lambda n: pl.BlockSpec((block, n), lambda i: (i, 0))
+    half = lambda n: pl.BlockSpec((block // 2, n), lambda i: (i, 0))
     rows = jax.ShapeDtypeStruct((length // 2, width), bf16)
     full = jax.ShapeDtypeStruct((length, width), bf16)
+    narrow = lambda kind: jax.ShapeDtypeStruct((length // 2, 128), kind)
     return pl.pallas_call(
         project_kernel,
         name="project",
         grid=(steps,),
-        out_shape=(jax.ShapeDtypeStruct((length // 2, width), f32), rows, rows, rows, full, full),
-        in_specs=[whole, pl.BlockSpec((block // 2, 128), lambda i: (i, 0)), fixed(*weight.shape), fixed(*small.shape)],
-        out_specs=[half, half, half, half, whole, whole],
-        compiler_params=pltpu.CompilerParams(vmem_limit_bytes=40 << 20),
+        out_shape=(jax.ShapeDtypeStruct((length // 2, width), f32), rows, rows, rows, full, full, narrow(bf16), narrow(f32)),
+        in_specs=[whole(width), whole(128), fixed(*weight.shape), fixed(*small.shape)],
+        out_specs=[half(width)] * 4 + [whole(width)] * 2 + [half(128)] * 2,
+        compiler_params=pltpu.CompilerParams(vmem_limit_bytes=VMEM_ALL),
         cost_estimate=pl.CostEstimate(flops=5 * length * width * width, bytes_accessed=10 * length * width, transcendentals=0),
-    )(tokens, mix, weight, small)
+    )(tokens, hot, weight, small)
 
 
 def mean(values):
@@ -916,7 +937,7 @@
         rows = pl.ds(pl.multiple_of(step * size, size), size)
 
         def vector(j):
-            return small_ref[FIRST_VECTOR + j : FIRST_VECTOR + j + 1, :].astype(f32)
+            return small_ref[2 + j : 3 + j, :].astype(f32)
 
         context = context_ref[...]
         context_all[rows, :] = context
@@ -956,12 +977,11 @@
         ):
             sums_ref[j : j + 1, :] += column_sum(term)
 
-    for c, cut in enumerate(chunks):
-
-        @pl.when(step == blocks + c)
-        def _():
-            outer_out[...] = tn(act[:, cut], outer_all[...]).astype(bf16)
-            inner_out[...] = tn(first_all[...], back[:, cut]).astype(bf16)
+    @pl.when((step >= blocks) & (step < blocks + len(chunks)))
+    def _():
+        cut = pl.ds(pl.multiple_of((step - blocks) * width, width), width)
+        outer_out[...] = tn(act[:, cut], outer_all[...]).astype(bf16)
+        inner_out[...] = tn(first_all[...], back[:, cut]).astype(bf16)
 
     @pl.when(step == blocks + len(chunks))
     def _():
@@ -1026,7 +1046,8 @@
     pooled_grad = sum_ref[...] + nt(query_low, weight_ref[:, :width])
     coarse = pooled_grad.astype(bf16)
     fine = (pooled_grad - coarse.astype(f32)).astype(bf16)
-    mix = mixing(mix_ref[...])
+    own = mix_ref[:, :1]
+    mix = mixing(own, 1.0 - own)
     tokens_grad_ref[...] = (
         tn(mix, coarse) + tn(mix, fine)
         + nt(key_low, weight_ref[:, width : 2 * width])
@@ -1054,9 +1075,132 @@
         in_specs=[whole, whole, whole, half, half, half, pl.BlockSpec((block // 2, 128), lambda i: (i, 0)), fixed(*weight.shape)],
         out_specs=[whole, fixed(width, 3 * width)],
         scratch_shapes=[pltpu.VMEM((width, 3 * width), f32)],
-        compiler_params=pltpu.CompilerParams(vmem_limit_bytes=48 << 20),
+        compiler_params=pltpu.CompilerParams(vmem_limit_bytes=VMEM_ALL),
         cost_estimate=pl.CostEstimate(flops=10 * length * width * width, bytes_accessed=16 * length * width, transcendentals=0),
     )(tokens, key_low, value_low, query_low, sum_grad, pooled, mix, weight)
+
+
+def pack_kernel(count, folds, *refs):
+    output_ref, inner_ref, relative_ref, order_ref = refs[:4]
+    vectors, bias_ref = refs[4 : 4 + count], refs[4 + count]
+    wide_ref, small_ref = refs[5 + count :]
+    width = output_ref.shape[1]
+    each = relative_ref.shape[1]
+    wide_ref[:, :width] = output_ref[...]
+    wide_ref[:, width:] = inner_ref[...]
+    small_ref[...] = jnp.zeros(small_ref.shape, bf16)
+    rows = [relative_ref[...].astype(f32), order_ref[...].astype(f32)]
+    rows += [ref[...].astype(f32).reshape(1, each) for ref in vectors]
+    bias = bias_ref[...].astype(f32).reshape(1, folds * each)
+    rows += [bias[:, j * each : (j + 1) * each] for j in range(folds)]
+    small_ref[: FIRST_VECTOR + count + folds, :each] = jnp.concatenate(rows, 0).astype(bf16)
+
+
+def pack(output, inner, relative, order, vectors, bias, folds):
+    rows = -(-(FIRST_VECTOR + len(vectors) + folds) // 16) * 16
+    return pl.pallas_call(
+        functools.partial(pack_kernel, len(vectors), folds),
+        name="pack",
+        out_shape=(
+            jax.ShapeDtypeStruct((output.shape[0], output.shape[1] + inner.shape[1]), bf16),
+            jax.ShapeDtypeStruct((rows, 128), bf16),
+        ),
+        cost_estimate=pl.CostEstimate(flops=0, bytes_accessed=4 * inner.size, transcendentals=0),
+    )(output, inner, relative, order, *vectors, bias)
+
+
+def finish_kernel(count, folds, projection_ref, output_ref, inner_ref, outer_ref, small_ref, *outs):
+    width = output_ref.shape[1]
+    squares, (output_out, inner_out, outer_out, relative_out, order_out) = outs[:3], outs[3:8]
+    vectors, bias_out = outs[8 : 8 + count], outs[8 + count]
+    each = relative_out.shape[1]
+    for j, ref in enumerate(squares):
+        ref[...] = projection_ref[:, j * width : (j + 1) * width]
+    output_out[...] = output_ref[...]
+    inner_out[...] = inner_ref[...]
+    outer_out[...] = outer_ref[...]
+    small = small_ref[...]
+    relative_out[...] = small[:32, :each]
+    order_out[...] = small[32:34, :each]
+    for j, ref in enumerate(vectors):
+        ref[...] = small[FIRST_VECTOR + j, :each]
+    start = FIRST_VECTOR + count
+    bias_out[...] = jnp.concatenate([small[start + j : start + j + 1, :each] for j in range(folds)], 1).reshape(folds * each)
+
+
+def finish(projection, output, inner, outer, small, count, folds):
+    each, width = small.shape[0], output.shape[1]
+    rows = output.shape[0]
+    shape = lambda *s: jax.ShapeDtypeStruct(s, f32)
+    return pl.pallas_call(
+        functools.partial(finish_kernel, count, folds),
+        name="finish",
+        out_shape=(
+            [shape(rows, width)] * 4 + [shape(*inner.shape), shape(*outer.shape), shape(32, rows), shape(2, rows)]
+            + [shape(rows)] * count + [shape(folds * rows)]
+        ),
+        cost_estimate=pl.CostEstimate(flops=0, bytes_accessed=8 * inner.size, transcendentals=0),
+    )(projection, output, inner, outer, small)
+
+
+def unpack_kernel(shards, folds, start, small_ref, segment_ref, relative_out, order_out, vectors_out, bias_out, hot_out, away_out):
+    each = relative_out.shape[1] // shards
+    length = segment_ref.shape[1]
+    own = [small_ref[s].astype(f32) for s in range(shards)]
+    whole = jnp.concatenate([piece[:start, :each] for piece in own], 1).astype(bf16)
+    relative_out[...] = whole[:32]
+    order_out[...] = whole[32:34]
+    vectors_out[: start - 32, :] = whole[32:]
+    bias_out[...] = jnp.concatenate(
+        [piece[start + j : start + j + 1, :each] for piece in own for j in range(folds)], 1
+    ).astype(bf16)
+    document = lax.broadcasted_iota(jnp.int32, (128, length), 0)
+    same = jnp.where(segment_ref[...] == document, 1.0, 0.0).T
+    counted = lax.broadcasted_iota(jnp.int32, same.shape, 1) < 8
+    hot_out[...] = same.astype(bf16)
+    away_out[256 : 256 + length, :] = jnp.where(counted, -BIG * (1.0 - same), 0.0).astype(bf16)
+    pad = jnp.where(counted[:256], -BIG, 0.0).astype(bf16)
+    away_out[:256, :] = pad
+    away_out[256 + length :, :] = pad
+
+
+def unpack(small, segments, width, count, folds):
+    shards = small.shape[0]
+    length = segments.shape[1]
+    start = FIRST_VECTOR + count
+    shape = lambda *s: jax.ShapeDtypeStruct(s, bf16)
+    return pl.pallas_call(
+        functools.partial(unpack_kernel, shards, folds, start),
+        name="unpack",
+        out_shape=(shape(32, width), shape(2, width), shape(16, width), shape(1, folds * width), shape(length, 128), shape(length + 512, 128)),
+        compiler_params=pltpu.CompilerParams(vmem_limit_bytes=VMEM_ALL),
+        cost_estimate=pl.CostEstimate(flops=0, bytes_accessed=1 << 20, transcendentals=0),
+    )(small, segments)
+
+
+def collect_kernel(folds, relative_ref, order_ref, bias_ref, sums_ref, inner_ref, out_ref):
+    shards, rows, _ = out_ref.shape
+    width = relative_ref.shape[1]
+    each = width // shards
+    whole = jnp.concatenate([relative_ref[...], order_ref[:2], bias_ref[:3], sums_ref[:5]], 0)
+    inner = inner_ref[0:1, :]
+    out_ref[...] = jnp.zeros(out_ref.shape, bf16)
+    for s in range(shards):
+        cut = slice(s * each, s * each + each)
+        own = [inner[:, (s * folds + j) * each : (s * folds + j + 1) * each] for j in range(folds)]
+        piece = jnp.concatenate([whole[:, cut], *own], 0)
+        out_ref[s, : piece.shape[0], :each] = piece.astype(bf16)
+
+
+def collect(relative, order, bias, sums, inner, shards, count, folds):
+    rows = -(-(FIRST_VECTOR + count + folds) // 16) * 16
+    return pl.pallas_call(
+        functools.partial(collect_kernel, folds),
+        name="collect",
+        out_shape=jax.ShapeDtypeStruct((shards, rows, 128), bf16),
+        compiler_params=pltpu.CompilerParams(vmem_limit_bytes=VMEM_ALL),
+        cost_estimate=pl.CostEstimate(flops=0, bytes_accessed=1 << 19, transcendentals=0),
+    )(relative, order, bias, sums, inner)
 
 
 def body(
@@ -1088,26 +1232,15 @@
     each = width // shards
     folds = hidden // width
     vectors = (content_bias, position_bias, order_bias, first_gain, first_shift, outer_bias, second_gain, second_shift)
-    small = jnp.concatenate(
-        [relative_table, order_table] + [v[None, :] for v in vectors] + [inner_bias.reshape(folds, each)], 0
-    )
-    small_rows = small.shape[0]
-    spare = -small_rows % 16
-    small = jnp.pad(small, ((0, spare), (0, 128 - each)))
+    wide_own, small = pack(output_weight, inner_weight, relative_table, order_table, vectors, inner_bias, folds)
     projections, small_all = gather(mesh, [jnp.concatenate([query_weight, key_weight, value_weight], 1), small], 0)
     projections = projections.reshape(width, 3 * width)
-    small_all = small_all[:, :, :each].transpose(1, 0, 2).reshape(-1, width)
-    weight_relative, weight_order = small_all[:32], small_all[32:34]
-    bias_inner = small_all[42 : 42 + folds].reshape(folds, shards, each).transpose(1, 0, 2).reshape(1, hidden)
-    wide = lax.all_gather(jnp.concatenate([output_weight, inner_weight], 1), "shard", axis=0, tiled=True)
+    weight_relative, weight_order, small_all, bias_inner, hot, away = unpack(small_all, segment_ids, width, len(vectors), folds)
+    wide = lax.all_gather(wide_own, "shard", axis=0, tiled=True)
     weight_outer = lax.all_gather(outer_weight, "shard", axis=0, tiled=True)
 
-    joined = (segment_ids[0, 0::2] == segment_ids[0, 1::2])[:, None]
-    own = jnp.where(joined, 0.5, 1.0)
-    mix = jnp.where(jnp.arange(128)[None, :] < 64, own, 1.0 - own)
-    pooled, content, position, ordering, keys, values = project(tokens, mix, projections, small_all)
     behind, ahead = ranges(segment_ids)
-    document, away = documents(segment_ids)
+    pooled, content, position, ordering, keys, values, document, mix = project(tokens, hot, projections, small_all)
     probs, context, mixed, inverse = attend(
         behind, ahead, content, position, ordering, keys, values, weight_relative, weight_order, away, document
     )
@@ -1119,13 +1252,7 @@
         keys, values, weight_relative, weight_order,
     )
     tokens_grad, projection_grad = tail(tokens, key_low, value_low, query_low, sum_grad, pooled, mix, projections)
-    small_grad = jnp.concatenate(
-        [relative_grad, order_grad[:2], bias_sums[:3], sums[:5],
-         inner_sums[0].reshape(shards, folds, each).transpose(1, 0, 2).reshape(folds, width)],
-        0,
-    )
-    small_grad = small_grad.reshape(small_rows, shards, each).transpose(1, 0, 2)
-    small_grad = jnp.pad(small_grad, ((0, 0), (0, spare), (0, 128 - each))).astype(bf16)
+    small_grad = collect(relative_grad, order_grad, bias_sums, sums, inner_sums, shards, len(vectors), folds)
     outer_part = lax.psum_scatter(outer_grad, "shard", scatter_dimension=0, tiled=True)
     inner_sum, output_sum, projection_sum, small_sum, outer_sum = scatter(
         mesh,
@@ -1139,20 +1266,12 @@
         [outer_part],
         1,
     )
-    small_sum = small_sum[:, :each]
-    own = [small_sum[34 + j] for j in range(8)]
+    parts = finish(projection_sum, output_sum, inner_sum, outer_sum, small_sum, len(vectors), folds)
+    squares, (inner_sum, outer_sum, relative_sum, order_sum) = parts[:4], parts[4:8]
+    own, bias_sum = parts[8:-1], parts[-1]
     return (
-        layer_out,
-        tokens_grad,
-        *[projection_sum[:, j * width : (j + 1) * width] for j in range(3)],
-        output_sum,
-        small_sum[:32],
-        small_sum[32:34],
-        *own[:5],
-        inner_sum,
-        small_sum[42 : 42 + folds].reshape(folds * each),
-        outer_sum,
-        *own[5:],
+        layer_out, tokens_grad, *squares, relative_sum, order_sum, *own[:5],
+        inner_sum, bias_sum, outer_sum, *own[5:],
     )
 
 

time: 456 us -> 412 us (0.904); the launches traced: 447 us -> 414 us
  local copies, waits for them, and re-layouts: 38.5 us -> 0 us
  Pallas kernels: 389 us -> 395 us
    unnamed x37 -> x0, local copies, waits for them, and re-layouts: 19.1 us -> none
    pallas_call x1, Pallas kernels: 60.2 us -> 50.9 us  [middle(): pl.pallas_call(functools.partial(middle_kernel, blocks), name='middle', g...]
    slice x17 -> x0, local copies, waits for them, and re-layouts: 9.02 us -> none  [the longest x2 1.88 us: body(): joined = (segment_ids[0, 0::2] == segment_ids[0, 1::2])[:, None]]
    pallas_call x0 -> x4, Pallas kernels: none -> 8.86 us  [the longest x1 2.73 us: finish(): pl.pallas_call(functools.partial(finish_kernel, count, folds), name='fini...]
    pallas_call x1, Pallas kernels: 72.8 us -> 80.2 us  [attend_back(): pl.pallas_call(functools.partial(backward_kernel, group), name='attend_ba...]
  transfers between devices with their start and end apart: 3 -> 3, of which waited for: 0 -> 0; matrix products, arithmetic and copies ran while one was open for 4% -> 1% of each run, Pallas kernels for 50% -> 57%
where the time goes in v3:
time: 412 us; the launch traced here: 414 us
  Pallas kernels  395 us (96%)
  between operations  13.8 us (3%)
  other arithmetic  4.57 us (1%)
    pallas_call x1, Pallas kernels, scatter(): pl.pallas_call(functools.partial(scatter_kernel, replicas, shards, count,...  106 us
    pallas_call x1, Pallas kernels, attend_back(): pl.pallas_call(functools.partial(backward_kernel, group), name='attend_ba...  80.2 us
    pallas_call x1, Pallas kernels, attend(): pl.pallas_call(functools.partial(forward_kernel, group), name='attend', o...  62.8 us
    pallas_call x1, Pallas kernels, middle(): pl.pallas_call(functools.partial(middle_kernel, blocks), name='middle', g...  50.9 us
    pallas_call x1, Pallas kernels, gather(): pl.pallas_call(functools.partial(gather_kernel, replicas, shards, count),...  47.2 us
    pallas_call x1, Pallas kernels, tail(): pl.pallas_call(tail_kernel, name='tail', grid=(length // block,), out_sha...  26.1 us
    pallas_call x1, Pallas kernels, project(): pl.pallas_call(project_kernel, name='project', grid=(steps,), out_shape=(...  13.4 us
  transfers between devices with their start and end apart: 3, of which 0 were waited for; matrix products, arithmetic and copies ran while one was open for 1% of the time, Pallas kernels for 57%

profile of v3, /device:TPU:0, one launch (start us, length us, event | category | flops | bytes accessed | tf_op | source)
XLA Modules:
  0.0 414.3 jit_solution(13857132292033558228)
XLA Ops:
  7.2 0.0 all-gather.5.cloned.1.call-start
  7.2 0.7 all-gather.5.cloned.1.call-update
  7.9 0.0 all-gather.3.cloned.1.call-start
  8.0 1.9 pack.1
  9.8 0.0 all-gather.3.cloned.1.call-update
  9.9 0.0 reduce-scatter.2.cloned.1.call-start
  9.9 1.7 pad_maximum_fusion.refs_0_
  11.6 47.2 %gather.1 = (bf16[16,48,2304]{2,1,0:T(8,128)(2,1)}, bf16[16,48,128]{2,1,0:T(8,128)(2,1)}) custom-call(bf16[48,2304]{1,0:T(8,128)(2,1)} %pad_maximum_fusion.refs_0_, bf16[48,128]{1,0:T(8,128)(2,1)} %get-tuple-element.79.refs_1_), custom_call_target="tpu_custom_call" | custom-call | bytes 14942208 | tf_op jit(solution)/shard_map/gather/pallas_call | solution.py:638
  58.7 2.3 unpack.1
  61.1 0.9 select_reduce_fusion
  62.0 0.9 convert_reduce_fusion
  62.9 0.5 and_select_fusion.ahead_ref
  63.5 0.5 and_select_fusion.1.behind_ref
  64.0 13.4 %project.1 = (f32[1024,768]{1,0:T(8,128)}, bf16[1024,768]{1,0:T(8,128)(2,1)}, bf16[1024,768]{1,0:T(8,128)(2,1)}, bf16[1024,768]{1,0:T(8,128)(2,1)}, bf16[2048,76...) custom-call(bf16[2048,768]{1,0:T(8,128)(2,1)} %tokens_ref.3, ...), custom_call_target="tpu_custom_call" | custom-call | flops 6039797760 | bytes 15728640 | tf_op jit(solution)/shard_map/project/pallas_call | solution.py:890
  77.4 62.8 %attend.1 = (bf16[6,8,256,2560]{3,2,1,0:T(8,128)(2,1)}, bf16[1024,768]{1,0:T(8,128)(2,1)}, f32[1024,768]{1,0:T(8,128)}, f32[1024,768]{1,0:T(8,128)}) custom-call(s32[8]{0:T(128)} %and_select_fusion.1.behind_ref, s32[8]{0:T(128)} %and_select_fusion.ahead_ref, bf16[1024,768]{1,0:T(8,128)(2,1)} %get-tuple-element.84.content_ref, ...), custom_call_target="tpu_custom_call" | custom-call | flops 40000000000 | bytes 70000000 | tf_op jit(solution)/shard_map/attend/pallas_call | solution.py:346
  140.2 0.0 all-gather.5.cloned.1.call-done.outer_ref
  140.2 0.0 all-gather.3.cloned.1.call-done.wide_ref
  140.2 50.9 %middle.1 = (bf16[1024,768]{1,0:T(8,128)(2,1)}, f32[1024,768]{1,0:T(8,128)}, bf16[1024,768]{1,0:T(8,128)(2,1)}, f32[8,768]{1,0:T(8,128)}, f32[8,3072]{1,0:T(8,12...) custom-call(bf16[1024,768]{1,0:T(8,128)(2,1)} %get-tuple-element.93.context_ref, ...), custom_call_target="tpu_custom_call" | custom-call | flops 43486543872 | bytes 31457280 | tf_op jit(solution)/shard_map/middle/pallas_call | solution.py:1000
  191.1 0.0 reduce-scatter.2.cloned.1.call-update
  191.1 80.2 %attend_back.1 = (bf16[1024,768]{1,0:T(8,128)(2,1)}, bf16[2048,768]{1,0:T(8,128)(2,1)}, bf16[2048,768]{1,0:T(8,128)(2,1)}, f32[32,768]{1,0:T(8,128)}, f32[8,768]{1,0:T(8,128)}, /*index=5*/f32[8,768]{1,0:T(8,128)}) custom-call(s32[8]{0:T(128)} %and_select_fusion.1.behind_ref, s32[8]{0:T(128)} %and_select_fusion.ahead_ref, ...), custom_call_target="tpu_custom_call" | custom-call | flops 80000000000 | bytes 70000000 | tf_op jit(solution)/shard_map/attend_back/pallas_call | solution.py:393
  271.3 1.9 collect.1
  273.2 26.1 %tail.1 = (f32[2048,768]{1,0:T(8,128)}, bf16[768,2304]{1,0:T(8,128)(2,1)}) custom-call(bf16[2048,768]{1,0:T(8,128)(2,1)} %tokens_ref.3, bf16[2048,768]{1,0:T(8,128)(2,1)} %get-tuple-element.102.key_ref, bf16[2048,768]{1,0:T(8,128)(2,1)} %get-tuple-element.103.value_ref, bf16[1024,768]{1,0:T(8,128)(2,1)} %get-tuple-element.104.query_ref, ...), custom_call_target="tpu_custom_call" | custom-call | flops 12079595520 | bytes 25165824 | tf_op jit(solution)/shard_map/tail/pallas_call | solution.py:1070
  299.3 0.0 reduce-scatter.2.cloned.1.call-done.refs_4_
  299.3 105.6 %scatter.1 = (f32[48,3072]{1,0:T(8,128)}, f32[48,768]{1,0:T(8,128)}, f32[48,2304]{1,0:T(8,128)}, f32[48,128]{1,0:T(8,128)}, f32[192,768]{1,0:T(8,128)}) custom-call(bf16[4,2,2,48,3072]{4,3,2,1,0:T(8,128)(2,1)} %bitcast.6, bf16[4,2,2,48,768]{4,3,2,1,0:T(8,128)(2,1)} %bitcast.8, bf16[4,2,2,48,2304]{4,3,2,1,0:T(8,128)(2,1)} %bitcast.7, ...), custom_call_target="tpu_custom_call" | custom-call | bytes 38535168 | tf_op jit(solution)/shard_map/scatter/pallas_call | solution.py:827
  405.0 2.7 finish.1
  (1 shorter events, 0.0 us)
Async XLA Ops:
  7.2 133.0 %all-gather.5.cloned.1.call-start = ((), (), s32[]{:S(2)}) async-start(), calls=%async_computation.2 | async-start | bytes 5013504 | tf_op jit(solution)/shard_map/all_gather | solution.py:1240
  7.9 132.3 %all-gather.3.cloned.1.call-start = ((), (), s32[]{:S(2)}) async-start(), calls=%async_computation.1 | async-start | bytes 6266880 | tf_op jit(solution)/shard_map/all_gather | solution.py:1239
  9.9 289.5 %reduce-scatter.2.cloned.1.call-start = ((), (), s32[]{:S(2)}) async-start(), calls=%async_computation.3 | async-start | bytes 5013504 | tf_op jit(solution)/shard_map/reduce_scatter | solution.py:1256
Sparse Core Ops, SparseCore 0:
  10.3 59.5 all-gather.4
  72.2 58.3 all-gather.2
  191.2 83.0 reduce-scatter.1

commit v4 on v3

--- a/solution.py
+++ b/solution.py
@@ -148,8 +148,8 @@
                     scores[p, rows, pl.ds(near + 128 * tile, 128)] = part
                     best = part if best is None else jnp.maximum(best, part)
                 peak[p, rows, :] = best
-    behind = behind_ref[step]
-    far = behind + ahead_ref[step]
+    behind = behind_ref[step, 0]
+    far = behind + ahead_ref[step, 0]
 
     def start_of(chunk):
         return far_start(chunk, behind, far, near)
@@ -274,9 +274,9 @@
                 far_total[p, 1, rows] = jnp.where(first, own[4], zero)
             for t in range(3):
                 bucket[p, rows, 128 * t : 128 * t + 128] = near_parts[t].astype(bf16)
-    behind = behind_ref[step]
-
-    far = behind + ahead_ref[step]
+    behind = behind_ref[step, 0]
+
+    far = behind + ahead_ref[step, 0]
 
     @pl.loop(0, (far + 1) // 2)
     def _(two):
@@ -316,20 +316,6 @@
 
 def fixed(*shape):
     return pl.BlockSpec(shape, lambda *_: (0,) * len(shape), pipeline_mode=pl.Buffered(1))
-
-
-def ranges(segments):
-    length = segments.shape[1]
-    own = segments[0][None, :]
-    place = jnp.arange(length, dtype=jnp.int32)[None, :]
-    start = 2 * BQ * jnp.arange(length // (2 * BQ), dtype=jnp.int32)
-    count = lambda marks: jnp.sum(marks.astype(jnp.int32), axis=1)
-    at = lambda where: jnp.sum(jnp.where(place == where[:, None], own, 0), axis=1)
-    first = count(own < at(start)[:, None])
-    last = count(own <= at(start + 2 * BQ - 2)[:, None])
-    behind = jnp.maximum(start - 256 - first + CHUNK - 1, 0) // CHUNK
-    ahead = jnp.maximum(last - (start - 256 + NEAR) + CHUNK - 1, 0) // CHUNK
-    return behind, ahead
 
 
 GROUP = 3
@@ -652,14 +638,26 @@
     )(*arrays)
 
 
-def scatter_kernel(replicas, shards, count, chunks, extra, *refs):
+WORK_INPUTS = ("key_low", "value_low", "query_low", "sum_grad", "mix", "weight")
+
+
+def scatter_kernel(replicas, shards, count, chunks, extra, work, *refs):
     here = Place(replicas, shards)
     take = lambda number: [refs_left.pop(0) for _ in range(number)]
     refs_left = list(refs)
-    sources, extras, outs, extra_outs = take(count), take(extra), take(count), take(extra)
-    core_bufs, rep_bufs, cross_bufs, line_bufs, last_bufs = (take(count) for _ in range(5))
+    sources, extras, work_in = take(count), take(extra), take(len(WORK_INPUTS))
+    outs, extra_outs, (tokens_grad,) = take(count), take(extra), take(1)
+    own_bufs, core_bufs, rep_bufs, cross_bufs, line_bufs, last_bufs = (take(count) for _ in range(6))
     extra_bufs = take(extra)
+    work_bufs, (block_buf, own_sems, work_sems, block_sems) = take(len(WORK_INPUTS)), take(4)
     (core_send, core_recv, rep_send, rep_recv, cross_send, cross_recv, line_send, line_recv, last_send, last_recv) = refs_left
+    local = []
+    for j, (k, low, size) in enumerate(chunks):
+        for column in range(here.across):
+            cut = pl.ds(low, size)
+            local.append(pltpu.make_async_copy(
+                sources[k].at[:, column, here.core, :, cut], own_bufs[k].at[column, :, :, cut], own_sems.at[j, column]
+            ))
     here.meet()
     pending = []
 
@@ -699,7 +697,12 @@
     def mixed(j, column):
         k = chunks[j][0]
         mine = core_bufs[k].at[column, :, :, columns(j)]
-        own = sources[k].at[:, column, here.core, :, columns(j)]
+        own = own_bufs[k].at[column, :, :, columns(j)]
+        _, low, size = chunks[j]
+        cut = pl.ds(low, size)
+        pltpu.make_async_copy(
+            sources[k].at[:, column, here.core, :, cut], own_bufs[k].at[column, :, :, cut], own_sems.at[j, column]
+        ).wait()
         if here.cores > 1:
             arrived(mine, core_recv.at[j, column])
             add(mine, own)
@@ -783,6 +786,25 @@
                 column = here.other_column(step)
                 send(sources[k].at[:, column, 1 - here.core, :, columns(j)], core_bufs[k].at[column, :, :, columns(j)],
                      core_send.at[j, column], core_recv.at[j, column], here.device(core=1 - here.core))
+    for copy in local:
+        copy.start()
+    loads = [pltpu.make_async_copy(ref, buf, work_sems.at[i]) for i, (ref, buf) in enumerate(zip(work_in, work_bufs))]
+    for copy in loads:
+        copy.start()
+    stores = []
+
+    def block(b):
+        if b == 0:
+            for copy in loads:
+                copy.wait()
+        if b >= 2:
+            stores[b - 2].wait()
+        block_buf[b % 2] = work(b, *work_bufs)
+        size = block_buf.shape[1]
+        stores.append(pltpu.make_async_copy(block_buf.at[b % 2], tokens_grad.at[pl.ds(b * size, size)], block_sems.at[b % 2]))
+        stores[b].start()
+
+    blocks = tokens_grad.shape[0] // block_buf.shape[1]
     stages = [stage_rep, stage_cross]
     stages += [functools.partial(stage_line, distance) for distance in range(here.line - 1, 0, -1)]
     stages += [stage_last, stage_finish]
@@ -796,13 +818,19 @@
                 for hop in hops:
                     send(extras[e], extra_bufs[e].at[here.replica], last_send.at[total + e, hop],
                          last_recv.at[total + e, here.replica], here.device(replica=here.other_replica(hop)))
+        elif time <= blocks:
+            block(time - 1)
+    for b in range(min(blocks, total + len(stages) - 2), blocks):
+        block(b)
+    for b in range(max(blocks - 2, 0), blocks):
+        stores[b].wait()
     for e in range(extra):
         finish(extras[e], extra_bufs[e], extra_outs[e], last_recv.at[total + e], pl.ds(0, extras[e].shape[1]))
     for condition, wait in pending:
         when(condition, wait)
 
 
-def scatter(mesh, arrays, widths, extras, collective_id):
+def scatter(mesh, arrays, widths, extras, inputs, work, collective_id):
     replicas, shards = mesh.shape["rep"], mesh.shape["shard"]
     count, extra = len(arrays), len(extras)
     dma = pltpu.SemaphoreType.DMA
@@ -816,20 +844,30 @@
     cuts = [(shapes[k][0], shapes[k][1] // parts_of(min(width, shapes[k][1]), replicas)) for k, width in enumerate(widths)]
     moved = sum(a.size * 2 for a in arrays)
     number = len(chunks)
+    rows = inputs[0].shape[0]
+    size = min(rows, 256)
+    anywhere = pl.BlockSpec(memory_space=pl.ANY)
     buffers = (
         [pltpu.VMEM((across, line) + s, bf16) for s in shapes]
+        + [pltpu.VMEM((across, line) + s, bf16) for s in shapes]
         + [pltpu.VMEM((replicas - 1, across - 1, line) + s, bf16) for s in cuts]
         + [pltpu.VMEM((across - 1, line) + s, bf16) for s in cuts]
         + [pltpu.VMEM((2, line) + s, bf16) for s in shapes]
         + [pltpu.VMEM((replicas,) + s, bf16) for s in shapes]
         + [pltpu.VMEM((replicas,) + e.shape, bf16) for e in extras]
+        + [pltpu.VMEM(i.shape, i.dtype) for i in inputs]
+        + [pltpu.VMEM((2, size, inputs[0].shape[1]), f32), dma((number, across)), dma((len(inputs),)), dma((2,))]
     )
     return pl.pallas_call(
-        functools.partial(scatter_kernel, replicas, shards, count, chunks, extra),
+        functools.partial(scatter_kernel, replicas, shards, count, chunks, extra, work),
         name="scatter",
-        out_shape=[jax.ShapeDtypeStruct(s, f32) for s in shapes] + [jax.ShapeDtypeStruct(e.shape, f32) for e in extras],
-        in_specs=[vmem] * (count + extra),
-        out_specs=[vmem] * (count + extra),
+        out_shape=(
+            [jax.ShapeDtypeStruct(s, f32) for s in shapes]
+            + [jax.ShapeDtypeStruct(e.shape, f32) for e in extras]
+            + [jax.ShapeDtypeStruct(inputs[0].shape, f32)]
+        ),
+        in_specs=[anywhere] * count + [vmem] * extra + [anywhere] * len(inputs),
+        out_specs=[vmem] * (count + extra) + [anywhere],
         scratch_shapes=buffers + [
             dma((number, across)), dma((number, across)),
             dma((number, replicas, across)), dma((number, replicas, across)),
@@ -839,7 +877,7 @@
         ],
         compiler_params=pltpu.CompilerParams(collective_id=collective_id, has_side_effects=True, vmem_limit_bytes=62 << 20),
         cost_estimate=pl.CostEstimate(flops=0, bytes_accessed=moved * 4, transcendentals=0),
-    )(*[a.reshape((line, across, cores) + a.shape[1:]) for a in arrays], *extras)
+    )(*[a.reshape((line, across, cores) + a.shape[1:]) for a in arrays], *extras, *inputs)
 
 
 FIRST_VECTOR = 34
@@ -1031,10 +1069,7 @@
     )(context, pooled, cotangent, wide, outer, small, bias)
 
 
-def tail_kernel(
-    tokens_ref, key_ref, value_ref, query_ref, sum_ref, pooled_ref, mix_ref, weight_ref,
-    tokens_grad_ref, weight_grad_ref, total,
-):
+def tail_kernel(tokens_ref, key_ref, value_ref, query_ref, pooled_ref, weight_grad_ref, total):
     step = pl.program_id(0)
     width = tokens_ref.shape[1]
 
@@ -1042,50 +1077,57 @@
     def _():
         total[...] = jnp.zeros(total.shape, f32)
 
-    tokens, query_low, key_low, value_low = tokens_ref[...], query_ref[...], key_ref[...], value_ref[...]
-    pooled_grad = sum_ref[...] + nt(query_low, weight_ref[:, :width])
-    coarse = pooled_grad.astype(bf16)
-    fine = (pooled_grad - coarse.astype(f32)).astype(bf16)
-    own = mix_ref[:, :1]
-    mix = mixing(own, 1.0 - own)
-    tokens_grad_ref[...] = (
-        tn(mix, coarse) + tn(mix, fine)
-        + nt(key_low, weight_ref[:, width : 2 * width])
-        + nt(value_low, weight_ref[:, 2 * width :])
-    )
-    total[:, :width] += tn(pooled_ref[...].astype(bf16), query_low)
-    total[:, width : 2 * width] += tn(tokens, key_low)
-    total[:, 2 * width :] += tn(tokens, value_low)
+    tokens = tokens_ref[...]
+    total[:, :width] += tn(pooled_ref[...].astype(bf16), query_ref[...])
+    total[:, width : 2 * width] += tn(tokens, key_ref[...])
+    total[:, 2 * width :] += tn(tokens, value_ref[...])
 
     @pl.when(step == pl.num_programs(0) - 1)
     def _():
         weight_grad_ref[...] = total[...].astype(bf16)
 
 
-def tail(tokens, key_low, value_low, query_low, sum_grad, pooled, mix, weight):
+def tail(tokens, key_low, value_low, query_low, pooled):
     length, width = tokens.shape
-    block = 256
+    block = 512
     whole = pl.BlockSpec((block, width), lambda i: (i, 0))
     half = pl.BlockSpec((block // 2, width), lambda i: (i, 0))
     return pl.pallas_call(
         tail_kernel,
         name="tail",
         grid=(length // block,),
-        out_shape=(jax.ShapeDtypeStruct((length, width), f32), jax.ShapeDtypeStruct((width, 3 * width), bf16)),
-        in_specs=[whole, whole, whole, half, half, half, pl.BlockSpec((block // 2, 128), lambda i: (i, 0)), fixed(*weight.shape)],
-        out_specs=[whole, fixed(width, 3 * width)],
+        out_shape=jax.ShapeDtypeStruct((width, 3 * width), bf16),
+        in_specs=[whole, whole, whole, half, half],
+        out_specs=fixed(width, 3 * width),
         scratch_shapes=[pltpu.VMEM((width, 3 * width), f32)],
         compiler_params=pltpu.CompilerParams(vmem_limit_bytes=VMEM_ALL),
-        cost_estimate=pl.CostEstimate(flops=10 * length * width * width, bytes_accessed=16 * length * width, transcendentals=0),
-    )(tokens, key_low, value_low, query_low, sum_grad, pooled, mix, weight)
+        cost_estimate=pl.CostEstimate(flops=5 * length * width * width, bytes_accessed=8 * length * width, transcendentals=0),
+    )(tokens, key_low, value_low, query_low, pooled)
+
+
+def tokens_block(block, key_ref, value_ref, query_ref, sum_ref, mix_ref, weight_ref):
+    width = key_ref.shape[1]
+    whole, half = slice(256 * block, 256 * block + 256), slice(128 * block, 128 * block + 128)
+    pooled_grad = sum_ref[half, :] + nt(query_ref[half, :], weight_ref[:, :width])
+    coarse = pooled_grad.astype(bf16)
+    fine = (pooled_grad - coarse.astype(f32)).astype(bf16)
+    own = mix_ref[half, :1]
+    mix = mixing(own, 1.0 - own)
+    return (
+        tn(mix, coarse) + tn(mix, fine)
+        + nt(key_ref[whole, :], weight_ref[:, width : 2 * width])
+        + nt(value_ref[whole, :], weight_ref[:, 2 * width :])
+    )
 
 
 def pack_kernel(count, folds, *refs):
-    output_ref, inner_ref, relative_ref, order_ref = refs[:4]
-    vectors, bias_ref = refs[4 : 4 + count], refs[4 + count]
-    wide_ref, small_ref = refs[5 + count :]
+    squares, (output_ref, inner_ref, relative_ref, order_ref) = refs[:3], refs[3:7]
+    vectors, bias_ref = refs[7 : 7 + count], refs[7 + count]
+    wide_ref, small_ref, projections_ref = refs[8 + count :]
     width = output_ref.shape[1]
     each = relative_ref.shape[1]
+    for j, ref in enumerate(squares):
+        projections_ref[:, j * width : (j + 1) * width] = ref[...]
     wide_ref[:, :width] = output_ref[...]
     wide_ref[:, width:] = inner_ref[...]
     small_ref[...] = jnp.zeros(small_ref.shape, bf16)
@@ -1096,7 +1138,7 @@
     small_ref[: FIRST_VECTOR + count + folds, :each] = jnp.concatenate(rows, 0).astype(bf16)
 
 
-def pack(output, inner, relative, order, vectors, bias, folds):
+def pack(squares, output, inner, relative, order, vectors, bias, folds):
     rows = -(-(FIRST_VECTOR + len(vectors) + folds) // 16) * 16
     return pl.pallas_call(
         functools.partial(pack_kernel, len(vectors), folds),
@@ -1104,9 +1146,10 @@
         out_shape=(
             jax.ShapeDtypeStruct((output.shape[0], output.shape[1] + inner.shape[1]), bf16),
             jax.ShapeDtypeStruct((rows, 128), bf16),
+            jax.ShapeDtypeStruct((output.shape[0], 3 * output.shape[1]), bf16),
         ),
         cost_estimate=pl.CostEstimate(flops=0, bytes_accessed=4 * inner.size, transcendentals=0),
-    )(output, inner, relative, order, *vectors, bias)
+    )(*squares, output, inner, relative, order, *vectors, bias)
 
 
 def finish_kernel(count, folds, projection_ref, output_ref, inner_ref, outer_ref, small_ref, *outs):
@@ -1143,7 +1186,7 @@
     )(projection, output, inner, outer, small)
 
 
-def unpack_kernel(shards, folds, start, small_ref, segment_ref, relative_out, order_out, vectors_out, bias_out, hot_out, away_out):
+def unpack_kernel(shards, folds, start, small_ref, segment_ref, relative_out, order_out, vectors_out, bias_out, hot_out, away_out, behind_out, ahead_out):
     each = relative_out.shape[1] // shards
     length = segment_ref.shape[1]
     own = [small_ref[s].astype(f32) for s in range(shards)]
@@ -1162,6 +1205,17 @@
     pad = jnp.where(counted[:256], -BIG, 0.0).astype(bf16)
     away_out[:256, :] = pad
     away_out[256 + length :, :] = pad
+    blocks = behind_out.shape[0]
+    own_row = jnp.broadcast_to(segment_ref[...], (blocks, length))
+    lane = lax.broadcasted_iota(jnp.int32, (blocks, length), 1)
+    start = 2 * BQ * lax.broadcasted_iota(jnp.int32, (blocks, length), 0)
+    total = lambda values: jnp.sum(values, axis=1, keepdims=True)
+    at = lambda place: total(jnp.where(lane == place, own_row, 0))
+    first = total(jnp.where(own_row < at(start), 1, 0))
+    last = total(jnp.where(own_row <= at(start + 2 * BQ - 2), 1, 0))
+    chunks = lambda rest: lax.shift_right_logical(jnp.maximum(rest + CHUNK - 1, 0), CHUNK.bit_length() - 1)
+    behind_out[...] = chunks(start[:, :128] - 256 - first)
+    ahead_out[...] = chunks(last - (start[:, :128] - 256 + NEAR))
 
 
 def unpack(small, segments, width, count, folds):
@@ -1172,7 +1226,8 @@
     return pl.pallas_call(
         functools.partial(unpack_kernel, shards, folds, start),
         name="unpack",
-        out_shape=(shape(32, width), shape(2, width), shape(16, width), shape(1, folds * width), shape(length, 128), shape(length + 512, 128)),
+        out_shape=(shape(32, width), shape(2, width), shape(16, width), shape(1, folds * width), shape(length, 128), shape(length + 512, 128))
+        + (jax.ShapeDtypeStruct((length // (2 * BQ), 128), jnp.int32),) * 2,
         compiler_params=pltpu.CompilerParams(vmem_limit_bytes=VMEM_ALL),
         cost_estimate=pl.CostEstimate(flops=0, bytes_accessed=1 << 20, transcendentals=0),
     )(small, segments)
@@ -1232,14 +1287,17 @@
     each = width // shards
     folds = hidden // width
     vectors = (content_bias, position_bias, order_bias, first_gain, first_shift, outer_bias, second_gain, second_shift)
-    wide_own, small = pack(output_weight, inner_weight, relative_table, order_table, vectors, inner_bias, folds)
-    projections, small_all = gather(mesh, [jnp.concatenate([query_weight, key_weight, value_weight], 1), small], 0)
+    wide_own, small, projections_own = pack(
+        (query_weight, key_weight, value_weight), output_weight, inner_weight, relative_table, order_table, vectors, inner_bias, folds
+    )
+    projections, small_all = gather(mesh, [projections_own, small], 0)
     projections = projections.reshape(width, 3 * width)
-    weight_relative, weight_order, small_all, bias_inner, hot, away = unpack(small_all, segment_ids, width, len(vectors), folds)
+    weight_relative, weight_order, small_all, bias_inner, hot, away, behind, ahead = unpack(
+        small_all, segment_ids, width, len(vectors), folds
+    )
     wide = lax.all_gather(wide_own, "shard", axis=0, tiled=True)
     weight_outer = lax.all_gather(outer_weight, "shard", axis=0, tiled=True)
 
-    behind, ahead = ranges(segment_ids)
     pooled, content, position, ordering, keys, values, document, mix = project(tokens, hot, projections, small_all)
     probs, context, mixed, inverse = attend(
         behind, ahead, content, position, ordering, keys, values, weight_relative, weight_order, away, document
@@ -1251,10 +1309,10 @@
         behind, ahead, probs, context_grad, mixed, inverse, content, position, ordering,
         keys, values, weight_relative, weight_order,
     )
-    tokens_grad, projection_grad = tail(tokens, key_low, value_low, query_low, sum_grad, pooled, mix, projections)
+    projection_grad = tail(tokens, key_low, value_low, query_low, pooled)
     small_grad = collect(relative_grad, order_grad, bias_sums, sums, inner_sums, shards, len(vectors), folds)
     outer_part = lax.psum_scatter(outer_grad, "shard", scatter_dimension=0, tiled=True)
-    inner_sum, output_sum, projection_sum, small_sum, outer_sum = scatter(
+    inner_sum, output_sum, projection_sum, small_sum, outer_sum, tokens_grad = scatter(
         mesh,
         [
             inner_grad.reshape(shards, each, hidden),
@@ -1264,6 +1322,8 @@
         ],
         [width, width, width, 128],
         [outer_part],
+        [key_low, value_low, query_low, sum_grad, mix, projections],
+        tokens_block,
         1,
     )
     parts = finish(projection_sum, output_sum, inner_sum, outer_sum, small_sum, len(vectors), folds)

time: 412 us -> 405 us (0.983); the launches traced: 414 us -> 401 us
  Pallas kernels: 395 us -> 380 us
  local copies, waits for them, and re-layouts: 0 us -> 5.89 us
  other arithmetic: 4.57 us -> 0 us
    pallas_call x1, Pallas kernels: 26.1 us -> 11.9 us  [tail(): pl.pallas_call(tail_kernel, name='tail', grid=(length // block,), out_sha...]
    unnamed x0 -> x1, local copies, waits for them, and re-layouts: none -> 5.89 us
  transfers between devices with their start and end apart: 3 -> 3, of which waited for: 0 -> 0; matrix products, arithmetic and copies ran while one was open for 1% -> 0% of each run, Pallas kernels for 57% -> 56%
where the time goes in v4:
time: 405 us; the launch traced here: 401 us
  Pallas kernels  380 us (94%)
  between operations  14.3 us (4%)
  local copies, waits for them, and re-layouts  5.89 us (1%)
    pallas_call x1, Pallas kernels, scatter(): pl.pallas_call(functools.partial(scatter_kernel, replicas, shards, count,...  102 us
    pallas_call x1, Pallas kernels, attend_back(): pl.pallas_call(functools.partial(backward_kernel, group), name='attend_ba...  83.5 us
    pallas_call x1, Pallas kernels, attend(): pl.pallas_call(functools.partial(forward_kernel, group), name='attend', o...  64.7 us
    pallas_call x1, Pallas kernels, middle(): pl.pallas_call(functools.partial(middle_kernel, blocks), name='middle', g...  50.9 us
    pallas_call x1, Pallas kernels, gather(): pl.pallas_call(functools.partial(gather_kernel, replicas, shards, count),...  44.6 us
    pallas_call x1, Pallas kernels, project(): pl.pallas_call(project_kernel, name='project', grid=(steps,), out_shape=(...  13.3 us
    pallas_call x1, Pallas kernels, tail(): pl.pallas_call(tail_kernel, name='tail', grid=(length // block,), out_sha...  11.9 us
  transfers between devices with their start and end apart: 3, of which 0 were waited for; matrix products, arithmetic and copies ran while one was open for 0% of the time, Pallas kernels for 56%

profile of v4, /device:TPU:0, one launch (start us, length us, event | category | flops | bytes accessed | tf_op | source)
XLA Modules:
  0.0 401.4 jit_solution(5449185425653558444)
XLA Ops:
  7.2 0.0 all-gather.5.cloned.1.call-start
  7.2 0.7 all-gather.5.cloned.1.call-update
  7.9 0.0 all-gather.3.cloned.1.call-start
  8.0 2.0 pack.1
  10.0 0.0 all-gather.3.cloned.1.call-update
  10.0 0.0 reduce-scatter.2.cloned.1.call-start
  10.1 44.6 %gather.1 = (bf16[16,48,2304]{2,1,0:T(8,128)(2,1)}, bf16[16,48,128]{2,1,0:T(8,128)(2,1)}) custom-call(bf16[48,2304]{1,0:T(8,128)(2,1)} %get-tuple-element.81.refs_0_, bf16[48,128]{1,0:T(8,128)(2,1)} %get-tuple-element.82.refs_1_), custom_call_target="tpu_custom_call" | custom-call | bytes 14942208 | tf_op jit(solution)/shard_map/gather/pallas_call | solution.py:624
  54.7 2.4 unpack.1
  57.1 13.3 %project.1 = (f32[1024,768]{1,0:T(8,128)}, bf16[1024,768]{1,0:T(8,128)(2,1)}, bf16[1024,768]{1,0:T(8,128)(2,1)}, bf16[1024,768]{1,0:T(8,128)(2,1)}, bf16[2048,76...) custom-call(bf16[2048,768]{1,0:T(8,128)(2,1)} %tokens_ref.3, ...), custom_call_target="tpu_custom_call" | custom-call | flops 6039797760 | bytes 15728640 | tf_op jit(solution)/shard_map/project/pallas_call | solution.py:928
  70.4 64.7 %attend.1 = (bf16[6,8,256,2560]{3,2,1,0:T(8,128)(2,1)}, bf16[1024,768]{1,0:T(8,128)(2,1)}, f32[1024,768]{1,0:T(8,128)}, f32[1024,768]{1,0:T(8,128)}) custom-call(s32[8,128]{1,0:T(8,128)} %get-tuple-element.84.behind_ref, s32[8,128]{1,0:T(8,128)} %get-tuple-element.85.ahead_ref, bf16[1024,768]{1,0:T(8,128)(2,1)} %get-tuple-element.89.content_ref, ...), custom_call_target="tpu_custom_call" | custom-call | flops 40000000000 | bytes 70000000 | tf_op jit(solution)/shard_map/attend/pallas_call | solution.py:332
  135.1 0.0 all-gather.5.cloned.1.call-done.outer_ref
  135.2 0.0 all-gather.3.cloned.1.call-done.wide_ref
  135.2 50.9 %middle.1 = (bf16[1024,768]{1,0:T(8,128)(2,1)}, f32[1024,768]{1,0:T(8,128)}, bf16[1024,768]{1,0:T(8,128)(2,1)}, f32[8,768]{1,0:T(8,128)}, f32[8,3072]{1,0:T(8,12...) custom-call(bf16[1024,768]{1,0:T(8,128)(2,1)} %get-tuple-element.98.context_ref, ...), custom_call_target="tpu_custom_call" | custom-call | flops 43486543872 | bytes 31457280 | tf_op jit(solution)/shard_map/middle/pallas_call | solution.py:1038
  186.1 0.0 reduce-scatter.2.cloned.1.call-update
  186.1 83.5 %attend_back.1 = (bf16[1024,768]{1,0:T(8,128)(2,1)}, bf16[2048,768]{1,0:T(8,128)(2,1)}, bf16[2048,768]{1,0:T(8,128)(2,1)}, f32[32,768]{1,0:T(8,128)}, f32[8,768]{1,0:T(8,128)}, /*index=5*/f32[8,768]{1,0:T(8,128)}) custom-call(s32[8,128]{1,0:T(8,128)} %get-tuple-element.84.behind_ref, s32[8,128]{1,0:T(8,128)} %get-tuple-element.85.ahead_ref, ...), custom_call_target="tpu_custom_call" | custom-call | flops 80000000000 | bytes 70000000 | tf_op jit(solution)/shard_map/attend_back/pallas_call | solution.py:379
  269.6 1.9 collect.1
  271.5 11.9 %tail.1 = bf16[768,2304]{1,0:T(8,128)(2,1)} custom-call(bf16[2048,768]{1,0:T(8,128)(2,1)} %tokens_ref.3, bf16[2048,768]{1,0:T(8,128)(2,1)} %get-tuple-element.109.key_ref.refs_5_, bf16[2048,768]{1,0:T(8,128)(2,1)} %get-tuple-element.110.value_ref.refs_6_, bf16[1024,768]{1,0:T(8,128)(2,1)} %get-tuple-element.111.query_ref.refs_7_, ...), custom_call_target="tpu_custom_call" | custom-call | flops 6039797760 | bytes 12582912 | tf_op jit(solution)/shard_map/tail/pallas_call | solution.py:1095
  283.4 0.0 reduce-scatter.2.cloned.1.call-done.refs_4_
  283.4 102.4 %scatter.1 = (f32[48,3072]{1,0:T(8,128)}, f32[48,768]{1,0:T(8,128)}, f32[48,2304]{1,0:T(8,128)}, f32[48,128]{1,0:T(8,128)}, f32[192,768]{1,0:T(8,128)}, /*index=5*/f32[2048,768]{1,0:T(8,128)}) custom-call(bf16[4,2,2,48,3072]{4,3,2,1,0:T(8,128)(2,1)} %bitcast.5, bf16[4,2,2,48,768]{4,3,2,1,0:T(8,128)(2,1)} %bitcast.9, bf16[4,2,2,48,2304]{4,3,2,1,0:T(8,128)(2,1)} %bitcast.8, ...), custom_call_target="tpu_custom_call" | custom-call | bytes 38535168 | tf_op jit(solution)/shard_map/scatter/pallas_call | solution.py:861
  385.8 2.7 finish.1
  388.6 5.9 %copy.43 = f32[2048,768]{1,0:T(8,128)} copy(f32[2048,768]{1,0:T(8,128)} %get-tuple-element.163) | data formatting | bytes 12582912
Async XLA Ops:
  7.2 128.0 %all-gather.5.cloned.1.call-start = ((), (), s32[]{:S(2)}) async-start(), calls=%async_computation.2 | async-start | bytes 5013504 | tf_op jit(solution)/shard_map/all_gather | solution.py:1299
  7.9 127.3 %all-gather.3.cloned.1.call-start = ((), (), s32[]{:S(2)}) async-start(), calls=%async_computation.1 | async-start | bytes 6266880 | tf_op jit(solution)/shard_map/all_gather | solution.py:1298
  10.0 273.4 %reduce-scatter.2.cloned.1.call-start = ((), (), s32[]{:S(2)}) async-start(), calls=%async_computation.3 | async-start | bytes 5013504 | tf_op jit(solution)/shard_map/reduce_scatter | solution.py:1314
Sparse Core Ops, SparseCore 0:
  10.3 59.3 all-gather.4
  72.6 58.2 all-gather.2
  186.2 83.9 reduce-scatter.1

commit v5 on v4

--- a/solution.py
+++ b/solution.py
@@ -26,13 +26,6 @@
     return np.where(offset < 0, 15 + passed + (distance >= 256), passed).astype(np.int32)
 
 
-def near_index():
-    row = np.arange(BQ)[None, :, None]
-    tile = np.arange(-2, 3)[:, None, None]
-    lane = np.arange(128)[None, None, :]
-    return bucket_of(128 * tile + lane - 2 * row)
-
-
 def bucket_onehot():
     out = np.zeros((4 * 128, 128), np.float32)
     offsets = np.concatenate([np.arange(-256, 128), np.full(64, -300), np.full(64, 300)])
@@ -85,30 +78,55 @@
 
 def forward_kernel(
     group, behind_ref, ahead_ref, content_ref, position_ref, ordering_ref, key_ref, value_ref,
-    relative_ref, order_ref, away_ref, document_ref, index_ref,
+    relative_ref, order_ref, away_ref, document_ref,
     probs_ref, context_ref, mixed_ref, inverse_ref,
-    keys, values, table, bias, scores, peak, total,
+    index_ref, keys, values, table, bias, scores, peak, total,
 ):
     step = pl.program_id(1)
     length = key_ref.shape[0]
 
+    rows_each = 256
+    pieces = length // rows_each
+
     @pl.when((step == 0) & (pl.program_id(0) == 0))
     def _():
-        for p in range(group):
+        @pl.loop(0, NEAR // 128)
+        def _(tile):
+            lane = lax.broadcasted_iota(jnp.int32, (BQ, 128), 1)
+            row = lax.broadcasted_iota(jnp.int32, (BQ, 128), 0)
+            offset = 128 * (tile - 2) + lane - 2 * row
+            distance = jnp.abs(offset)
+            passed = jnp.zeros_like(offset)
+            for limit in LIMITS:
+                passed = passed + jnp.where(distance >= limit, 1, 0)
+            index_ref[tile] = jnp.where(offset < 0, 15 + passed + jnp.where(distance >= 256, 1, 0), passed)
+
+        @pl.loop(0, group)
+        def _(p):
             for scratch in (keys, values):
                 scratch[p, :256, :128] = jnp.zeros((256, 128), bf16)
                 scratch[p, 256 + length :, :128] = jnp.zeros((256, 128), bf16)
-            keys[p, :, 128:] = away_ref[...]
-            values[p, :, 128:] = jnp.ones((length + 512, 128), bf16)
+
+            @pl.loop(0, pieces + 2)
+            def _(piece):
+                rows = pl.ds(pl.multiple_of(piece * rows_each, rows_each), rows_each)
+                keys[p, rows, 128:] = away_ref[rows, :]
+                values[p, rows, 128:] = jnp.ones((rows_each, 128), bf16)
 
     @pl.when(step == 0)
     def _():
+        @pl.loop(0, pieces)
+        def _(piece):
+            source = pl.ds(pl.multiple_of(piece * rows_each, rows_each), rows_each)
+            target = pl.ds(pl.multiple_of((piece + 1) * rows_each, rows_each), rows_each)
+            for p in range(group):
+                keys[p, target, :128] = key_ref[source, lanes_of(p)]
+                values[p, target, :128] = value_ref[source, lanes_of(p)]
+
         after = lax.broadcasted_iota(jnp.int32, (32, 128), 0) < 16
         table[...] = jnp.zeros(table.shape, bf16)
         for p in range(group):
             lanes = lanes_of(p)
-            keys[p, 256 : 256 + length, :128] = key_ref[:, lanes]
-            values[p, 256 : 256 + length, :128] = value_ref[:, lanes]
             orders = jnp.where(after, order_ref[0:1, lanes].astype(f32), order_ref[1:2, lanes].astype(f32)).astype(bf16)
             for half, (relative, order) in enumerate(zip(halves(relative_ref[:, lanes]), halves(orders))):
                 both = jnp.concatenate([relative, order], 1)
@@ -212,10 +230,6 @@
         table[...] = jnp.zeros(table.shape, bf16)
         for p in range(group):
             lanes = lanes_of(p)
-            for scratch, ref in ((keys, key_ref), (values, value_ref)):
-                scratch[p, :256, :] = jnp.zeros((256, 128), bf16)
-                scratch[p, 256 + length :, :] = jnp.zeros((256, 128), bf16)
-                scratch[p, 256 : 256 + length, :] = ref[:, lanes]
             even, odd = halves(relative_ref[:, lanes])
             table[p, 0:32, :128] = even
             table[p, 128:160, :128] = odd
@@ -223,8 +237,26 @@
             even, odd = halves(jnp.where(slot < 2, orders, 0.0))
             table[p, 32:64, 128:] = even.astype(bf16)
             table[p, 160:192, 128:] = odd.astype(bf16)
-        key_total[...] = jnp.zeros(key_total.shape, f32)
-        value_total[...] = jnp.zeros(value_total.shape, f32)
+
+        @pl.loop(0, length // 256 + 2)
+        def _(piece):
+            rows = pl.ds(pl.multiple_of(piece * 256, 256), 256)
+            for p in range(group):
+                for total in (key_total, value_total):
+                    total[p, :, rows] = jnp.zeros((128, 256), f32)
+
+        for scratch in (keys, values):
+            scratch[:, :256, :] = jnp.zeros((group, 256, 128), bf16)
+            scratch[:, 256 + length :, :] = jnp.zeros((group, 256, 128), bf16)
+
+        @pl.loop(0, length // 256)
+        def _(piece):
+            source = pl.ds(pl.multiple_of(piece * 256, 256), 256)
+            target = pl.ds(pl.multiple_of((piece + 1) * 256, 256), 256)
+            for p in range(group):
+                for scratch, ref in ((keys, key_ref), (values, value_ref)):
+                    scratch[p, target, :] = ref[source, lanes_of(p)]
+
         table_total[...] = jnp.zeros(table_total.shape, f32)
         sums[...] = jnp.zeros(sums.shape, f32)
 
@@ -307,11 +339,17 @@
         low_lane = lax.broadcasted_iota(jnp.int32, (32, 128), 1) < 64
         for p in range(group):
             lanes = lanes_of(p)
-            key_low_ref[:, lanes] = (key_total[p, :, 256 : 256 + length] * LN2).T.astype(bf16)
-            value_low_ref[:, lanes] = value_total[p, :, 256 : 256 + length].T.astype(bf16)
             relative_out[:, lanes] = jnp.where(low_lane, table_total[p, 0:32, :128], table_total[p, 128:160, :128])
             order_out[:, lanes] = jnp.where(low_lane[:8], table_total[p, 32:40, 128:], table_total[p, 160:168, 128:])
         sums_out[...] = sums[...]
+
+        @pl.loop(0, length // 512)
+        def _(piece):
+            rows = pl.ds(pl.multiple_of(piece * 512, 512), 512)
+            columns = pl.ds(pl.multiple_of(piece * 512 + 256, 256), 512)
+            for p in range(group):
+                key_low_ref[rows, lanes_of(p)] = (key_total[p, :, columns] * LN2).T.astype(bf16)
+                value_low_ref[rows, lanes_of(p)] = value_total[p, :, columns].T.astype(bf16)
 
 
 def fixed(*shape):
@@ -347,10 +385,10 @@
                 pl.BlockSpec((2, wide), lambda p, i, *_: (0, p)),
                 fixed(padded, 128),
                 pl.BlockSpec((BQ, 128), lambda p, i, *_: (i, 0)),
-                fixed(5, BQ, 128),
             ],
             out_specs=[pl.BlockSpec((group, 1, 2 * BQ, padded), lambda p, i, *_: (p, i, 0, 0)), tile, tile, tile],
             scratch_shapes=[
+                pltpu.VMEM((NEAR // 128, BQ, 128), jnp.int32),
                 pltpu.VMEM((group, padded, 256), bf16),
                 pltpu.VMEM((group, padded, 256), bf16),
                 pltpu.VMEM((group, 768, 256), bf16),
@@ -362,8 +400,7 @@
         ),
         compiler_params=pltpu.CompilerParams(dimension_semantics=("arbitrary", "arbitrary"), vmem_limit_bytes=62 << 20),
         cost_estimate=pl.CostEstimate(flops=40 * 10**9, bytes_accessed=70 * 10**6, transcendentals=10**7),
-    )(behind, ahead, content, position, ordering, keys, values, relative, order, away, document,
-      jnp.asarray(near_index()))
+    )(behind, ahead, content, position, ordering, keys, values, relative, order, away, document)
 
 
 def attend_back(behind, ahead, probs, grad, mixed, inverse, content, position, ordering, keys, values, relative, order):
@@ -791,20 +828,25 @@
     loads = [pltpu.make_async_copy(ref, buf, work_sems.at[i]) for i, (ref, buf) in enumerate(zip(work_in, work_bufs))]
     for copy in loads:
         copy.start()
-    stores = []
-
-    def block(b):
-        if b == 0:
+    size = block_buf.shape[1]
+    blocks = tokens_grad.shape[0] // size
+
+    def stored(b, slot):
+        return pltpu.make_async_copy(block_buf.at[slot], tokens_grad.at[pl.ds(pl.multiple_of(b * size, size), size)], block_sems.at[slot])
+
+    def pair(turn):
+        if turn == 0:
             for copy in loads:
                 copy.wait()
-        if b >= 2:
-            stores[b - 2].wait()
-        block_buf[b % 2] = work(b, *work_bufs)
-        size = block_buf.shape[1]
-        stores.append(pltpu.make_async_copy(block_buf.at[b % 2], tokens_grad.at[pl.ds(b * size, size)], block_sems.at[b % 2]))
-        stores[b].start()
-
-    blocks = tokens_grad.shape[0] // block_buf.shape[1]
+
+        @pl.loop(0, 2)
+        def _(slot):
+            b = 2 * turn + slot
+            if turn > 0:
+                stored(b - 2, slot).wait()
+            block_buf[slot] = work(b, *work_bufs)
+            stored(b, slot).start()
+
     stages = [stage_rep, stage_cross]
     stages += [functools.partial(stage_line, distance) for distance in range(here.line - 1, 0, -1)]
     stages += [stage_last, stage_finish]
@@ -818,12 +860,12 @@
                 for hop in hops:
                     send(extras[e], extra_bufs[e].at[here.replica], last_send.at[total + e, hop],
                          last_recv.at[total + e, here.replica], here.device(replica=here.other_replica(hop)))
-        elif time <= blocks:
-            block(time - 1)
-    for b in range(min(blocks, total + len(stages) - 2), blocks):
-        block(b)
-    for b in range(max(blocks - 2, 0), blocks):
-        stores[b].wait()
+        elif time % 2 == 1 and time < blocks:
+            pair(time // 2)
+    for turn in range((total + len(stages) - 1) // 2, blocks // 2):
+        pair(turn)
+    for slot in range(2):
+        stored(blocks - 2 + slot, slot).wait()
     for e in range(extra):
         finish(extras[e], extra_bufs[e], extra_outs[e], last_recv.at[total + e], pl.ds(0, extras[e].shape[1]))
     for condition, wait in pending:
@@ -1107,7 +1149,7 @@
 
 def tokens_block(block, key_ref, value_ref, query_ref, sum_ref, mix_ref, weight_ref):
     width = key_ref.shape[1]
-    whole, half = slice(256 * block, 256 * block + 256), slice(128 * block, 128 * block + 128)
+    whole, half = (pl.ds(pl.multiple_of(block * rows, rows), rows) for rows in (256, 128))
     pooled_grad = sum_ref[half, :] + nt(query_ref[half, :], weight_ref[:, :width])
     coarse = pooled_grad.astype(bf16)
     fine = (pooled_grad - coarse.astype(f32)).astype(bf16)

time: 405 us -> 397 us (0.980)
  Pallas kernels: 380 us -> 373 us
    pallas_call x1, Pallas kernels: 102 us -> 82.6 us  [scatter(): pl.pallas_call(functools.partial(scatter_kernel, replicas, shards, count,...]
    pallas_call x1, Pallas kernels: 83.5 us -> 90.2 us  [attend_back(): pl.pallas_call(functools.partial(backward_kernel, group), name='attend_ba...]
    pallas_call x1, Pallas kernels: 64.7 us -> 69.9 us  [attend(): pl.pallas_call(functools.partial(forward_kernel, group), name='attend', o...]
  transfers between devices with their start and end apart: 3 -> 3, of which waited for: 0 -> 0; matrix products, arithmetic and copies ran while one was open for 0% -> 0% of each run, Pallas kernels for 56% -> 60%
where the time goes in v5:
time: 397 us; the launch traced here: 393 us
  Pallas kernels  373 us (94%)
  between operations  13.8 us (3%)
  local copies, waits for them, and re-layouts  5.89 us (1%)
    pallas_call x1, Pallas kernels, attend_back(): pl.pallas_call(functools.partial(backward_kernel, group), name='attend_ba...  90.2 us
    pallas_call x1, Pallas kernels, scatter(): pl.pallas_call(functools.partial(scatter_kernel, replicas, shards, count,...  82.6 us
    pallas_call x1, Pallas kernels, attend(): pl.pallas_call(functools.partial(forward_kernel, group), name='attend', o...  69.9 us
    pallas_call x1, Pallas kernels, middle(): pl.pallas_call(functools.partial(middle_kernel, blocks), name='middle', g...  50.9 us
    pallas_call x1, Pallas kernels, gather(): pl.pallas_call(functools.partial(gather_kernel, replicas, shards, count),...  44.6 us
    pallas_call x1, Pallas kernels, project(): pl.pallas_call(project_kernel, name='project', grid=(steps,), out_shape=(...  13.3 us
    pallas_call x1, Pallas kernels, tail(): pl.pallas_call(tail_kernel, name='tail', grid=(length // block,), out_sha...  11.9 us
  transfers between devices with their start and end apart: 3, of which 0 were waited for; matrix products, arithmetic and copies ran while one was open for 0% of the time, Pallas kernels for 60%

profile of v5, /device:TPU:0, one launch (start us, length us, event | category | flops | bytes accessed | tf_op | source)
XLA Modules:
  0.0 393.1 jit_solution(14888003330285426048)
XLA Ops:
  7.2 0.0 all-gather.5.cloned.1.call-start
  7.2 0.7 all-gather.5.cloned.1.call-update
  7.9 0.0 all-gather.3.cloned.1.call-start
  8.0 2.0 pack.1
  10.0 0.0 all-gather.3.cloned.1.call-update
  10.0 0.0 reduce-scatter.2.cloned.1.call-start
  10.1 44.6 %gather.1 = (bf16[16,48,2304]{2,1,0:T(8,128)(2,1)}, bf16[16,48,128]{2,1,0:T(8,128)(2,1)}) custom-call(bf16[48,2304]{1,0:T(8,128)(2,1)} %get-tuple-element.81.refs_0_, bf16[48,128]{1,0:T(8,128)(2,1)} %get-tuple-element.82.refs_1_), custom_call_target="tpu_custom_call" | custom-call | bytes 14942208 | tf_op jit(solution)/shard_map/gather/pallas_call | solution.py:661
  54.7 2.4 unpack.1
  57.1 13.3 %project.1 = (f32[1024,768]{1,0:T(8,128)}, bf16[1024,768]{1,0:T(8,128)(2,1)}, bf16[1024,768]{1,0:T(8,128)(2,1)}, bf16[1024,768]{1,0:T(8,128)(2,1)}, bf16[2048,76...) custom-call(bf16[2048,768]{1,0:T(8,128)(2,1)} %tokens_ref.3, ...), custom_call_target="tpu_custom_call" | custom-call | flops 6039797760 | bytes 15728640 | tf_op jit(solution)/shard_map/project/pallas_call | solution.py:970
  70.4 69.9 %attend.1 = (bf16[6,8,256,2560]{3,2,1,0:T(8,128)(2,1)}, bf16[1024,768]{1,0:T(8,128)(2,1)}, f32[1024,768]{1,0:T(8,128)}, f32[1024,768]{1,0:T(8,128)}) custom-call(s32[8,128]{1,0:T(8,128)} %get-tuple-element.84.behind_ref, s32[8,128]{1,0:T(8,128)} %get-tuple-element.85.ahead_ref, bf16[1024,768]{1,0:T(8,128)(2,1)} %get-tuple-element.89.content_ref, ...), custom_call_target="tpu_custom_call" | custom-call | flops 40000000000 | bytes 70000000 | tf_op jit(solution)/shard_map/attend/pallas_call | solution.py:370
  140.4 0.0 all-gather.5.cloned.1.call-done.outer_ref
  140.4 0.0 all-gather.3.cloned.1.call-done.wide_ref
  140.4 50.9 %middle.1 = (bf16[1024,768]{1,0:T(8,128)(2,1)}, f32[1024,768]{1,0:T(8,128)}, bf16[1024,768]{1,0:T(8,128)(2,1)}, f32[8,768]{1,0:T(8,128)}, f32[8,3072]{1,0:T(8,12...) custom-call(bf16[1024,768]{1,0:T(8,128)(2,1)} %get-tuple-element.98.context_ref, ...), custom_call_target="tpu_custom_call" | custom-call | flops 43486543872 | bytes 31457280 | tf_op jit(solution)/shard_map/middle/pallas_call | solution.py:1080
  191.3 0.0 reduce-scatter.2.cloned.1.call-update
  191.3 90.2 %attend_back.1 = (bf16[1024,768]{1,0:T(8,128)(2,1)}, bf16[2048,768]{1,0:T(8,128)(2,1)}, bf16[2048,768]{1,0:T(8,128)(2,1)}, f32[32,768]{1,0:T(8,128)}, f32[8,768]{1,0:T(8,128)}, /*index=5*/f32[8,768]{1,0:T(8,128)}) custom-call(s32[8,128]{1,0:T(8,128)} %get-tuple-element.84.behind_ref, s32[8,128]{1,0:T(8,128)} %get-tuple-element.85.ahead_ref, ...), custom_call_target="tpu_custom_call" | custom-call | flops 80000000000 | bytes 70000000 | tf_op jit(solution)/shard_map/attend_back/pallas_call | solution.py:416
  281.6 1.9 collect.1
  283.5 11.9 %tail.1 = bf16[768,2304]{1,0:T(8,128)(2,1)} custom-call(bf16[2048,768]{1,0:T(8,128)(2,1)} %tokens_ref.3, bf16[2048,768]{1,0:T(8,128)(2,1)} %get-tuple-element.109.key_ref.refs_5_, bf16[2048,768]{1,0:T(8,128)(2,1)} %get-tuple-element.110.value_ref.refs_6_, bf16[1024,768]{1,0:T(8,128)(2,1)} %get-tuple-element.111.query_ref.refs_7_, ...), custom_call_target="tpu_custom_call" | custom-call | flops 6039797760 | bytes 12582912 | tf_op jit(solution)/shard_map/tail/pallas_call | solution.py:1137
  295.4 0.0 reduce-scatter.2.cloned.1.call-done.refs_4_
  295.4 82.6 %scatter.1 = (f32[48,3072]{1,0:T(8,128)}, f32[48,768]{1,0:T(8,128)}, f32[48,2304]{1,0:T(8,128)}, f32[48,128]{1,0:T(8,128)}, f32[192,768]{1,0:T(8,128)}, /*index=5*/f32[2048,768]{1,0:T(8,128)}) custom-call(bf16[4,2,2,48,3072]{4,3,2,1,0:T(8,128)(2,1)} %bitcast.5, bf16[4,2,2,48,768]{4,3,2,1,0:T(8,128)(2,1)} %bitcast.9, bf16[4,2,2,48,2304]{4,3,2,1,0:T(8,128)(2,1)} %bitcast.8, ...), custom_call_target="tpu_custom_call" | custom-call | bytes 38535168 | tf_op jit(solution)/shard_map/scatter/pallas_call | solution.py:903
  378.0 2.7 finish.1
  380.7 5.9 %copy.42 = f32[2048,768]{1,0:T(8,128)} copy(f32[2048,768]{1,0:T(8,128)} %get-tuple-element.163) | data formatting | bytes 12582912
Async XLA Ops:
  7.2 133.2 %all-gather.5.cloned.1.call-start = ((), (), s32[]{:S(2)}) async-start(), calls=%async_computation.2 | async-start | bytes 5013504 | tf_op jit(solution)/shard_map/all_gather | solution.py:1341
  7.9 132.5 %all-gather.3.cloned.1.call-start = ((), (), s32[]{:S(2)}) async-start(), calls=%async_computation.1 | async-start | bytes 6266880 | tf_op jit(solution)/shard_map/all_gather | solution.py:1340
  10.0 285.4 %reduce-scatter.2.cloned.1.call-start = ((), (), s32[]{:S(2)}) async-start(), calls=%async_computation.3 | async-start | bytes 5013504 | tf_op jit(solution)/shard_map/reduce_scatter | solution.py:1356
Sparse Core Ops, SparseCore 0:
  10.3 59.3 all-gather.4
  72.6 58.2 all-gather.2
  191.4 75.1 reduce-scatter.1

commit v6 on v5

--- a/solution.py
+++ b/solution.py
@@ -695,6 +695,8 @@
             local.append(pltpu.make_async_copy(
                 sources[k].at[:, column, here.core, :, cut], own_bufs[k].at[column, :, :, cut], own_sems.at[j, column]
             ))
+    for copy in local:
+        copy.start()
     here.meet()
     pending = []
 
@@ -823,8 +825,6 @@
                 column = here.other_column(step)
                 send(sources[k].at[:, column, 1 - here.core, :, columns(j)], core_bufs[k].at[column, :, :, columns(j)],
                      core_send.at[j, column], core_recv.at[j, column], here.device(core=1 - here.core))
-    for copy in local:
-        copy.start()
     loads = [pltpu.make_async_copy(ref, buf, work_sems.at[i]) for i, (ref, buf) in enumerate(zip(work_in, work_bufs))]
     for copy in loads:
         copy.start()

time: 397 us -> 395 us (level); the launches traced: 393 us -> 397 us
    pallas_call x1, Pallas kernels: 82.6 us -> 102 us  [scatter(): pl.pallas_call(functools.partial(scatter_kernel, replicas, shards, count,...]
    pallas_call x1, Pallas kernels: 90.2 us -> 81 us  [attend_back(): pl.pallas_call(functools.partial(backward_kernel, group), name='attend_ba...]
    pallas_call x1, Pallas kernels: 69.9 us -> 63.4 us  [attend(): pl.pallas_call(functools.partial(forward_kernel, group), name='attend', o...]
  transfers between devices with their start and end apart: 3 -> 3, of which waited for: 0 -> 0; matrix products, arithmetic and copies ran while one was open for 0% -> 0% of each run, Pallas kernels for 60% -> 56%
where the time goes in v6:
time: 395 us; the launch traced here: 397 us
  Pallas kernels  376 us (95%)
  between operations  13.8 us (3%)
  local copies, waits for them, and re-layouts  5.89 us (1%)
    pallas_call x1, Pallas kernels, scatter(): pl.pallas_call(functools.partial(scatter_kernel, replicas, shards, count,...  102 us
    pallas_call x1, Pallas kernels, attend_back(): pl.pallas_call(functools.partial(backward_kernel, group), name='attend_ba...  81 us
    pallas_call x1, Pallas kernels, attend(): pl.pallas_call(functools.partial(forward_kernel, group), name='attend', o...  63.4 us
    pallas_call x1, Pallas kernels, middle(): pl.pallas_call(functools.partial(middle_kernel, blocks), name='middle', g...  50.9 us
    pallas_call x1, Pallas kernels, gather(): pl.pallas_call(functools.partial(gather_kernel, replicas, shards, count),...  44.6 us
    pallas_call x1, Pallas kernels, project(): pl.pallas_call(project_kernel, name='project', grid=(steps,), out_shape=(...  13.3 us
    pallas_call x1, Pallas kernels, tail(): pl.pallas_call(tail_kernel, name='tail', grid=(length // block,), out_sha...  11.9 us
  transfers between devices with their start and end apart: 3, of which 0 were waited for; matrix products, arithmetic and copies ran while one was open for 0% of the time, Pallas kernels for 56%

profile of v6, /device:TPU:0, one launch (start us, length us, event | category | flops | bytes accessed | tf_op | source)
XLA Modules:
  0.0 396.9 jit_solution(4959370410001103089)
XLA Ops:
  7.2 0.0 all-gather.5.cloned.1.call-start
  7.2 0.7 all-gather.5.cloned.1.call-update
  7.9 0.0 all-gather.3.cloned.1.call-start
  8.0 2.0 pack.1
  10.0 0.0 all-gather.3.cloned.1.call-update
  10.0 0.0 reduce-scatter.2.cloned.1.call-start
  10.1 44.6 %gather.1 = (bf16[16,48,2304]{2,1,0:T(8,128)(2,1)}, bf16[16,48,128]{2,1,0:T(8,128)(2,1)}) custom-call(bf16[48,2304]{1,0:T(8,128)(2,1)} %get-tuple-element.81.refs_0_, bf16[48,128]{1,0:T(8,128)(2,1)} %get-tuple-element.82.refs_1_), custom_call_target="tpu_custom_call" | custom-call | bytes 14942208 | tf_op jit(solution)/shard_map/gather/pallas_call | solution.py:661
  54.7 2.4 unpack.1
  57.1 13.3 %project.1 = (f32[1024,768]{1,0:T(8,128)}, bf16[1024,768]{1,0:T(8,128)(2,1)}, bf16[1024,768]{1,0:T(8,128)(2,1)}, bf16[1024,768]{1,0:T(8,128)(2,1)}, bf16[2048,76...) custom-call(bf16[2048,768]{1,0:T(8,128)(2,1)} %tokens_ref.3, ...), custom_call_target="tpu_custom_call" | custom-call | flops 6039797760 | bytes 15728640 | tf_op jit(solution)/shard_map/project/pallas_call | solution.py:970
  70.4 63.4 %attend.1 = (bf16[6,8,256,2560]{3,2,1,0:T(8,128)(2,1)}, bf16[1024,768]{1,0:T(8,128)(2,1)}, f32[1024,768]{1,0:T(8,128)}, f32[1024,768]{1,0:T(8,128)}) custom-call(s32[8,128]{1,0:T(8,128)} %get-tuple-element.84.behind_ref, s32[8,128]{1,0:T(8,128)} %get-tuple-element.85.ahead_ref, bf16[1024,768]{1,0:T(8,128)(2,1)} %get-tuple-element.89.content_ref, ...), custom_call_target="tpu_custom_call" | custom-call | flops 40000000000 | bytes 70000000 | tf_op jit(solution)/shard_map/attend/pallas_call | solution.py:370
  133.8 0.0 all-gather.5.cloned.1.call-done.outer_ref
  133.8 0.0 all-gather.3.cloned.1.call-done.wide_ref
  133.9 50.9 %middle.1 = (bf16[1024,768]{1,0:T(8,128)(2,1)}, f32[1024,768]{1,0:T(8,128)}, bf16[1024,768]{1,0:T(8,128)(2,1)}, f32[8,768]{1,0:T(8,128)}, f32[8,3072]{1,0:T(8,12...) custom-call(bf16[1024,768]{1,0:T(8,128)(2,1)} %get-tuple-element.98.context_ref, ...), custom_call_target="tpu_custom_call" | custom-call | flops 43486543872 | bytes 31457280 | tf_op jit(solution)/shard_map/middle/pallas_call | solution.py:1080
  184.7 0.0 reduce-scatter.2.cloned.1.call-update
  184.8 81.0 %attend_back.1 = (bf16[1024,768]{1,0:T(8,128)(2,1)}, bf16[2048,768]{1,0:T(8,128)(2,1)}, bf16[2048,768]{1,0:T(8,128)(2,1)}, f32[32,768]{1,0:T(8,128)}, f32[8,768]{1,0:T(8,128)}, /*index=5*/f32[8,768]{1,0:T(8,128)}) custom-call(s32[8,128]{1,0:T(8,128)} %get-tuple-element.84.behind_ref, s32[8,128]{1,0:T(8,128)} %get-tuple-element.85.ahead_ref, ...), custom_call_target="tpu_custom_call" | custom-call | flops 80000000000 | bytes 70000000 | tf_op jit(solution)/shard_map/attend_back/pallas_call | solution.py:416
  265.8 1.9 collect.1
  267.8 11.9 %tail.1 = bf16[768,2304]{1,0:T(8,128)(2,1)} custom-call(bf16[2048,768]{1,0:T(8,128)(2,1)} %tokens_ref.3, bf16[2048,768]{1,0:T(8,128)(2,1)} %get-tuple-element.109.key_ref.refs_5_, bf16[2048,768]{1,0:T(8,128)(2,1)} %get-tuple-element.110.value_ref.refs_6_, bf16[1024,768]{1,0:T(8,128)(2,1)} %get-tuple-element.111.query_ref.refs_7_, ...), custom_call_target="tpu_custom_call" | custom-call | flops 6039797760 | bytes 12582912 | tf_op jit(solution)/shard_map/tail/pallas_call | solution.py:1137
  279.7 0.0 reduce-scatter.2.cloned.1.call-done.refs_4_
  279.7 102.1 %scatter.1 = (f32[48,3072]{1,0:T(8,128)}, f32[48,768]{1,0:T(8,128)}, f32[48,2304]{1,0:T(8,128)}, f32[48,128]{1,0:T(8,128)}, f32[192,768]{1,0:T(8,128)}, /*index=5*/f32[2048,768]{1,0:T(8,128)}) custom-call(bf16[4,2,2,48,3072]{4,3,2,1,0:T(8,128)(2,1)} %bitcast.5, bf16[4,2,2,48,768]{4,3,2,1,0:T(8,128)(2,1)} %bitcast.9, bf16[4,2,2,48,2304]{4,3,2,1,0:T(8,128)(2,1)} %bitcast.8, ...), custom_call_target="tpu_custom_call" | custom-call | bytes 38535168 | tf_op jit(solution)/shard_map/scatter/pallas_call | solution.py:903
  381.7 2.7 finish.1
  384.5 5.9 %copy.42 = f32[2048,768]{1,0:T(8,128)} copy(f32[2048,768]{1,0:T(8,128)} %get-tuple-element.163) | data formatting | bytes 12582912
Async XLA Ops:
  7.2 126.6 %all-gather.5.cloned.1.call-start = ((), (), s32[]{:S(2)}) async-start(), calls=%async_computation.2 | async-start | bytes 5013504 | tf_op jit(solution)/shard_map/all_gather | solution.py:1341
  7.9 125.9 %all-gather.3.cloned.1.call-start = ((), (), s32[]{:S(2)}) async-start(), calls=%async_computation.1 | async-start | bytes 6266880 | tf_op jit(solution)/shard_map/all_gather | solution.py:1340
  10.0 269.6 %reduce-scatter.2.cloned.1.call-start = ((), (), s32[]{:S(2)}) async-start(), calls=%async_computation.3 | async-start | bytes 5013504 | tf_op jit(solution)/shard_map/reduce_scatter | solution.py:1356
Sparse Core Ops, SparseCore 0:
  10.3 59.3 all-gather.4
  72.6 58.0 all-gather.2
  184.9 83.8 reduce-scatter.1
